TPU v7x, 32 devices: a whole 2x2x4 slice. The times are simulated.
32 devices in a mesh: fsdp: 8 (over y, x, core), rep: 4 (over z).
Axes of the slice: x: 2, y: 2, z: 4, core: 2. Of those that a mesh axis runs over, the one named last changes fastest.
Arguments:
- tokens: bfloat16 [65536, 768], P(('fsdp', 'rep')), may hold values from -6 to 6
- segment_ids: int32 [65536], P(('fsdp', 'rep')), may hold values from -1 to 8, as said below
- cotangent: bfloat16 [65536, 768], P(('fsdp', 'rep')), may hold values from -8 to 8
- norm_params: bfloat16 [4, 768], P(None, 'fsdp')
- qkv_weight: bfloat16 [768, 2304], P(None, 'fsdp'), may hold values from -0.21875 to 0.21875
- proj_weight: bfloat16 [768, 768], P(None, 'fsdp'), may hold values from -1.25 to 1.25
- up_weight: bfloat16 [768, 3072], P(None, 'fsdp'), may hold values from -0.21875 to 0.21875
- down_weight: bfloat16 [3072, 768], P(None, 'fsdp'), may hold values from -0.109375 to 0.109375
- target_norms: float32 [4, 768], P(None, 'fsdp'), may hold values from -3 to 3
- target_qkv: float32 [768, 2304], P(None, 'fsdp'), may hold values from -0.21875 to 0.21875
- target_proj: float32 [768, 768], P(None, 'fsdp'), may hold values from -1.25 to 1.25
- target_up: float32 [768, 3072], P(None, 'fsdp'), may hold values from -0.21875 to 0.21875
- target_down: float32 [3072, 768], P(None, 'fsdp'), may hold values from -0.109375 to 0.109375
Outputs:
- block_output: bfloat16 [65536, 768], P(('fsdp', 'rep'))
- input_grad: bfloat16 [65536, 768], P(('fsdp', 'rep'))
- norm_grad: float32 [4, 768], P(None, 'fsdp')
- qkv_grad: float32 [768, 2304], P(None, 'fsdp')
- proj_grad: float32 [768, 768], P(None, 'fsdp')
- up_grad: float32 [768, 3072], P(None, 'fsdp')
- down_grad: float32 [3072, 768], P(None, 'fsdp')
- new_target_norms: float32 [4, 768], P(None, 'fsdp')
- new_target_qkv: float32 [768, 2304], P(None, 'fsdp')
- new_target_proj: float32 [768, 768], P(None, 'fsdp')
- new_target_up: float32 [768, 3072], P(None, 'fsdp')
- new_target_down: float32 [3072, 768], P(None, 'fsdp')
Inputs may be any that keep to these rules, and one draw needn't show every extreme that they name: `segment_ids`: in each packed row of 1024 slots, images fill consecutive slots from the row's start with ids 0, 1, 2, ... in order; each image has 98 to 196 slots and one image of each row has exactly 196; the remaining slots at the row's end are -1. In the first packed row all images except the one of 196 slots have exactly 98 slots.
All inputs are finite; a program needn't handle non-finite values.
Results may differ from a plain program's by a relative error of at most 0.014.
Values may be sent and summed in bfloat16 or wider, within the bound.
No kernel may reach another device: no remote copies, remote signals or barrier semaphores. Data moves between devices by JAX's collectives and lax.ppermute only.
A program may use at most 256 MiB of HBM per device.

v0:
```python
import jax
import jax.numpy as jnp
from jax import lax
from jax.sharding import PartitionSpec as P

HEAD = 64
ROW_LEN = 1024


layer_eps = 1e-06
ema_rate = 0.75


def layer_norm(values, gain, shift):
    center = values - jnp.mean(values, axis=-1, keepdims=True)
    spread = jnp.mean(center * center, axis=-1, keepdims=True)
    return center * lax.rsqrt(spread + layer_eps) * gain + shift


def gelu_exact(values):
    return jax.nn.gelu(values, approximate=False)


def product(left, right):
    return jnp.dot(left, right, preferred_element_type=jnp.float32)


def outer_sum(left, right):
    return lax.dot_general(
        left, right, (((0,), (0,)), ((), ())), preferred_element_type=jnp.float32
    )


def against(left, right):
    return lax.dot_general(
        left, right, (((1,), (1,)), ((), ())), preferred_element_type=jnp.float32
    )


def split_heads(matrix, rows):
    count, width = matrix.shape
    heads = width // HEAD
    shaped = matrix.reshape(rows, count // rows, heads, HEAD)
    return shaped.transpose(0, 2, 1, 3).reshape(rows * heads, count // rows, HEAD)


def merge_heads(stacked, rows):
    items, length, size = stacked.shape
    heads = items // rows
    shaped = stacked.reshape(rows, heads, length, size).transpose(0, 2, 1, 3)
    return shaped.reshape(rows * length, heads * size)


def masked_scores(query, keyset, segment):
    same = segment[:, None] == segment[None, :]
    return jnp.where(same, against(query, keyset) * 0.125, -1e30)


def head_forward(item):
    query, keyset, value, segment = item
    scores = masked_scores(query, keyset, segment)
    top = jnp.max(scores, axis=1, keepdims=True)
    expo = jnp.exp(scores - top)
    total = jnp.sum(expo, axis=1, keepdims=True)
    weights = (expo / total).astype(jnp.bfloat16)
    return (product(weights, value), top, total)


def head_backward(item):
    query, keyset, value, segment, top, total, grad_head = item
    scores = masked_scores(query, keyset, segment)
    probs = jnp.exp(scores - top) / total
    grad_probs = against(grad_head, value)
    center = jnp.sum(probs * grad_probs, axis=1, keepdims=True)
    grad_scores = (probs * (grad_probs - center)).astype(jnp.bfloat16)
    grad_query = product(grad_scores, keyset) * 0.125
    grad_key = outer_sum(grad_scores, query) * 0.125
    grad_value = outer_sum(probs.astype(jnp.bfloat16), grad_head)
    return (grad_query, grad_key, grad_value)


def per_device(
    tokens,
    segment_ids,
    cotangent,
    norm_params,
    qkv_weight,
    proj_weight,
    up_weight,
    down_weight,
    target_norms,
    target_qkv,
    target_proj,
    target_up,
    target_down,
):
    norms, w_qkv, w_proj, w_up, w_down = (
        lax.all_gather(norm_params, "fsdp", axis=1, tiled=True),
        lax.all_gather(qkv_weight, "fsdp", axis=1, tiled=True),
        lax.all_gather(proj_weight, "fsdp", axis=1, tiled=True),
        lax.all_gather(up_weight, "fsdp", axis=1, tiled=True),
        lax.all_gather(down_weight, "fsdp", axis=1, tiled=True),
    )
    gains = norms.astype(jnp.float32)
    count, width = tokens.shape
    rows = count // ROW_LEN
    heads = width // HEAD
    inputs = tokens.astype(jnp.float32)
    valid = (segment_ids >= 0).astype(jnp.float32)[:, None]
    first = layer_norm(inputs, gains[0], gains[1]).astype(jnp.bfloat16)
    qkv = product(first, w_qkv).astype(jnp.bfloat16)
    query = split_heads(qkv[:, :width], rows)
    keyset = split_heads(qkv[:, width : 2 * width], rows)
    value = split_heads(qkv[:, 2 * width :], rows)
    segments = jnp.repeat(segment_ids.reshape(rows, ROW_LEN), heads, axis=0)
    head_out, tops, totals = lax.map(head_forward, (query, keyset, value, segments))
    attended = merge_heads(head_out, rows).astype(jnp.bfloat16)
    middle = inputs + product(attended, w_proj)
    second = layer_norm(middle, gains[2], gains[3]).astype(jnp.bfloat16)
    upper = product(second, w_up)
    activated = gelu_exact(upper).astype(jnp.bfloat16)
    final = middle + product(activated, w_down)
    block_output = (final * valid).astype(jnp.bfloat16)
    norms, w_qkv, w_proj, w_up, w_down = (
        lax.all_gather(norm_params, "fsdp", axis=1, tiled=True),
        lax.all_gather(qkv_weight, "fsdp", axis=1, tiled=True),
        lax.all_gather(proj_weight, "fsdp", axis=1, tiled=True),
        lax.all_gather(up_weight, "fsdp", axis=1, tiled=True),
        lax.all_gather(down_weight, "fsdp", axis=1, tiled=True),
    )
    gains = norms.astype(jnp.float32)
    grad_out = (cotangent.astype(jnp.float32) * valid).astype(jnp.bfloat16)
    grad_down = outer_sum(activated, grad_out)
    grad_act = against(grad_out, w_down)
    gelu_back = jax.vjp(gelu_exact, upper)[1]
    grad_upper = gelu_back(grad_act)[0].astype(jnp.bfloat16)
    grad_up = outer_sum(second, grad_upper)
    grad_second = against(grad_upper, w_up)
    second_back = jax.vjp(layer_norm, middle, gains[2], gains[3])[1]
    grad_mid_norm, grad_gain_two, grad_shift_two = second_back(grad_second)
    grad_middle = grad_out.astype(jnp.float32) + grad_mid_norm
    grad_branch = grad_middle.astype(jnp.bfloat16)
    grad_proj = outer_sum(attended, grad_branch)
    grad_attended = against(grad_branch, w_proj).astype(jnp.bfloat16)
    grad_heads = split_heads(grad_attended, rows)
    grad_query, grad_key, grad_value = lax.map(
        head_backward, (query, keyset, value, segments, tops, totals, grad_heads)
    )
    grad_qkv = jnp.concatenate(
        [merge_heads(grad_query, rows), merge_heads(grad_key, rows), merge_heads(grad_value, rows)],
        axis=1,
    ).astype(jnp.bfloat16)
    grad_wqkv = outer_sum(first, grad_qkv)
    grad_first = against(grad_qkv, w_qkv)
    first_back = jax.vjp(layer_norm, inputs, gains[0], gains[1])[1]
    grad_in_norm, grad_gain_one, grad_shift_one = first_back(grad_first)
    input_grad = (grad_middle + grad_in_norm).astype(jnp.bfloat16)
    grad_norms = jnp.stack([grad_gain_one, grad_shift_one, grad_gain_two, grad_shift_two])
    owned = (
        lax.psum_scatter(grad_norms, "fsdp", scatter_dimension=1, tiled=True),
        lax.psum_scatter(grad_wqkv, "fsdp", scatter_dimension=1, tiled=True),
        lax.psum_scatter(grad_proj, "fsdp", scatter_dimension=1, tiled=True),
        lax.psum_scatter(grad_up, "fsdp", scatter_dimension=1, tiled=True),
        lax.psum_scatter(grad_down, "fsdp", scatter_dimension=1, tiled=True),
    )
    summed = (
        lax.psum(owned[0].astype(jnp.bfloat16), "rep").astype(jnp.float32),
        lax.psum(owned[1].astype(jnp.bfloat16), "rep").astype(jnp.float32),
        lax.psum(owned[2].astype(jnp.bfloat16), "rep").astype(jnp.float32),
        lax.psum(owned[3].astype(jnp.bfloat16), "rep").astype(jnp.float32),
        lax.psum(owned[4].astype(jnp.bfloat16), "rep").astype(jnp.float32),
    )
    keep_rate = 1.0 - ema_rate
    new_norms = ema_rate * target_norms + keep_rate * norm_params.astype(jnp.float32)
    new_qkv = ema_rate * target_qkv + keep_rate * qkv_weight.astype(jnp.float32)
    new_proj = ema_rate * target_proj + keep_rate * proj_weight.astype(jnp.float32)
    new_up = ema_rate * target_up + keep_rate * up_weight.astype(jnp.float32)
    new_down = ema_rate * target_down + keep_rate * down_weight.astype(jnp.float32)
    return (
        block_output,
        input_grad,
        summed[0],
        summed[1],
        summed[2],
        summed[3],
        summed[4],
        new_norms,
        new_qkv,
        new_proj,
        new_up,
        new_down,
    )


def solution(mesh):
    return jax.shard_map(
        per_device,
        mesh=mesh,
        in_specs=(
            P(("fsdp", "rep"), None),
            P(("fsdp", "rep")),
            P(("fsdp", "rep"), None),
            P(None, "fsdp"),
            P(None, "fsdp"),
            P(None, "fsdp"),
            P(None, "fsdp"),
            P(None, "fsdp"),
            P(None, "fsdp"),
            P(None, "fsdp"),
            P(None, "fsdp"),
            P(None, "fsdp"),
            P(None, "fsdp"),
        ),
        out_specs=(
            P(("fsdp", "rep"), None),
            P(("fsdp", "rep"), None),
            P(None, "fsdp"),
            P(None, "fsdp"),
            P(None, "fsdp"),
            P(None, "fsdp"),
            P(None, "fsdp"),
            P(None, "fsdp"),
            P(None, "fsdp"),
            P(None, "fsdp"),
            P(None, "fsdp"),
            P(None, "fsdp"),
        ),
        check_vma=False,
    )
```

profile of v0, /device:TPU:0, one launch (start us, length us, event | category | flops | bytes accessed | tf_op | source)
XLA Modules:
  0.0 1168.2 jit_solution(18009675124772495406)
XLA Ops:
  16.7 10.4 all-gather
  32.0 14.6 %all-gather.6.cloned.1.call-done = bf16[768,2304]{0,1:T(8,128)(2,1)} async-done(((bf16[768,288]{0,1:T(8,128)(2,1)}), bf16[768,2304]{0,1:T(8,128)(2,1)}) %all-gather.6.cloned.1.call-update) | async-done | bytes 3538960 | tf_op jit(solution)/shard_map/all_gather | solution.py:99
  46.6 10.6 convolution_convert_fusion
  65.9 6.1 reshape.164
  72.0 9.8 copy.144
  86.6 6.1 reshape.166
  92.7 9.9 copy.145
  107.3 6.1 reshape.168
  113.4 9.7 copy.146
  125.2 152.9 %while.28 = (s32[]{:T(128)}, bf16[24,1024,64]{1,2,0:T(8,128)(2,1)}, f32[24,1024,1]{1,2,0:T(1,128)}, f32[24,1024,1]{1,2,0:T(1,128)}, s32[24,1024]{1,0:T(8,128)S(1...) while((s32[]{:T(128)}, bf16[24,1024,64]{1,2,0:T(8,128)(2,1)}, ...), condition=%wide.region_5.6_spmd, body=%wide.region_2.5_spmd.sunk | while | flops 284162048 | bytes 13699681 | solution.py:116
  278.2 5.2 copy.125
  296.4 67.5 %multiply_convert_fusion.1 = (bf16[2048,3072]{1,0:T(8,128)(2,1)}, f32[2048,3072]{1,0:T(8,128)}, f32[2048,3072]{1,0:T(8,128)}) fusion(bf16[768,3072]{1,0:T(8,128)(2,1)} %all-gather.10.cloned.1.call-done, bf16[2048,768]{0,1:T(8,128)(2,1)} %add_convert_fusion.4.clone.4), kind=kOutput, calls=%fused_computation.61 | convolution fusion | flops 10072621056 | bytes 70778880 | tf_op jit(solution)/shard_map/dot_general | solution.py:25
  364.0 27.9 %add_convert_fusion = bf16[2048,3072]{1,0:T(8,128)(2,1)} fusion(f32[2048,3072]{1,0:T(8,128)} %get-tuple-element.291, f32[2048,3072]{1,0:T(8,128)} %get-tuple-element.305, bf16[3072,768]{0,1:T(8,128)(2,1)} %all-gather.12.cloned.1.call-done, bf16[2048,768]{0,1:T(8,128)(2,1)S(1)} %copy-done.6, f32[2048]{0:T(1024)S(1)} %copy-done.21), kind=kOutput, calls=%fused_computation.60 | convolution fusion | flops 9756475392 | bytes 70787072 | tf_op jit(solution)/shard_map/dot_general | solution.py:35
  391.9 16.6 %fusion.79 = (f32[768]{0:T(1024)}, f32[2048,768]{1,0:T(8,128)}) fusion(bf16[2048,3072]{1,0:T(8,128)(2,1)} %add_convert_fusion, bf16[768,3072]{1,0:T(8,128)(2,1)} %all-gather.10.cloned.1.call-done), kind=kOutput, calls=%fused_computation.135 | convolution fusion | flops 9665248256 | bytes 23596032 | tf_op jit(solution)/shard_map/dot_general | solution.py:35
  408.4 6.7 copy.128
  415.2 6.7 multiply_reduce_fusion.1
  433.3 5.3 convolution_convert_fusion.1
  445.7 9.8 copy.149
  460.1 320.7 %while.29 = (s32[]{:T(128)}, bf16[24,1024,64]{1,2,0:T(8,128)(2,1)S(1)}, bf16[24,1024,64]{1,2,0:T(8,128)(2,1)}, bf16[24,1024,64]{1,2,0:T(8,128)(2,1)}, s32[24,102...) while((s32[]{:T(128)}, ...), condition=%wide.region_12.13_spmd, body=%wide.region_10.12_spmd.sunk | while | flops 682753024 | bytes 34133116 | solution.py:146
  789.4 5.3 copy.137
  800.6 10.0 fusion.70
  811.4 17.0 %fusion.73 = f32[768,3072]{1,0:T(8,128)} fusion(bf16[2048,3072]{1,0:T(8,128)(2,1)} %add_convert_fusion, f32[2048,768]{0,1:T(8,128)} %copy-done.2, f32[768]{0:T(1024)S(1)} %copy-done.35, f32[768]{0:T(1024)S(1)} %copy-done.33, f32[2048]{0:T(1024)S(1)} %copy-done.20, f32[2048]{0:T(1024)S(1)} %copy-done.15), kind=kOutput, calls=%fused_computation.130 | convolution fusion | flops 9671540736 | bytes 28334080 | tf_op jit(solution)/shard_map/dot_general | solution.py:29
  828.5 16.1 %fusion.66 = f32[3072,768]{0,1:T(8,128)} fusion(bf16[2048,3072]{1,0:T(8,128)(2,1)} %get-tuple-element.290, bf16[2048,768]{0,1:T(8,128)(2,1)} %copy.127, f32[2048]{0:T(1024)S(1)} %copy-done.21), kind=kOutput, calls=%fused_computation.102 | convolution fusion | flops 9668395008 | bytes 25174016 | tf_op jit(solution)/shard_map/dot_general | solution.py:29
  854.1 12.1 %fusion.80 = (f32[768]{0:T(1024)S(1)}, f32[2048,768]{1,0:T(8,128)}) fusion(bf16[2048,2304]{0,1:T(8,128)(2,1)} %copy-done.12, bf16[768,2304]{0,1:T(8,128)(2,1)S(1)} %copy-done.43), kind=kOutput, calls=%fused_computation.136 | convolution fusion | flops 7249329152 | bytes 19270656 | tf_op jit(solution)/shard_map/dot_general | solution.py:35
  866.1 6.6 copy.138
  882.0 10.0 add_convert_fusion.1
  900.6 55.7 %reduce-scatter.12.cloned.1.call-done = f32[768,384]{1,0:T(8,128)} async-done(((f32[768,3072]{1,0:T(8,128)}), f32[768,384]{1,0:T(8,128)}) %reduce-scatter.12.cloned.1.call-update) | async-done | bytes 1179664 | tf_op jit(solution)/shard_map/reduce_scatter | solution.py:163
  958.5 77.9 %reduce-scatter.14.cloned.1.call-done = f32[3072,96]{0,1:T(8,128)} async-done(((f32[3072,768]{0,1:T(8,128)}), f32[3072,96]{0,1:T(8,128)}) %reduce-scatter.14.cloned.1.call-update) | async-done | bytes 1179664 | tf_op jit(solution)/shard_map/reduce_scatter | solution.py:164
  1038.5 17.1 %multiply_convert_fusion.3 = bf16[2048,768]{0,1:T(8,128)(2,1)S(1)} fusion(f32[2048,768]{0,1:T(8,128)} %copy-done.2, bf16[2048,3072]{1,0:T(8,128)(2,1)} %get-tuple-element.290, bf16[3072,768]{0,1:T(8,128)(2,1)} %all-gather.12.cloned.1.call-done, f32[2048]{0:T(1024)S(1)} %copy-done.21), kind=kOutput, calls=%fused_computation.97 | convolution fusion | flops 9668395008 | bytes 26746880 | tf_op jit(solution)/shard_map/dot_general | solution.py:25
  1058.4 14.9 %reduce-scatter.16.cloned.1.call-done = f32[96,4]{1,0:T(8,128)} async-done(((f32[768,4]{1,0:T(8,128)}), f32[96,4]{1,0:T(8,128)}) %reduce-scatter.16.cloned.1.call-update) | async-done | bytes 1552
  1074.2 11.8 %psum.35 = bf16[4,96]{1,0:T(4,128)(2,1)S(1)} all-reduce(bf16[4,96]{1,0:T(4,128)(2,1)S(1)} %copy.152), channel_id=1, replica_groups=mesh['fsdp'=8,'rep'=4] {'rep'}, use_global_device_ids=true, to_apply=%region_20.21 | all-reduce | flops 384 | bytes 1536 | tf_op jit(solution)/shard_map/psum | solution.py:167
  1086.5 66.5 %all-reduce.3.cloned.1.call-done = (bf16[768,288]{0,1:T(8,128)(2,1)}, bf16[768,96]{0,1:T(8,128)(2,1)}, bf16[768,384]{1,0:T(8,128)(2,1)}, bf16[3072,96]{0,1:T(8,128)(2,1)}) async-done(((bf16[768,288]{0,1:T(8,128)(2,1)}, bf16[768,96]{0,1:T(8,128)(2,1)}, bf16[768,384]{1,0:T(8,128)(2,1)}, bf16[3072,96]{0,1:T(8,128)(2,1)}), (bf16[768,288]{0,1:T(8,128)(2,1)}, bf16[768,96]{0,1:T(8,128)(2,1)}, ...) | async-done | bytes 1769488 | tf_op jit(solution)/shard_map/psum | solution.py:168
  (501 shorter events, 601.4 us)
Async XLA Ops:
  7.2 39.4 %all-gather.6.cloned.1.call-start = ((), (), s32[]{:S(2)}) async-start(), calls=%async_computation.5 | async-start | bytes 3981312 | tf_op jit(solution)/shard_map/all_gather | solution.py:99
  7.9 278.2 %all-gather.8.cloned.1.call-start = ((), (), s32[]{:S(2)}) async-start(), calls=%async_computation.6 | async-start | bytes 1327104 | tf_op jit(solution)/shard_map/all_gather | solution.py:100
  8.7 287.7 %all-gather.10.cloned.1.call-start = ((), (), s32[]{:S(2)}) async-start(), calls=%async_computation.7 | async-start | bytes 5308416 | tf_op jit(solution)/shard_map/all_gather | solution.py:101
  9.4 354.5 %all-gather.12.cloned.1.call-start = ((), (), s32[]{:S(2)}) async-start(), calls=%async_computation.8 | async-start | bytes 5308416 | tf_op jit(solution)/shard_map/all_gather | solution.py:102
  10.0 887.0 %reduce-scatter.10.cloned.1.call-start = ((), (), s32[]{:S(2)}) async-start(), calls=%async_computation.10 | async-start | bytes 2654208 | tf_op jit(solution)/shard_map/reduce_scatter | solution.py:162
  15.2 270.8 %copy-start = (bf16[2048,768]{0,1:T(8,128)(2,1)}, bf16[2048,768]{0,1:T(8,128)(2,1)S(1)}, u32[]{:S(2)}) copy-start(bf16[2048,768]{0,1:T(8,128)(2,1)S(1)} %copy.114) | copy-start | bytes 9437188
  15.8 41.5 %copy-start.16 = (f32[2048]{0:T(1024)}, f32[2048]{0:T(1024)S(1)}, u32[]{:S(2)}) copy-start(f32[2048]{0:T(1024)S(1)} %broadcast_multiply_fusion.1) | copy-start | bytes 24580
  16.6 10.5 copy-start.24
  16.6 40.6 %copy-start.28 = (f32[2048]{0:T(1024)}, f32[2048]{0:T(1024)S(1)}, u32[]{:S(2)}) copy-start(f32[2048]{0:T(1024)S(1)} %fusion.68) | copy-start | bytes 24580
  27.2 30.1 %copy-start.30 = (f32[768]{0:T(1024)}, f32[768]{0:T(1024)S(1)}, u32[]{:S(2)}) copy-start(f32[768]{0:T(1024)S(1)} %get-tuple-element.245) | copy-start | bytes 9220
  27.2 30.1 %copy-start.37 = (f32[768]{0:T(1024)}, f32[768]{0:T(1024)S(1)}, u32[]{:S(2)}) copy-start(f32[768]{0:T(1024)S(1)} %get-tuple-element.244) | copy-start | bytes 9220
  27.2 265.6 %copy-start.32 = (f32[768]{0:T(1024)}, f32[768]{0:T(1024)S(1)}, u32[]{:S(2)}) copy-start(f32[768]{0:T(1024)S(1)} %get-tuple-element.242) | copy-start | bytes 9220
  27.2 265.6 %copy-start.34 = (f32[768]{0:T(1024)}, f32[768]{0:T(1024)S(1)}, u32[]{:S(2)}) copy-start(f32[768]{0:T(1024)S(1)} %get-tuple-element.243) | copy-start | bytes 9220
  278.2 7.9 copy-start.18
  296.4 67.5 %copy-start.6 = (bf16[2048,768]{0,1:T(8,128)(2,1)S(1)}, bf16[2048,768]{0,1:T(8,128)(2,1)}, u32[]{:S(2)}) copy-start(bf16[2048,768]{0,1:T(8,128)(2,1)} %copy.127) | copy-start | bytes 9437188
  296.4 67.5 %copy-start.21 = (f32[2048]{0:T(1024)S(1)}, f32[2048]{0:T(1024)}, u32[]{:S(2)}) copy-start(f32[2048]{0:T(1024)} %compare_convert_fusion) | copy-start | bytes 24580
  408.4 6.7 copy-start.15
  408.4 6.7 copy-start.20
  408.4 6.7 copy-start.33
  408.4 13.5 %slice-start = ((s8[6291456]{0:T(1024)(128)(4,1)}), s8[2097152]{0:T(1024)(128)(4,1)S(1)}, s32[]{:S(2)}) async-start(s8[6291456]{0:T(1024)(128)(4,1)} %bitcast.182), calls=%async_computation.15 | async-start | bytes 4194304
  415.2 6.8 copy-start.27
  415.2 6.8 slice-start.1
  415.2 7.7 copy-start.4
  455.5 443.1 %reduce-scatter.8.cloned.1.call-start = ((), (), s32[]{:S(2)}) async-start(), calls=%async_computation.9 | async-start | bytes 7962624 | tf_op jit(solution)/shard_map/reduce_scatter | solution.py:161
  810.7 145.6 %reduce-scatter.12.cloned.1.call-start = ((), (), s32[]{:S(2)}) async-start(), calls=%async_computation.11 | async-start | bytes 10616832 | tf_op jit(solution)/shard_map/reduce_scatter | solution.py:163
  828.4 207.9 %reduce-scatter.14.cloned.1.call-start = ((), (), s32[]{:S(2)}) async-start(), calls=%async_computation.12 | async-start | bytes 10616832 | tf_op jit(solution)/shard_map/reduce_scatter | solution.py:164
  844.6 228.7 %reduce-scatter.16.cloned.1.call-start = ((), (), s32[]{:S(2)}) async-start(), calls=%async_computation.13 | async-start | bytes 442368
  845.2 7.6 copy-start.10
  845.2 7.6 copy-start.11
  845.2 8.8 copy-start.43
  876.8 5.2 copy-start.23
  881.7 271.3 %all-reduce.3.cloned.1.call-start = ((), (), s32[]{:S(2)}) async-start(), calls=%async_computation.14 | async-start | bytes 3538944 | tf_op jit(solution)/shard_map/psum | solution.py:168
  (24 other events, 75.4 us)
Sparse Core Ops, SparseCore 0:
  9.9 36.6 all-gather.5
  48.5 24.0 all-gather.7
  74.5 39.7 all-gather.9
  116.0 38.9 all-gather.11
  455.6 42.4 reduce-scatter.9
  810.8 65.4 reduce-scatter.7
  879.8 76.4 reduce-scatter.11
  959.8 76.4 reduce-scatter.13
  1039.4 33.8 reduce-scatter.15
  1076.4 76.5 all-reduce.2
where the time goes:
time: 1190 us; the launch traced here: 1170 us
  matrix products  579 us (49%)
  waiting for transfers between devices  232 us (19%)
  local copies, waits for them, and re-layouts  206 us (17%)
  other arithmetic  111 us (9%)
  blocking collectives  22.2 us (2%)
  between operations  15.3 us (1%)
    dot_general x76, matrix products, against(): lax.dot_general(left, right, (((1,), (1,)), ((), ())), preferred_element_...  211 us
    dot_general x52, matrix products, product(): return jnp.dot(left, right, preferred_element_type=jnp.float32)  206 us
    dot_general x52, matrix products, outer_sum(): lax.dot_general(left, right, (((0,), (0,)), ((), ())), preferred_element_...  162 us
    reduce_scatter x1, waiting for transfers between devices, per_device(): lax.psum_scatter(grad_down, 'fsdp', scatter_dimension=1, tiled=True)  77.9 us
    psum x1, waiting for transfers between devices, per_device(): lax.psum(owned[1].astype(jnp.bfloat16), 'rep').astype(jnp.float32)  66.5 us
    reduce_scatter x1, waiting for transfers between devices, per_device(): lax.psum_scatter(grad_up, 'fsdp', scatter_dimension=1, tiled=True)  55.7 us
    reshape x4, local copies, waits for them, and re-layouts, split_heads(): shaped.transpose(0, 2, 1, 3).reshape(rows * heads, count // rows, HEAD)  39.2 us
    unnamed x104, local copies, waits for them, and re-layouts  35.3 us
  transfers between devices with their start and end apart: 10, of which 5 were waited for; matrix products, arithmetic and copies ran while one was open for 68% of the time, Pallas kernels for 0%

commit v1 on v0

v1 whole, which is shorter than its diff:
```python
import math
from functools import partial

import jax
import jax.numpy as jnp
from jax import lax
from jax.experimental import pallas as pl
from jax.experimental.pallas import tpu as pltpu
from jax.sharding import PartitionSpec as P

HEAD = 64
ROW_LEN = 1024
layer_eps = 1e-06
ema_rate = 0.75

BF = jnp.bfloat16
F32 = jnp.float32
NN = (((1,), (0,)), ((), ()))
NT = (((1,), (1,)), ((), ()))
TN = (((0,), (0,)), ((), ()))
VMEM_LIMIT = 66_000_000

QW = 256
KW = 224
FIT = KW - 15
KB = 128
STRIDE = 35


def mm(left, right, dims):
    return lax.dot_general(left, right, dims, preferred_element_type=F32)


def cost(flops, moved, exps=0):
    return pl.CostEstimate(flops=int(flops), bytes_accessed=int(moved), transcendentals=int(exps))


def job_table(segment_ids, rows, device):
    seg = segment_ids.reshape(rows, 1, ROW_LEN)
    ident = jnp.arange(16, dtype=jnp.int32)[None, :, None]
    real = seg >= 0
    starts = jnp.sum((real & (seg < ident)).astype(jnp.int32), axis=2)
    after = jnp.sum((real & (seg < ident + 1)).astype(jnp.int32), axis=2)
    images = jnp.max(seg, axis=2) + 1
    ends = jnp.where(jnp.arange(16, dtype=jnp.int32)[None, :] < images, after, ROW_LEN)
    valid = jnp.sum(real.astype(jnp.int32), axis=2)
    pad = ROW_LEN - valid
    fits = pad <= FIT
    jobs = images + jnp.where((pad > 0) & fits, 1, 0)
    wide = jnp.where(fits, 0, (pad + 15 + QW - 1) // QW)
    table = jnp.concatenate([starts, ends, jobs, valid, wide], axis=1).reshape(-1)
    return jnp.concatenate([table, device.astype(jnp.int32).reshape(1)])


def lane_of(count):
    return lax.broadcasted_iota(jnp.int32, (count, 128), 1)


def slot_of(count, base):
    return lax.broadcasted_iota(jnp.int32, (count, 128), 0) + base


def half_lanes(count, par):
    return (lane_of(count) < 64) if par == 0 else (lane_of(count) >= 64)


def spare_lane(count, par):
    return lane_of(count) == (64 if par == 0 else 0)


def query_side(q, par):
    n = q.shape[0]
    return jnp.where(half_lanes(n, par), q * BF(0.125), jnp.where(spare_lane(n, par), BF(1), BF(0)))


def key_side(k, par, inside):
    n = k.shape[0]
    return jnp.where(half_lanes(n, par), k, jnp.where(spare_lane(n, par) & (~inside), BF(-1e30), BF(0)))


def one_head(x, par):
    return jnp.where(half_lanes(x.shape[0], par), x, BF(0))


def image_window(tab, base, job):
    begin = tab[base + job]
    end = tab[base + 16 + job]
    low = lax.div(begin, 16) * 16
    q0 = pl.multiple_of(jnp.minimum(low, ROW_LEN - QW), 16)
    k0 = pl.multiple_of(jnp.minimum(low, ROW_LEN - KW), 16)
    return begin, end, q0, k0


def attend_kernel(pairs, row0, tab, q_ref, k_ref, v_ref, o_ref, a_sc):
    base = (pl.program_id(0) + row0) * STRIDE
    o_ref[...] = jnp.zeros_like(o_ref)

    def job(j, carry):
        begin, end, q0, k0 = image_window(tab, base, j)
        kr = slot_of(KW, k0)
        inside = (kr >= begin) & (kr < end)
        qr = slot_of(QW, q0)
        qin = (qr >= begin) & (qr < end)
        scores = []
        for p in range(pairs):
            cs = pl.ds(128 * p, 128)
            q = q_ref[pl.ds(q0, QW), cs]
            k = k_ref[pl.ds(k0, KW), cs]
            for par in range(2):
                scores.append(mm(key_side(k, par, inside), query_side(q, par), NT))
        probs = []
        for st in scores:
            expo = jnp.exp(st - jnp.max(st, axis=0, keepdims=True))
            total = jnp.sum(expo, axis=0, keepdims=True)
            probs.append((expo * (1.0 / total)).astype(BF))
        for p in range(pairs):
            cs = pl.ds(128 * p, 128)
            v = v_ref[pl.ds(k0, KW), cs]
            o = jnp.concatenate(
                [mm(v[:, 64 * par : 64 * par + 64], probs[2 * p + par], TN) for par in range(2)], axis=0
            ).T
            o_ref[pl.ds(q0, QW), cs] = jnp.where(qin, o.astype(BF), o_ref[pl.ds(q0, QW), cs])
        return carry

    lax.fori_loop(0, tab[base + 32], job, 0)

    start = tab[base + 33]
    low = lax.div(start, 16) * 16

    def wide(i, carry):
        q0 = pl.multiple_of(jnp.minimum(low + i * QW, ROW_LEN - QW), 16)
        qin = slot_of(QW, q0) >= start
        for p in range(pairs):
            cs = pl.ds(128 * p, 128)
            q = q_ref[pl.ds(q0, QW), cs]
            for par in range(2):
                qs = query_side(q, par)

                def block(kb):
                    k0 = pl.multiple_of(kb * KB, KB)
                    k = k_ref[pl.ds(k0, KB), cs]
                    return k0, mm(key_side(k, par, slot_of(KB, k0) >= start), qs, NT)

                def take_max(kb, top):
                    return jnp.maximum(top, jnp.max(block(kb)[1], axis=0, keepdims=True))

                top = lax.fori_loop(0, ROW_LEN // KB, take_max, jnp.full((1, QW), -1e30, F32))

                def take_sum(kb, total):
                    return total + jnp.sum(jnp.exp(block(kb)[1] - top), axis=0, keepdims=True)

                total = lax.fori_loop(0, ROW_LEN // KB, take_sum, jnp.zeros((1, QW), F32))
                a_sc[...] = jnp.zeros_like(a_sc)

                def take_out(kb, c):
                    k0, st = block(kb)
                    prob = (jnp.exp(st - top) * (1.0 / total)).astype(BF)
                    a_sc[...] += mm(one_head(v_ref[pl.ds(k0, KB), cs], par), prob, TN)
                    return c

                lax.fori_loop(0, ROW_LEN // KB, take_out, 0)
                hit = qin & half_lanes(QW, par)
                o_ref[pl.ds(q0, QW), cs] = jnp.where(hit, a_sc[...].T.astype(BF), o_ref[pl.ds(q0, QW), cs])
        return carry

    lax.fori_loop(0, tab[base + 34], wide, 0)


def attend_back_kernel(pairs, row0, tab, q_ref, k_ref, v_ref, d_ref, *rest):
    dq_ref, dk_ref, dv_ref, a_sc, dk_sc, dv_sc = rest[-6:]
    base = (pl.program_id(0) + row0) * STRIDE
    dq_ref[...] = jnp.zeros_like(dq_ref)
    dk_ref[...] = jnp.zeros_like(dk_ref)
    dv_ref[...] = jnp.zeros_like(dv_ref)

    def job(j, carry):
        begin, end, q0, k0 = image_window(tab, base, j)
        kr = slot_of(KW, k0)
        inside = (kr >= begin) & (kr < end)
        qr = slot_of(QW, q0)
        qin = (qr >= begin) & (qr < end)
        ks = pl.ds(k0, KW)
        qs = pl.ds(q0, QW)
        scores = []
        grads = []
        for p in range(pairs):
            cs = pl.ds(128 * p, 128)
            q = q_ref[qs, cs]
            k = k_ref[ks, cs]
            v = v_ref[ks, cs]
            d = jnp.where(qin, d_ref[qs, cs], BF(0))
            for par in range(2):
                scores.append(mm(key_side(k, par, inside), query_side(q, par), NT))
                grads.append(mm(v, one_head(d, par), NT))
        probs = []
        dscores = []
        for st, dp in zip(scores, grads):
            expo = jnp.exp(st - jnp.max(st, axis=0, keepdims=True))
            total = jnp.sum(expo, axis=0, keepdims=True)
            prob = expo * (1.0 / total)
            center = jnp.sum(prob * dp, axis=0, keepdims=True)
            dscores.append((prob * (dp - center)).astype(BF))
            probs.append(prob.astype(BF))
        for p in range(pairs):
            cs = pl.ds(128 * p, 128)
            q = q_ref[qs, cs]
            k = k_ref[ks, cs]
            d = jnp.where(qin, d_ref[qs, cs], BF(0))
            dv = mm(probs[2 * p], one_head(d, 0), NN) + mm(probs[2 * p + 1], one_head(d, 1), NN)
            dk = mm(dscores[2 * p], one_head(q, 0), NN) + mm(dscores[2 * p + 1], one_head(q, 1), NN)
            dq = jnp.concatenate(
                [mm(k[:, 64 * par : 64 * par + 64], dscores[2 * p + par], TN) for par in range(2)], axis=0
            ).T
            dq_ref[qs, cs] = jnp.where(qin, (dq * 0.125).astype(BF), dq_ref[qs, cs])
            dk_ref[ks, cs] = jnp.where(inside, (dk * 0.125).astype(BF), dk_ref[ks, cs])
            dv_ref[ks, cs] = jnp.where(inside, dv.astype(BF), dv_ref[ks, cs])
        return carry

    lax.fori_loop(0, tab[base + 32], job, 0)

    start = tab[base + 33]
    low = lax.div(start, 16) * 16
    windows = tab[base + 34]
    for p in range(pairs):
        cs = pl.ds(128 * p, 128)

        @pl.when(windows > 0)
        def _():
            dk_sc[...] = jnp.zeros_like(dk_sc)
            dv_sc[...] = jnp.zeros_like(dv_sc)

        def wide(i, carry):
            first = jnp.maximum(start, low + i * QW)
            q0 = pl.multiple_of(jnp.minimum(low + i * QW, ROW_LEN - QW), 16)
            qin = slot_of(QW, q0) >= first
            q = q_ref[pl.ds(q0, QW), cs]
            d = jnp.where(qin, d_ref[pl.ds(q0, QW), cs], BF(0))
            for par in range(2):
                qh = query_side(q, par)
                dh = one_head(d, par)
                qo = one_head(q, par)

                def block(kb):
                    k0 = pl.multiple_of(kb * KB, KB)
                    k = k_ref[pl.ds(k0, KB), cs]
                    v = v_ref[pl.ds(k0, KB), cs]
                    return k0, k, mm(key_side(k, par, slot_of(KB, k0) >= start), qh, NT), mm(v, dh, NT)

                def take_max(kb, top):
                    return jnp.maximum(top, jnp.max(block(kb)[2], axis=0, keepdims=True))

                top = lax.fori_loop(0, ROW_LEN // KB, take_max, jnp.full((1, QW), -1e30, F32))

                def take_sums(kb, sums):
                    _, _, st, dp = block(kb)
                    expo = jnp.exp(st - top)
                    return (
                        sums[0] + jnp.sum(expo, axis=0, keepdims=True),
                        sums[1] + jnp.sum(expo * dp, axis=0, keepdims=True),
                    )

                none = jnp.zeros((1, QW), F32)
                total, weighted = lax.fori_loop(0, ROW_LEN // KB, take_sums, (none, none))
                scale = 1.0 / total
                center = weighted * scale
                a_sc[...] = jnp.zeros_like(a_sc)

                def take_grads(kb, c):
                    k0, k, st, dp = block(kb)
                    prob = jnp.exp(st - top) * scale
                    ds = (prob * (dp - center)).astype(BF)
                    a_sc[...] += mm(one_head(k, par), ds, TN)
                    dk_sc[pl.ds(k0, KB), :] += mm(ds, qo, NN)
                    dv_sc[pl.ds(k0, KB), :] += mm(prob.astype(BF), dh, NN)
                    return c

                lax.fori_loop(0, ROW_LEN // KB, take_grads, 0)
                hit = qin & half_lanes(QW, par)
                dq = (a_sc[...].T * 0.125).astype(BF)
                dq_ref[pl.ds(q0, QW), cs] = jnp.where(hit, dq, dq_ref[pl.ds(q0, QW), cs])
            return carry

        lax.fori_loop(0, windows, wide, 0)

        @pl.when(windows > 0)
        def _():
            kin = slot_of(ROW_LEN, 0) >= start
            dk_ref[:, cs] = jnp.where(kin, (dk_sc[...] * 0.125).astype(BF), dk_ref[:, cs])
            dv_ref[:, cs] = jnp.where(kin, dv_sc[...].astype(BF), dv_ref[:, cs])


def attention_forward(qkv, table, rows, pairs=6):
    n = qkv.shape[0]
    width = qkv.shape[1] // 3
    w = 128 * pairs
    g = width // w
    spec = lambda part: pl.BlockSpec((ROW_LEN, w), lambda r, h, t: (r, part * g + h))
    return pl.pallas_call(
        partial(attend_kernel, pairs, 0),
        out_shape=jax.ShapeDtypeStruct((n, width), BF),
        grid_spec=pltpu.PrefetchScalarGridSpec(
            num_scalar_prefetch=1,
            grid=(rows, g),
            in_specs=[spec(0), spec(1), spec(2)],
            out_specs=spec(0),
            scratch_shapes=[pltpu.VMEM((128, QW), F32)],
        ),
        compiler_params=pltpu.CompilerParams(vmem_limit_bytes=VMEM_LIMIT),
        cost_estimate=cost(18e9, n * width * 8),
        name="attend",
    )(table, qkv, qkv, qkv)


def attention_backward(qkv, da, table, row, rows, before, pairs=6):
    n = qkv.shape[0]
    width = qkv.shape[1] // 3
    w = 128 * pairs
    g = width // w
    spec = lambda part: pl.BlockSpec((ROW_LEN, w), lambda r, h, t: (r + row, part * g + h))
    anywhere = pl.BlockSpec(memory_space=pl.ANY)
    extra = list(before) if before is not None else []
    return pl.pallas_call(
        partial(attend_back_kernel, pairs, row),
        out_shape=[jax.ShapeDtypeStruct((n, width), BF)] * 3,
        grid_spec=pltpu.PrefetchScalarGridSpec(
            num_scalar_prefetch=1,
            grid=(rows, g),
            in_specs=[spec(0), spec(1), spec(2), spec(0)] + [anywhere] * len(extra),
            out_specs=[spec(0)] * 3,
            scratch_shapes=[
                pltpu.VMEM((128, QW), F32),
                pltpu.VMEM((ROW_LEN, 128), F32),
                pltpu.VMEM((ROW_LEN, 128), F32),
            ],
        ),
        input_output_aliases={5 + i: i for i in range(len(extra))},
        compiler_params=pltpu.CompilerParams(vmem_limit_bytes=VMEM_LIMIT),
        cost_estimate=cost(18e9 * rows, rows * ROW_LEN * width * 14),
        name="attend_back",
    )(table, qkv, qkv, qkv, da, *extra)


def hop(value, bit, size):
    return lax.ppermute(value, "fsdp", [(i, i ^ bit) for i in range(size)])


def gather_cross(shard):
    half = shard.shape[0] // 2
    along_x = hop(shard, 2, 8)
    along_y = hop(shard, 4, 8)
    first = hop(along_x[:half], 4, 8)
    second = hop(along_y[half:], 2, 8)
    return [(shard, 0, 0), (along_x, 2, 0), (along_y, 4, 0), (first, 6, 0), (second, 6, half)]


def gather(shard, size):
    if size != 8:
        return [(lax.all_gather(shard, "fsdp", axis=0, tiled=True), None, 0)]
    pieces = gather_cross(shard)
    return pieces + [(hop(array, 1, 8), slot + 1, row) for array, slot, row in pieces]


def after(value, *others):
    return lax.optimization_barrier((value, *others))[0]


def low_sum(a, b):
    return (a.astype(F32) + b.astype(F32)).astype(BF)


def scatter_core(even, odd):
    return even, hop(odd, 1, 8)


def scatter_cross(even, received):
    half = even.shape[1] // 2
    add = lambda q, part: low_sum(even[q, part], received[q, part])
    up, down = slice(0, half), slice(half, None)
    from_x = hop(jnp.stack([add(1, up), add(3, up)]), 2, 8)
    from_y = hop(jnp.stack([add(2, down), add(3, down)]), 4, 8)
    up_own = low_sum(add(0, up), from_x[0])
    down_own = low_sum(add(0, down), from_y[0])
    up_last = hop(low_sum(add(2, up), from_x[1]), 4, 8)
    down_last = hop(low_sum(add(1, down), from_y[1]), 2, 8)
    return jnp.concatenate([low_sum(up_own, up_last), low_sum(down_own, down_last)], axis=0)


def replica_sum(block, size):
    if size != 4:
        return lax.psum(block, "rep").astype(F32)
    z = lax.axis_index("rep")
    inner = low_sum(block, lax.ppermute(block, "rep", [(0, 1), (3, 2)]))
    whole = low_sum(inner, lax.ppermute(inner, "rep", [(1, 2), (2, 1)]))
    outer = lax.ppermute(whole, "rep", [(1, 0), (2, 3)])
    return jnp.where((z == 1) | (z == 2), whole, outer).astype(F32)


def everywhere_sum(value, size, replicas):
    if size != 8 or replicas not in (None, 4):
        return lax.psum(value, "fsdp" if replicas is None else ("fsdp", "rep"))
    for bit in (1, 2, 4):
        value = value + hop(value, bit, 8)
    if replicas is not None:
        for bit in (1, 2):
            value = value + lax.ppermute(value, "rep", [(i, i ^ bit) for i in range(4)])
    return value


class Pieces:
    def __init__(self, pieces, per):
        self.arrays = [p[0] for p in pieces]
        self.places = [(p[1], p[2]) for p in pieces]
        self.per = per

    def copies(self, refs, dst, sems, me, cols=None):
        out = []
        for i, (ref, (slot, row)) in enumerate(zip(refs, self.places)):
            src = ref if cols is None else ref.at[:, cols]
            if slot is None:
                into = dst
            else:
                at = pl.multiple_of((me ^ slot) * self.per + row, math.gcd(self.per, row) if row else self.per)
                into = dst.at[pl.ds(at, ref.shape[0]), :]
            out.append(pltpu.make_async_copy(src, into, sems.at[i]))
        return out


def norm_stats(values):
    center = values - jnp.mean(values, axis=1, keepdims=True)
    rate = lax.rsqrt(jnp.mean(center * center, axis=1, keepdims=True) + layer_eps)
    return center * rate, rate


def norm_back(unit, rate, gain, grad):
    scaled = grad * gain
    mean = jnp.mean(scaled, axis=1, keepdims=True)
    along = jnp.mean(scaled * unit, axis=1, keepdims=True)
    return rate * (scaled - mean - unit * along)


def project_kernel(weight, count, tab, nrm_ref, x_ref, *rest):
    w_refs = rest[:count]
    h_ref, qkv_ref, w_sc, sems = rest[count:]
    me = tab[tab.shape[0] - 1]

    @pl.when(pl.program_id(0) == 0)
    def _():
        copies = weight.copies(w_refs, w_sc, sems, me)
        for c in copies:
            c.start()
        for c in copies:
            c.wait()

    unit, _ = norm_stats(x_ref[...].astype(F32))
    h = (unit * nrm_ref[0:1, :] + nrm_ref[1:2, :]).astype(BF)
    h_ref[...] = h
    width = x_ref.shape[1]
    for part in range(3):
        at = pl.ds(part * width, width)
        qkv_ref[:, at] = mm(h, w_sc[at, :], NT).astype(BF)


def project(table, norms, x, weight, tb=512):
    n, width = x.shape
    count = len(weight.arrays)
    anywhere = pl.BlockSpec(memory_space=pl.ANY)
    return pl.pallas_call(
        partial(project_kernel, weight, count),
        out_shape=[jax.ShapeDtypeStruct((n, width), BF), jax.ShapeDtypeStruct((n, 3 * width), BF)],
        grid_spec=pltpu.PrefetchScalarGridSpec(
            num_scalar_prefetch=1,
            grid=(n // tb,),
            in_specs=[
                pl.BlockSpec((8, width), lambda t, tab: (0, 0)),
                pl.BlockSpec((tb, width), lambda t, tab: (t, 0)),
            ]
            + [anywhere] * count,
            out_specs=[
                pl.BlockSpec((tb, width), lambda t, tab: (t, 0)),
                pl.BlockSpec((tb, 3 * width), lambda t, tab: (t, 0)),
            ],
            scratch_shapes=[pltpu.VMEM((3 * width, width), BF), pltpu.SemaphoreType.DMA((count,))],
        ),
        compiler_params=pltpu.CompilerParams(vmem_limit_bytes=VMEM_LIMIT),
        cost_estimate=cost(6 * n * width * width, n * width * 10 + 6 * width * width),
        name="project",
    )(table, norms, x, *weight.arrays)


def by_owner(acc, per, even_ref, odd_ref, me):
    for q in range(4):
        for parity, ref in ((0, even_ref), (1, odd_ref)):
            at = pl.multiple_of((me ^ (2 * q + parity)) * per, per)
            ref[q] = acc[pl.ds(at, per), :].astype(BF)


def project_grad_kernel(size, tab, dq_ref, dk_ref, dv_ref, h_ref, *rest):
    out_refs, acc = rest[:-1], rest[-1]
    t = pl.program_id(0)
    width = h_ref.shape[1]

    @pl.when(t == 0)
    def _():
        acc[...] = jnp.zeros_like(acc)

    for part, ref in enumerate((dq_ref, dk_ref, dv_ref)):
        acc[pl.ds(part * width, width), :] += mm(ref[...], h_ref[...], TN)

    @pl.when(t == pl.num_programs(0) - 1)
    def _():
        if size == 8:
            by_owner(acc, acc.shape[0] // 8, *out_refs, tab[tab.shape[0] - 1])
        else:
            out_refs[0][...] = acc[...].astype(BF)


def project_grad(table, dq, dk, dv, h, size, tb=512):
    n, width = h.shape
    rows = 3 * width
    block = pl.BlockSpec((tb, width), lambda t, tab: (t, 0))
    shapes = [(4, rows // 8, width)] * 2 if size == 8 else [(rows, width)]
    return pl.pallas_call(
        partial(project_grad_kernel, size),
        out_shape=[jax.ShapeDtypeStruct(s, BF) for s in shapes],
        grid_spec=pltpu.PrefetchScalarGridSpec(
            num_scalar_prefetch=1,
            grid=(n // tb,),
            in_specs=[block] * 4,
            out_specs=[pl.BlockSpec(s, lambda t, tab, k=len(s): (0,) * k) for s in shapes],
            scratch_shapes=[pltpu.VMEM((rows, width), F32)],
        ),
        compiler_params=pltpu.CompilerParams(vmem_limit_bytes=VMEM_LIMIT),
        cost_estimate=cost(6 * n * width * width, n * width * 8 + 6 * width * width),
        name="project_grad",
    )(table, dq, dk, dv, h)


def project_back_kernel(weight, count, tab, nrm_ref, dq_ref, dk_ref, dv_ref, x_ref, dx_ref, *rest):
    w_refs = rest[:count]
    out_ref, gn_ref, w_sc, sems = rest[count:]
    t = pl.program_id(0)
    me = tab[tab.shape[0] - 1]
    width = x_ref.shape[1]

    @pl.when(t == 0)
    def _():
        copies = weight.copies(w_refs, w_sc, sems, me)
        for c in copies:
            c.start()
        gn_ref[...] = jnp.zeros_like(gn_ref)
        for c in copies:
            c.wait()

    grad = mm(dq_ref[...], w_sc[pl.ds(0, width), :], NN)
    grad += mm(dk_ref[...], w_sc[pl.ds(width, width), :], NN)
    grad += mm(dv_ref[...], w_sc[pl.ds(2 * width, width), :], NN)
    unit, rate = norm_stats(x_ref[...].astype(F32))
    out_ref[...] = (dx_ref[...] + norm_back(unit, rate, nrm_ref[0:1, :], grad)).astype(BF)
    gn_ref[0:1, :] += jnp.sum(grad * unit, axis=0, keepdims=True)
    gn_ref[1:2, :] += jnp.sum(grad, axis=0, keepdims=True)


def project_back(table, norms, dq, dk, dv, x, dx, weight, tb=512):
    n, width = x.shape
    count = len(weight.arrays)
    anywhere = pl.BlockSpec(memory_space=pl.ANY)
    block = pl.BlockSpec((tb, width), lambda t, tab: (t, 0))
    fixed = pl.BlockSpec((8, width), lambda t, tab: (0, 0))
    return pl.pallas_call(
        partial(project_back_kernel, weight, count),
        out_shape=[jax.ShapeDtypeStruct((n, width), BF), jax.ShapeDtypeStruct((8, width), F32)],
        grid_spec=pltpu.PrefetchScalarGridSpec(
            num_scalar_prefetch=1,
            grid=(n // tb,),
            in_specs=[fixed] + [block] * 5 + [anywhere] * count,
            out_specs=[block, fixed],
            scratch_shapes=[pltpu.VMEM((3 * width, width), BF), pltpu.SemaphoreType.DMA((count,))],
        ),
        compiler_params=pltpu.CompilerParams(vmem_limit_bytes=VMEM_LIMIT),
        cost_estimate=cost(6 * n * width * width, n * width * 14 + 6 * width * width),
        name="project_back",
    )(table, norms, dq, dk, dv, x, dx, *weight.arrays)


def gelu_both(values):
    phi = 0.5 + 0.5 * lax.erf(values * math.sqrt(0.5))
    bell = jnp.exp(values * values * -0.5) * (1.0 / math.sqrt(2.0 * math.pi))
    return values * phi, phi + values * bell


def middle_kernel(size, tb, sub, chunks, w_proj, w_up, w_down, tab, nrm_ref, att_ref, x_ref, cot_ref, *rest):
    counts = [len(w.arrays) for w in (w_proj, w_up, w_down)]
    proj_refs = rest[: counts[0]]
    up_refs = rest[counts[0] : counts[0] + counts[1]]
    down_refs = rest[counts[0] + counts[1] : sum(counts)]
    rest = rest[sum(counts) :]
    outs = 6 if size == 8 else 3
    out_ref, dx_ref, da_ref, gn_ref = rest[:4]
    g_refs = rest[4 : 4 + outs]
    x1_sc, h_sc, ht_sc, dy_sc, dyt_sc, x2_sc, dh_sc, gu_sc, gd_sc, wp_sc, wu_sc, wd_sc, p_sem, u_sem, d_sem = rest[4 + outs :]
    j = pl.program_id(0)
    t = pl.program_id(1)
    steps = pl.num_programs(1)
    me = tab[tab.shape[0] - 1]
    per = ROW_LEN // tb
    valid = tab[lax.div(t, per) * STRIDE + 33]
    ok = (lax.broadcasted_iota(jnp.int32, (tb, 1), 0) + lax.rem(t, per) * tb) < valid
    ts = pl.ds(pl.multiple_of(t * tb, tb), tb)
    width = x_ref.shape[1]
    gain = nrm_ref[2:3, :]
    shift = nrm_ref[3:4, :]

    def chunk_copies(m):
        b = m % 2
        if size != 8:
            piece = pl.ds(m * width, width)
            up = [pltpu.make_async_copy(up_refs[0].at[piece, :], wu_sc.at[b], u_sem.at[b, 0])]
            down = [pltpu.make_async_copy(down_refs[0].at[:, piece], wd_sc.at[b], d_sem.at[b, 0])]
            return up + down
        up = []
        for i, (ref, (slot, row)) in enumerate(zip(up_refs, w_up.places)):
            if slot // 2 == m:
                at = pl.multiple_of(((me & 1) ^ (slot & 1)) * w_up.per + row, w_up.per // 2)
                into = wu_sc.at[b].at[pl.ds(at, ref.shape[0]), :]
                up.append(pltpu.make_async_copy(ref, into, u_sem.at[b, i]))
        piece = pl.ds(pl.multiple_of(((me >> 1) ^ m) * width, width), width)
        return up + w_down.copies(down_refs, wd_sc.at[b], d_sem.at[b], me, piece)

    @pl.when((j == 0) & (t == 0))
    def _():
        for c in w_proj.copies(proj_refs, wp_sc, p_sem, me):
            c.start()
        for c in chunk_copies(0):
            c.start()
        for c in w_proj.copies(proj_refs, wp_sc, p_sem, me):
            c.wait()

    for m in range(chunks):

        @pl.when((j == m) & (t == 0))
        def _():
            for c in chunk_copies(m):
                c.wait()
            if m + 1 < chunks:
                for c in chunk_copies(m + 1):
                    c.start()

    @pl.when(j == 0)
    def _():
        x1 = x_ref[...].astype(F32) + mm(att_ref[...], wp_sc[...], NT)
        x1_sc[ts, :] = x1
        x2_sc[ts, :] = x1
        unit, _ = norm_stats(x1)
        h = (unit * gain + shift).astype(BF)
        h_sc[ts, :] = h
        ht_sc[:, ts] = h.T
        dy = jnp.where(ok, cot_ref[...], BF(0))
        dy_sc[ts, :] = dy
        dyt_sc[:, ts] = dy.T
        dh_sc[ts, :] = jnp.zeros((tb, width), F32)

    @pl.when((t == 0) & (j < chunks))
    def _():
        gu_sc[...] = jnp.zeros_like(gu_sc)
        gd_sc[...] = jnp.zeros_like(gd_sc)

    @pl.when(j < chunks)
    def _():
        wu = wu_sc[lax.rem(j, 2)]
        wd = wd_sc[lax.rem(j, 2)]
        parts = [pl.ds(pl.multiple_of(t * tb + i * sub, sub), sub) for i in range(tb // sub)]
        uppers = [mm(h_sc[p, :], wu, NT) for p in parts]
        acts = []
        dups = []
        for p, upper in zip(parts, uppers):
            dact = mm(dy_sc[p, :], wd, NN)
            act, slope = gelu_both(upper)
            acts.append(act.astype(BF))
            dups.append((dact * slope).astype(BF))
        for p, act, dup in zip(parts, acts, dups):
            x2_sc[p, :] += mm(act, wd, NT)
            dh_sc[p, :] += mm(dup, wu, NN)
        gd_sc[...] += mm(dyt_sc[:, ts], jnp.concatenate(acts, axis=0), NN)
        gu_sc[...] += mm(ht_sc[:, ts], jnp.concatenate(dups, axis=0), NN)

    @pl.when((t == steps - 1) & (j < chunks))
    def _():
        if size == 8:
            half = w_up.per
            for parity in range(2):
                at = pl.multiple_of(((me & 1) ^ parity) * half, half)
                g_refs[parity][0] = gu_sc[:, pl.ds(at, half)].astype(BF)
            by_owner(gd_sc, w_down.per, g_refs[2], g_refs[3], me)
        else:
            g_refs[0][...] = gu_sc[...].astype(BF)
            g_refs[1][...] = gd_sc[...].astype(BF)

    @pl.when(j == chunks)
    def _():
        out_ref[...] = jnp.where(ok, x2_sc[ts, :], 0.0).astype(BF)
        unit, rate = norm_stats(x1_sc[ts, :])
        dh = dh_sc[ts, :]
        dx = dy_sc[ts, :].astype(F32) + norm_back(unit, rate, gain, dh)
        dx_ref[...] = dx
        db = dx.astype(BF)
        da_ref[...] = mm(db, wp_sc[...], NN).astype(BF)

        @pl.when(t == 0)
        def _():
            gu_sc[...] = jnp.zeros_like(gu_sc)
            gn_ref[...] = jnp.zeros_like(gn_ref)

        gu_sc[...] += mm(db, att_ref[...], TN)
        gn_ref[0:1, :] += jnp.sum(dh * unit, axis=0, keepdims=True)
        gn_ref[1:2, :] += jnp.sum(dh, axis=0, keepdims=True)

        @pl.when(t == steps - 1)
        def _():
            if size == 8:
                by_owner(gu_sc, w_proj.per, g_refs[4], g_refs[5], me)
            else:
                g_refs[2][...] = gu_sc[...].astype(BF)


def middle(table, norms, att, x, cot, w_proj, w_up, w_down, hidden, size, tb=512, sub=256):
    n, width = x.shape
    chunks = hidden // width
    steps = n // tb
    last = chunks - 1
    dev = table.shape[0] - 1
    first = lambda j, t, tab: (jnp.where(j == 0, t, steps - 1), 0)
    ends = lambda j, t, tab: (jnp.where((j == 0) | (j == chunks), t, steps - 1), 0)
    final = lambda j, t, tab: (jnp.where(j == chunks, t, 0), 0)
    fixed = lambda j, t, tab: (0, 0)
    anywhere = pl.BlockSpec(memory_space=pl.ANY)
    now = lambda j: jnp.minimum(j, last)
    sds = jax.ShapeDtypeStruct
    if size == 8:
        fw, dw = w_up.per, w_down.per
        pair = lambda j, tab: lax.bitwise_xor(lax.shift_right_logical(tab[dev], 1), now(j))
        g_shapes = [sds((4, width, fw), BF)] * 2 + [sds((4, dw, hidden), BF)] * 2 + [sds((4, dw, width), BF)] * 2
        g_specs = (
            [pl.BlockSpec((1, width, fw), lambda j, t, tab: (now(j), 0, 0))] * 2
            + [pl.BlockSpec((4, dw, width), lambda j, t, tab: (0, 0, pair(j, tab)))] * 2
            + [pl.BlockSpec((4, dw, width), lambda j, t, tab: (0, 0, 0))] * 2
        )
    else:
        g_shapes = [sds((width, hidden), BF)] * 2 + [sds((width, width), BF)]
        g_specs = [pl.BlockSpec((width, width), lambda j, t, tab: (0, now(j)))] * 2 + [
            pl.BlockSpec((width, width), fixed)
        ]
    block = lambda index: pl.BlockSpec((tb, width), index)
    weights = w_proj.arrays + w_up.arrays + w_down.arrays
    dma = pltpu.SemaphoreType.DMA
    return pl.pallas_call(
        partial(middle_kernel, size, tb, sub, chunks, w_proj, w_up, w_down),
        out_shape=[sds((n, width), BF), sds((n, width), F32), sds((n, width), BF), sds((8, width), F32)] + g_shapes,
        grid_spec=pltpu.PrefetchScalarGridSpec(
            num_scalar_prefetch=1,
            grid=(chunks + 1, steps),
            in_specs=[pl.BlockSpec((8, width), fixed), block(ends), block(first), block(first)]
            + [anywhere] * len(weights),
            out_specs=[block(final), block(final), block(final), pl.BlockSpec((8, width), fixed)] + g_specs,
            scratch_shapes=[
                pltpu.VMEM((n, width), F32),
                pltpu.VMEM((n, width), BF),
                pltpu.VMEM((width, n), BF),
                pltpu.VMEM((n, width), BF),
                pltpu.VMEM((width, n), BF),
                pltpu.VMEM((n, width), F32),
                pltpu.VMEM((n, width), F32),
                pltpu.VMEM((width, width), F32),
                pltpu.VMEM((width, width), F32),
                pltpu.VMEM((width, width), BF),
                pltpu.VMEM((2, width, width), BF),
                pltpu.VMEM((2, width, width), BF),
                dma((len(w_proj.arrays),)),
                dma((2, len(w_up.arrays))),
                dma((2, len(w_down.arrays))),
            ],
        ),
        compiler_params=pltpu.CompilerParams(vmem_limit_bytes=VMEM_LIMIT),
        cost_estimate=cost(n * width * (12 * hidden + 6 * width), n * width * 22 + 8 * hidden * width),
        name="middle",
    )(table, norms, att, x, cot, *weights)


def per_device(
    size,
    replicas,
    tokens,
    segment_ids,
    cotangent,
    norm_params,
    qkv_weight,
    proj_weight,
    up_weight,
    down_weight,
    target_norms,
    target_qkv,
    target_proj,
    target_up,
    target_down,
):
    count, width = tokens.shape
    rows = count // ROW_LEN
    hidden = down_weight.shape[0]
    own = width // size
    me = lax.axis_index("fsdp")
    with jax.named_scope("gather_weights"):
        placed = lax.dynamic_update_slice(jnp.zeros((8, width), F32), norm_params.astype(F32), (0, me * own))
        norms = everywhere_sum(placed, size, None)
        pieces = gather(qkv_weight.T, size)
        w_qkv = Pieces(pieces, qkv_weight.shape[1])
        late = after((proj_weight.T, up_weight.T, down_weight.T), *[p[0] for p in pieces[1:3]])
        w_proj = Pieces(gather(late[0], size), own)
        w_up = Pieces(gather(late[1], size), up_weight.shape[1])
        w_down = Pieces(gather(late[2], size), own)
    table = job_table(segment_ids, rows, me)

    h1, qkv = project(table, norms, tokens, w_qkv)
    attended = attention_forward(qkv, table, rows)
    block_output, grad_middle, grad_attended, grad_norm2, *grads = middle(
        table, norms, attended, tokens, cotangent, w_proj, w_up, w_down, hidden, size
    )
    dqkv = None
    for row in range(rows):
        dqkv = attention_backward(qkv, grad_attended, table, row, 1, dqkv)
    grad_qkv = project_grad(table, *dqkv, h1, size)
    input_grad, grad_norm1 = project_back(table, norms, *dqkv, tokens, grad_middle, w_qkv)

    with jax.named_scope("sum_gradients"):
        if size == 8:
            up, down, proj, qkv_own = (
                scatter_cross(*scatter_core(*pair)) for pair in (grads[0:2], grads[2:4], grads[4:6], grad_qkv)
            )
        else:
            sums = lambda g, dim: lax.psum_scatter(g, "fsdp", scatter_dimension=dim, tiled=True)
            up, down, proj, qkv_own = sums(grads[0], 1), sums(grads[1], 0), sums(grads[2], 0), sums(grad_qkv[0], 0)
        up, down, proj, qkv_own = (replica_sum(g, replicas) for g in (up, down, proj, qkv_own))
        sums = [everywhere_sum(g, size, replicas)[:2] for g in (grad_norm1, grad_norm2)]
        norm_grad = lax.dynamic_slice(jnp.concatenate(sums, axis=0), (0, me * own), (4, own))

    keep_rate = 1.0 - ema_rate
    blend = lambda target, weight: ema_rate * target + keep_rate * weight.astype(F32)
    return (
        block_output,
        input_grad,
        norm_grad,
        qkv_own.T,
        proj.T,
        up,
        down.T,
        blend(target_norms, norm_params),
        blend(target_qkv, qkv_weight),
        blend(target_proj, proj_weight),
        blend(target_up, up_weight),
        blend(target_down, down_weight),
    )


def solution(mesh):
    tokens = P(("fsdp", "rep"), None)
    columns = P(None, "fsdp")
    return jax.shard_map(
        partial(per_device, mesh.shape["fsdp"], mesh.shape["rep"]),
        mesh=mesh,
        in_specs=(tokens, P(("fsdp", "rep")), tokens) + (columns,) * 10,
        out_specs=(tokens, tokens) + (columns,) * 10,
        check_vma=False,
    )
```

time: 1190 us -> 460 us (0.39); the launches traced: 1170 us -> 455 us
  matrix products: 579 us -> 0 us
  Pallas kernels: 0 us -> 229 us
  local copies, waits for them, and re-layouts: 206 us -> 7.01 us
  waiting for transfers between devices: 232 us -> 118 us
  other arithmetic: 111 us -> 27.7 us
  starting transfers between devices: 0.86 us -> 71 us
  blocking collectives: 22.2 us -> 0 us
  between operations: 15.3 us -> 2 us
    dot_general x180 -> x0, matrix products: 579 us -> none  [the longest x76 211 us: against(): lax.dot_general(left, right, (((1,), (1,)), ((), ())), preferred_element_...]
    pallas_call x0 -> x7, Pallas kernels: none -> 229 us  [the longest x1 97.5 us: middle(): pl.pallas_call(partial(middle_kernel, size, tb, sub, chunks, w_proj, w_up...]
    reduce_scatter x4 -> x0, waiting for transfers between devices: 134 us -> none  [the longest x1 77.9 us: per_device(): lax.psum_scatter(grad_down, 'fsdp', scatter_dimension=1, tiled=True)]
    ppermute x0 -> x81, waiting for transfers between devices: none -> 118 us  [the longest x65 78.6 us: hop(): return lax.ppermute(value, 'fsdp', [(i, i ^ bit) for i in range(size)])]
    reshape x17 -> x2, local copies, waits for them, and re-layouts: 74.1 us -> 0.1 us  [the longest x1 0.08 us: job_table(): jnp.concatenate([starts, ends, jobs, valid, wide], axis=1).reshape(-1)]
    ppermute x0 -> x81, starting transfers between devices: none -> 71 us  [the longest x65 44.8 us: hop(): return lax.ppermute(value, 'fsdp', [(i, i ^ bit) for i in range(size)])]
    psum x1 -> x0, waiting for transfers between devices: 66.5 us -> none  [per_device(): lax.psum(owned[1].astype(jnp.bfloat16), 'rep').astype(jnp.float32)]
    convert_element_type x38 -> x23, other arithmetic: 59 us -> 11.5 us  [the longest x20 9.76 us: low_sum(): return (a.astype(F32) + b.astype(F32)).astype(BF)]
  transfers between devices with their start and end apart: 10 -> 81, of which waited for: 5 -> 31; matrix products, arithmetic and copies ran while one was open for 68% -> 7% of each run, Pallas kernels for 0% -> 22%
where the time goes in v1:
time: 460 us; the launch traced here: 455 us
  Pallas kernels  229 us (50%)
  waiting for transfers between devices  118 us (26%)
  starting transfers between devices  71 us (15%)
  other arithmetic  27.7 us (6%)
  local copies, waits for them, and re-layouts  7.01 us (2%)
    pallas_call x1, Pallas kernels, middle(): pl.pallas_call(partial(middle_kernel, size, tb, sub, chunks, w_proj, w_up...  97.5 us
    ppermute x65, waiting for transfers between devices, hop(): return lax.ppermute(value, 'fsdp', [(i, i ^ bit) for i in range(size)])  78.6 us
    pallas_call x2, Pallas kernels, attention_backward(): pl.pallas_call(partial(attend_back_kernel, pairs, row), out_shape=[jax.Sh...  58.3 us
    ppermute x65, starting transfers between devices, hop(): return lax.ppermute(value, 'fsdp', [(i, i ^ bit) for i in range(size)])  44.8 us
    pallas_call x1, Pallas kernels, attention_forward(): pl.pallas_call(partial(attend_kernel, pairs, 0), out_shape=jax.ShapeDtype...  27.4 us
    ppermute x4, waiting for transfers between devices, replica_sum(): outer = lax.ppermute(whole, 'rep', [(1, 0), (2, 3)])  26.6 us
    pallas_call x1, Pallas kernels, project_back(): pl.pallas_call(partial(project_back_kernel, weight, count), out_shape=[ja...  17.3 us
    pallas_call x1, Pallas kernels, project(): pl.pallas_call(partial(project_kernel, weight, count), out_shape=[jax.Sha...  15 us
  transfers between devices with their start and end apart: 81, of which 31 were waited for; matrix products, arithmetic and copies ran while one was open for 7% of the time, Pallas kernels for 22%

profile of v1, /device:TPU:0, one launch (start us, length us, event | category | flops | bytes accessed | tf_op | source)
XLA Modules:
  0.0 454.7 jit_solution(14597995089371596951)
XLA Ops:
  0.7 3.0 collective-permute-start.3
  7.5 6.5 %collective-permute-done.3.rest_1_ = bf16[288,768]{1,0:T(8,128)(2,1)S(1)} collective-permute-done((bf16[288,768]{1,0:T(8,128)(2,1)}, bf16[288,768]{1,0:T(8,128)(2,1)S(1)}, u32[]{:S(2)}, u32[]{:S(2)}) %collective-permute-start.3) | collective-permute-done | bytes 442400 | tf_op jit(solution)/shard_map/gather_weights/ppermute | solution.py:344
  20.2 2.1 collective-permute-done.1
  26.2 2.2 multiply_add_fusion
  31.8 4.2 collective-permute-done.5.rest_3_
  42.8 7.3 %collective-permute-done.21.rest_11_ = bf16[384,768]{1,0:T(8,128)(2,1)S(1)} collective-permute-done((bf16[384,768]{1,0:T(8,128)(2,1)S(1)}, bf16[384,768]{1,0:T(8,128)(2,1)S(1)}, u32[]{:S(2)}, u32[]{:S(2)}) %collective-permute-start.21) | collective-permute-done | bytes 589856 | tf_op jit(solution)/shard_map/gather_weights/ppermute | solution.py:344
  52.3 9.1 %collective-permute-done.30.rest_21_ = bf16[96,3072]{1,0:T(8,128)(2,1)S(1)} collective-permute-done((bf16[96,3072]{1,0:T(8,128)(2,1)}, bf16[96,3072]{1,0:T(8,128)(2,1)S(1)}, u32[]{:S(2)}, u32[]{:S(2)}) %collective-permute-start.30) | collective-permute-done | bytes 589856 | tf_op jit(solution)/shard_map/gather_weights/ppermute | solution.py:344
  70.3 3.0 collective-permute-done.23.rest_13_
  74.9 3.7 collective-permute-done.32.rest_23_
  78.6 15.0 %project.1 = (bf16[2048,768]{1,0:T(8,128)(2,1)}, bf16[2048,2304]{1,0:T(8,128)(2,1)}) custom-call(s32[71]{0:T(128)} %pad_add_fusion.tab, f32[8,768]{1,0:T(8,128)} %add.347.nrm_ref, bf16[2048,768]{1,0:T(8,128)(2,1)} %x_ref.5, bf16[288,768]{1,0:T(8,128)(2,1)} %bitcast.77, bf16[288,768]{1,0:T(8,128)(2,1)} %copy-done.16, bf16[288,768]{1,0:T(8,128)(2,1)} %copy-done.17, ...), custom_call_target="tpu_custom_call" | custom-call | flops 7247757312 | bytes 19267584 | tf_op jit(solution)/shard_map/project/pallas_call | solution.py:467
  95.3 27.4 %attend.1.att_ref = bf16[2048,768]{1,0:T(8,128)(2,1)} custom-call(s32[71]{0:T(128)} %pad_add_fusion.tab, bf16[2048,2304]{1,0:T(8,128)(2,1)} %get-tuple-element.37.q_ref.k_ref.v_ref, bf16[2048,2304]{1,0:T(8,128)(2,1)} %get-tuple-element.37.q_ref.k_ref.v_ref, bf16[2048,2304]{1,0:T(8,128)(2,1)} %get-tuple-element.37.q_ref.k_ref.v_ref), custom_call_target="tpu_custom_call" | custom-call | flops 17999998976 | bytes 12582912 | tf_op jit(solution)/shard_map/attend/pallas_call | solution.py:298
  123.4 97.5 %middle.1 = (bf16[2048,768]{1,0:T(8,128)(2,1)}, f32[2048,768]{1,0:T(8,128)}, bf16[2048,768]{1,0:T(8,128)(2,1)}, f32[8,768]{1,0:T(8,128)}, bf16[4,768,384]{2,1,0:...) custom-call(s32[71]{0:T(128)} %pad_add_fusion.tab, ...), custom_call_target="tpu_custom_call" | custom-call | flops 65229815808 | bytes 53477376 | tf_op jit(solution)/shard_map/middle/pallas_call | solution.py:755
  221.0 33.0 %attend_back.2 = (bf16[2048,768]{1,0:T(8,128)(2,1)}, bf16[2048,768]{1,0:T(8,128)(2,1)}, bf16[2048,768]{1,0:T(8,128)(2,1)}) custom-call(s32[71]{0:T(128)} %pad_add_fusion.tab, bf16[2048,2304]{1,0:T(8,128)(2,1)} %get-tuple-element.37.q_ref.k_ref.v_ref, bf16[2048,2304]{1,0:T(8,128)(2,1)} %get-tuple-element.37.q_ref.k_ref.v_ref, ...), custom_call_target="tpu_custom_call" | custom-call | flops 17999998976 | bytes 11010048 | tf_op jit(solution)/shard_map/attend_back/pallas_call | solution.py:322
  254.0 25.3 %attend_back.3 = (bf16[2048,768]{1,0:T(8,128)(2,1)}, bf16[2048,768]{1,0:T(8,128)(2,1)}, bf16[2048,768]{1,0:T(8,128)(2,1)}) custom-call(s32[71]{0:T(128)} %pad_add_fusion.tab, bf16[2048,2304]{1,0:T(8,128)(2,1)} %get-tuple-element.37.q_ref.k_ref.v_ref, ...), custom_call_target="tpu_custom_call", output_to_operand_aliasing={{0}: (5, {}), {1}: (6, {}), {2}: (7, {})} | custom-call | flops 17999998976 | bytes 11010048 | tf_op jit(solution)/shard_map/attend_back/pallas_call | solution.py:322
  279.3 17.3 %project_back.1 = (bf16[2048,768]{1,0:T(8,128)(2,1)}, f32[8,768]{1,0:T(8,128)}) custom-call(s32[71]{0:T(128)} %pad_add_fusion.tab, f32[8,768]{1,0:T(8,128)} %add.347.nrm_ref, bf16[2048,768]{1,0:T(8,128)(2,1)} %get-tuple-element.46.dq_ref, bf16[2048,768]{1,0:T(8,128)(2,1)} %get-tuple-element.47.dk_ref, bf16[2048,768]{1,0:T(8,128)(2,1)} %get-tuple-element.48.dv_ref, ...), custom_call_target="tpu_custom_call" | custom-call | flops 7247757312 | bytes 25559040 | tf_op jit(solution)/shard_map/project_back/pallas_call | solution.py:569
  297.1 2.5 multiply_add_fusion.1
  301.9 13.6 %project_grad.1 = (bf16[4,288,768]{2,1,0:T(8,128)(2,1)}, bf16[4,288,768]{2,1,0:T(8,128)(2,1)}) custom-call(s32[71]{0:T(128)} %pad_add_fusion.tab, bf16[2048,768]{1,0:T(8,128)(2,1)} %get-tuple-element.46.dq_ref, bf16[2048,768]{1,0:T(8,128)(2,1)} %get-tuple-element.47.dk_ref, bf16[2048,768]{1,0:T(8,128)(2,1)} %get-tuple-element.48.dv_ref, ...), custom_call_target="tpu_custom_call" | custom-call | flops 7247757312 | bytes 16121856 | tf_op jit(solution)/shard_map/project_grad/pallas_call | solution.py:522
  326.6 2.8 collective-permute-done.60
  334.9 2.8 collective-permute-start.43
  339.5 2.5 collective-permute-start.62
  346.1 6.6 %collective-permute-done.52 = bf16[2,144,768]{2,1,0:T(8,128)(2,1)S(1)} collective-permute-done((bf16[2,144,768]{2,1,0:T(8,128)(2,1)S(1)}, bf16[2,144,768]{2,1,0:T(8,128)(2,1)S(1)}, u32[]{:S(2)}, u32[]{:S(2)}) %collective-permute-start.52) | collective-permute-done | bytes 442400 | tf_op jit(solution)/shard_map/sum_gradients/ppermute | solution.py:344
  359.8 2.7 collective-permute-done.51
  366.9 8.2 %collective-permute-done.76 = bf16[2,48,3072]{2,1,0:T(8,128)(2,1)S(1)} collective-permute-done((bf16[2,48,3072]{2,1,0:T(8,128)(2,1)S(1)}, bf16[2,48,3072]{2,1,0:T(8,128)(2,1)S(1)}, u32[]{:S(2)}, u32[]{:S(2)}) %collective-permute-start.76) | collective-permute-done | bytes 589856 | tf_op jit(solution)/shard_map/sum_gradients/ppermute | solution.py:344
  379.0 8.7 %collective-permute-done.68 = bf16[2,384,384]{2,1,0:T(8,128)(2,1)S(1)} collective-permute-done((bf16[2,384,384]{2,1,0:T(8,128)(2,1)S(1)}, bf16[2,384,384]{2,1,0:T(8,128)(2,1)S(1)}, u32[]{:S(2)}, u32[]{:S(2)}) %collective-permute-start.68) | collective-permute-done | bytes 589856 | tf_op jit(solution)/shard_map/sum_gradients/ppermute | solution.py:344
  391.4 2.3 collective-permute-done.75
  396.9 2.8 collective-permute-done.54
  401.0 7.4 %collective-permute-start.70 = (bf16[768,384]{1,0:T(8,128)(2,1)S(1)}, bf16[768,384]{1,0:T(8,128)(2,1)S(1)}, u32[]{:S(2)}, u32[]{:S(2)}) collective-permute-start(bf16[768,384]{1,0:T(8,128)(2,1)S(1)} %pad_maximum_fusion.2), channel_id=1, source_target_pairs={{0,1},{3,2},{4,5},{7,6},{8,9},{11,10},{12,13},{15,14},{16,17},{19,... | collective-permute-start | bytes 1769480 | tf_op jit(solution)/shard_map/sum_gradients/ppermute | solution.py:392
  408.4 4.0 collective-permute-done.78
  416.0 3.9 collective-permute-done.70
  423.9 8.3 %collective-permute-done.56 = bf16[288,768]{1,0:T(8,128)(2,1)S(1)} collective-permute-done((bf16[288,768]{1,0:T(8,128)(2,1)S(1)}, bf16[288,768]{1,0:T(8,128)(2,1)S(1)}, u32[]{:S(2)}, u32[]{:S(2)}) %collective-permute-start.56) | collective-permute-done | bytes 442400 | tf_op jit(solution)/shard_map/sum_gradients/ppermute | solution.py:394
  434.6 8.9 %collective-permute-done.80 = bf16[96,3072]{1,0:T(8,128)(2,1)S(1)} collective-permute-done((bf16[96,3072]{1,0:T(8,128)(2,1)S(1)}, bf16[96,3072]{1,0:T(8,128)(2,1)S(1)}, u32[]{:S(2)}, u32[]{:S(2)}) %collective-permute-start.80) | collective-permute-done | bytes 589856 | tf_op jit(solution)/shard_map/sum_gradients/ppermute | solution.py:394
  444.7 8.5 %collective-permute-done.72 = bf16[768,384]{1,0:T(8,128)(2,1)S(1)} collective-permute-done((bf16[768,384]{1,0:T(8,128)(2,1)S(1)}, bf16[768,384]{1,0:T(8,128)(2,1)S(1)}, u32[]{:S(2)}, u32[]{:S(2)}) %collective-permute-start.72) | collective-permute-done | bytes 589856 | tf_op jit(solution)/shard_map/sum_gradients/ppermute | solution.py:394
  (292 shorter events, 99.3 us)
Async XLA Ops:
  29.3 20.8 %collective-permute-start.21 = (bf16[384,768]{1,0:T(8,128)(2,1)S(1)}, bf16[384,768]{1,0:T(8,128)(2,1)S(1)}, u32[]{:S(2)}, u32[]{:S(2)}) collective-permute-start(bf16[384,768]{1,0:T(8,128)(2,1)S(1)} %bitcast.70), channel_id=1, source_target_pairs={{0,8},{4,12},{8,0},{12,4},{16,24},{20,28},{24,16},{28,20},{1,9},{5... | collective-permute-start | bytes 1769480 | tf_op jit(solution)/shard_map/gather_weights/ppermute | solution.py:344
  36.0 16.3 %collective-permute-start.22 = (bf16[384,768]{1,0:T(8,128)(2,1)S(1)}, bf16[384,768]{1,0:T(8,128)(2,1)S(1)}, u32[]{:S(2)}, u32[]{:S(2)}) collective-permute-start(bf16[384,768]{1,0:T(8,128)(2,1)S(1)} %bitcast.71), channel_id=1, source_target_pairs={{0,16},{4,20},{8,24},{12,28},{16,0},{20,4},{24,8},{28,12},{1,17},{... | collective-permute-start | bytes 1769480 | tf_op jit(solution)/shard_map/gather_weights/ppermute | solution.py:344
  37.6 23.8 %collective-permute-start.30 = (bf16[96,3072]{1,0:T(8,128)(2,1)}, bf16[96,3072]{1,0:T(8,128)(2,1)S(1)}, u32[]{:S(2)}, u32[]{:S(2)}) collective-permute-start(bf16[96,3072]{1,0:T(8,128)(2,1)} %bitcast.6.rest_20_), channel_id=1, source_target_pairs={{0,8},{4,12},{8,0},{12,4},{16,24},{20,28},{24,16},{28,20},{1,9},{5... | collective-permute-start | bytes 1769480 | tf_op jit(solution)/shard_map/gather_weights/ppermute | solution.py:344
  39.2 26.0 %collective-permute-start.31 = (bf16[96,3072]{1,0:T(8,128)(2,1)}, bf16[96,3072]{1,0:T(8,128)(2,1)S(1)}, u32[]{:S(2)}, u32[]{:S(2)}) collective-permute-start(bf16[96,3072]{1,0:T(8,128)(2,1)} %bitcast.6.rest_20_), channel_id=1, source_target_pairs={{0,16},{4,20},{8,24},{12,28},{16,0},{20,4},{24,8},{28,12},{1,17},{... | collective-permute-start | bytes 1769480 | tf_op jit(solution)/shard_map/gather_weights/ppermute | solution.py:344
  42.6 26.0 %collective-permute-start.25 = (bf16[384,768]{1,0:T(8,128)(2,1)S(1)}, bf16[384,768]{1,0:T(8,128)(2,1)}, u32[]{:S(2)}, u32[]{:S(2)}) collective-permute-start(bf16[384,768]{1,0:T(8,128)(2,1)S(1)} %bitcast.72), channel_id=1, source_target_pairs={{0,4},{4,0},{8,12},{12,8},{16,20},{20,16},{24,28},{28,24},{1,5},{5... | collective-permute-start | bytes 1769480 | tf_op jit(solution)/shard_map/gather_weights/ppermute | solution.py:344
  68.5 25.1 %collective-permute-start.34 = (bf16[96,3072]{1,0:T(8,128)(2,1)}, bf16[96,3072]{1,0:T(8,128)(2,1)}, u32[]{:S(2)}, u32[]{:S(2)}) collective-permute-start(bf16[96,3072]{1,0:T(8,128)(2,1)} %bitcast.6.rest_20_), channel_id=1, source_target_pairs={{0,4},{4,0},{8,12},{12,8},{16,20},{20,16},{24,28},{28,24},{1,5},{5... | collective-permute-start | bytes 1769480 | tf_op jit(solution)/shard_map/gather_weights/ppermute | solution.py:344
  68.6 25.6 %collective-permute-start.33 = (bf16[48,3072]{1,0:T(8,128)(2,1)S(1)}, bf16[48,3072]{1,0:T(8,128)(2,1)}, u32[]{:S(2)}, u32[]{:S(2)}) collective-permute-start(bf16[48,3072]{1,0:T(8,128)(2,1)S(1)} %slice.367), channel_id=1, source_target_pairs={{0,8},{4,12},{8,0},{12,4},{16,24},{20,28},{24,16},{28,20},{1,9},{5... | collective-permute-start | bytes 884744 | tf_op jit(solution)/shard_map/gather_weights/ppermute | solution.py:344
  73.3 21.0 %collective-permute-start.28 = (bf16[192,768]{1,0:T(8,128)(2,1)}, bf16[192,768]{1,0:T(8,128)(2,1)}, u32[]{:S(2)}, u32[]{:S(2)}) collective-permute-start(bf16[192,768]{1,0:T(8,128)(2,1)} %collective-permute-done.23.rest_13_), channel_id=1, source_target_pairs={{0,4},{4,0},{8,12},{12,8},{16,20},{20,16},{24,28},{28,24},{1,5},{5... | collective-permute-start | bytes 884744 | tf_op jit(solution)/shard_map/gather_weights/ppermute | solution.py:344
  74.9 19.9 %collective-permute-start.29 = (bf16[192,768]{1,0:T(8,128)(2,1)}, bf16[192,768]{1,0:T(8,128)(2,1)}, u32[]{:S(2)}, u32[]{:S(2)}) collective-permute-start(bf16[192,768]{1,0:T(8,128)(2,1)} %collective-permute-done.24.rest_14_), channel_id=1, source_target_pairs={{0,4},{4,0},{8,12},{12,8},{16,20},{20,16},{24,28},{28,24},{1,5},{5... | collective-permute-start | bytes 884744 | tf_op jit(solution)/shard_map/gather_weights/ppermute | solution.py:344
  78.6 16.2 %collective-permute-start.37 = (bf16[48,3072]{1,0:T(8,128)(2,1)}, bf16[48,3072]{1,0:T(8,128)(2,1)}, u32[]{:S(2)}, u32[]{:S(2)}) collective-permute-start(bf16[48,3072]{1,0:T(8,128)(2,1)} %collective-permute-done.32.rest_23_), channel_id=1, source_target_pairs={{0,4},{4,0},{8,12},{12,8},{16,20},{20,16},{24,28},{28,24},{1,5},{5... | collective-permute-start | bytes 884744 | tf_op jit(solution)/shard_map/gather_weights/ppermute | solution.py:344
  93.7 29.1 %collective-permute-start.26 = (bf16[384,768]{1,0:T(8,128)(2,1)S(1)}, bf16[384,768]{1,0:T(8,128)(2,1)}, u32[]{:S(2)}, u32[]{:S(2)}) collective-permute-start(bf16[384,768]{1,0:T(8,128)(2,1)S(1)} %collective-permute-done.21.rest_11_), channel_id=1, source_target_pairs={{0,4},{4,0},{8,12},{12,8},{16,20},{20,16},{24,28},{28,24},{1,5},{5... | collective-permute-start | bytes 1769480 | tf_op jit(solution)/shard_map/gather_weights/ppermute | solution.py:344
  94.2 28.5 %collective-permute-start.27 = (bf16[384,768]{1,0:T(8,128)(2,1)}, bf16[384,768]{1,0:T(8,128)(2,1)}, u32[]{:S(2)}, u32[]{:S(2)}) collective-permute-start(bf16[384,768]{1,0:T(8,128)(2,1)} %copy-done.11), channel_id=1, source_target_pairs={{0,4},{4,0},{8,12},{12,8},{16,20},{20,16},{24,28},{28,24},{1,5},{5... | collective-permute-start | bytes 1769480 | tf_op jit(solution)/shard_map/gather_weights/ppermute | solution.py:344
  94.3 28.4 %collective-permute-start.35 = (bf16[96,3072]{1,0:T(8,128)(2,1)}, bf16[96,3072]{1,0:T(8,128)(2,1)}, u32[]{:S(2)}, u32[]{:S(2)}) collective-permute-start(bf16[96,3072]{1,0:T(8,128)(2,1)} %copy-done.12), channel_id=1, source_target_pairs={{0,4},{4,0},{8,12},{12,8},{16,20},{20,16},{24,28},{28,24},{1,5},{5... | collective-permute-start | bytes 1769480 | tf_op jit(solution)/shard_map/gather_weights/ppermute | solution.py:344
  94.7 28.0 %collective-permute-start.36 = (bf16[96,3072]{1,0:T(8,128)(2,1)}, bf16[96,3072]{1,0:T(8,128)(2,1)}, u32[]{:S(2)}, u32[]{:S(2)}) collective-permute-start(bf16[96,3072]{1,0:T(8,128)(2,1)} %copy-done.13), channel_id=1, source_target_pairs={{0,4},{4,0},{8,12},{12,8},{16,20},{20,16},{24,28},{28,24},{1,5},{5... | collective-permute-start | bytes 1769480 | tf_op jit(solution)/shard_map/gather_weights/ppermute | solution.py:344
  94.8 27.9 %collective-permute-start.38 = (bf16[48,3072]{1,0:T(8,128)(2,1)}, bf16[48,3072]{1,0:T(8,128)(2,1)S(1)}, u32[]{:S(2)}, u32[]{:S(2)}) collective-permute-start(bf16[48,3072]{1,0:T(8,128)(2,1)} %collective-permute-done.33.rest_24_), channel_id=1, source_target_pairs={{0,4},{4,0},{8,12},{12,8},{16,20},{20,16},{24,28},{28,24},{1,5},{5... | collective-permute-start | bytes 884744 | tf_op jit(solution)/shard_map/gather_weights/ppermute | solution.py:344
  254.0 45.7 %collective-permute-start.44 = (f32[8,768]{1,0:T(8,128)S(1)}, f32[8,768]{1,0:T(8,128)S(1)}, u32[]{:S(2)}, u32[]{:S(2)}) collective-permute-start(f32[8,768]{1,0:T(8,128)S(1)} %copy-done.22), channel_id=1, source_target_pairs={{0,4},{4,0},{8,12},{12,8},{16,20},{20,16},{24,28},{28,24},{1,5},{5... | collective-permute-start | bytes 73736 | tf_op jit(solution)/shard_map/sum_gradients/ppermute | solution.py:344
  299.5 22.9 %collective-permute-start.57 = (bf16[4,96,768]{2,1,0:T(8,128)(2,1)}, bf16[4,96,768]{2,1,0:T(8,128)(2,1)}, u32[]{:S(2)}, u32[]{:S(2)}) collective-permute-start(bf16[4,96,768]{2,1,0:T(8,128)(2,1)} %get-tuple-element.57), channel_id=1, source_target_pairs={{0,4},{4,0},{8,12},{12,8},{16,20},{20,16},{24,28},{28,24},{1,5},{5... | collective-permute-start | bytes 1769480 | tf_op jit(solution)/shard_map/sum_gradients/ppermute | solution.py:344
  315.5 26.5 %collective-permute-start.49 = (bf16[4,288,768]{2,1,0:T(8,128)(2,1)}, bf16[4,288,768]{2,1,0:T(8,128)(2,1)}, u32[]{:S(2)}, u32[]{:S(2)}) collective-permute-start(bf16[4,288,768]{2,1,0:T(8,128)(2,1)} %get-tuple-element.55), channel_id=1, source_target_pairs={{0,4},{4,0},{8,12},{12,8},{16,20},{20,16},{24,28},{28,24},{1,5},{5... | collective-permute-start | bytes 5308424 | tf_op jit(solution)/shard_map/sum_gradients/ppermute | solution.py:344
  319.7 37.6 %collective-permute-start.73 = (bf16[4,96,3072]{2,1,0:T(8,128)(2,1)}, bf16[4,96,3072]{2,1,0:T(8,128)(2,1)S(1)}, u32[]{:S(2)}, u32[]{:S(2)}) collective-permute-start(bf16[4,96,3072]{2,1,0:T(8,128)(2,1)} %get-tuple-element.61), channel_id=1, source_target_pairs={{0,4},{4,0},{8,12},{12,8},{16,20},{20,16},{24,28},{28,24},{1,5},{5... | collective-permute-start | bytes 7077896 | tf_op jit(solution)/shard_map/sum_gradients/ppermute | solution.py:344
  325.8 32.5 %collective-permute-start.65 = (bf16[4,768,384]{2,1,0:T(8,128)(2,1)}, bf16[4,768,384]{2,1,0:T(8,128)(2,1)S(1)}, u32[]{:S(2)}, u32[]{:S(2)}) collective-permute-start(bf16[4,768,384]{2,1,0:T(8,128)(2,1)} %get-tuple-element.59), channel_id=1, source_target_pairs={{0,4},{4,0},{8,12},{12,8},{16,20},{20,16},{24,28},{28,24},{1,5},{5... | collective-permute-start | bytes 7077896 | tf_op jit(solution)/shard_map/sum_gradients/ppermute | solution.py:344
  345.4 67.8 %collective-permute-start.63 = (bf16[96,768]{1,0:T(8,128)(2,1)S(1)}, bf16[96,768]{1,0:T(8,128)(2,1)S(1)}, u32[]{:S(2)}, u32[]{:S(2)}) collective-permute-start(bf16[96,768]{1,0:T(8,128)(2,1)S(1)} %add_convert_fusion.43), channel_id=1, source_target_pairs={{1,2},{2,1},{5,6},{6,5},{9,10},{10,9},{13,14},{14,13},{17,18},{18,... | collective-permute-start | bytes 442376 | tf_op jit(solution)/shard_map/sum_gradients/ppermute | solution.py:393
  357.7 17.4 %collective-permute-start.76 = (bf16[2,48,3072]{2,1,0:T(8,128)(2,1)S(1)}, bf16[2,48,3072]{2,1,0:T(8,128)(2,1)S(1)}, u32[]{:S(2)}, u32[]{:S(2)}) collective-permute-start(bf16[2,48,3072]{2,1,0:T(8,128)(2,1)S(1)} %pad_maximum_fusion.4), channel_id=1, source_target_pairs={{0,16},{4,20},{8,24},{12,28},{16,0},{20,4},{24,8},{28,12},{1,17},{... | collective-permute-start | bytes 1769480 | tf_op jit(solution)/shard_map/sum_gradients/ppermute | solution.py:344
  358.3 18.6 %collective-permute-start.74 = (bf16[2,48,3072]{2,1,0:T(8,128)(2,1)S(1)}, bf16[2,48,3072]{2,1,0:T(8,128)(2,1)S(1)}, u32[]{:S(2)}, u32[]{:S(2)}) collective-permute-start(bf16[2,48,3072]{2,1,0:T(8,128)(2,1)S(1)} %pad_maximum_fusion.3), channel_id=1, source_target_pairs={{0,8},{4,12},{8,0},{12,4},{16,24},{20,28},{24,16},{28,20},{1,9},{5... | collective-permute-start | bytes 1769480 | tf_op jit(solution)/shard_map/sum_gradients/ppermute | solution.py:344
  362.5 25.3 %collective-permute-start.68 = (bf16[2,384,384]{2,1,0:T(8,128)(2,1)S(1)}, bf16[2,384,384]{2,1,0:T(8,128)(2,1)S(1)}, u32[]{:S(2)}, u32[]{:S(2)}) collective-permute-start(bf16[2,384,384]{2,1,0:T(8,128)(2,1)S(1)} %pad_maximum_fusion.1), channel_id=1, source_target_pairs={{0,16},{4,20},{8,24},{12,28},{16,0},{20,4},{24,8},{28,12},{1,17},{... | collective-permute-start | bytes 1769480 | tf_op jit(solution)/shard_map/sum_gradients/ppermute | solution.py:344
  364.3 25.1 %collective-permute-start.66 = (bf16[2,384,384]{2,1,0:T(8,128)(2,1)S(1)}, bf16[2,384,384]{2,1,0:T(8,128)(2,1)S(1)}, u32[]{:S(2)}, u32[]{:S(2)}) collective-permute-start(bf16[2,384,384]{2,1,0:T(8,128)(2,1)S(1)} %pad_maximum_fusion), channel_id=1, source_target_pairs={{0,8},{4,12},{8,0},{12,4},{16,24},{20,28},{24,16},{28,20},{1,9},{5... | collective-permute-start | bytes 1769480 | tf_op jit(solution)/shard_map/sum_gradients/ppermute | solution.py:344
  377.1 16.7 %collective-permute-start.75 = (bf16[48,3072]{1,0:T(8,128)(2,1)S(1)}, bf16[48,3072]{1,0:T(8,128)(2,1)S(1)}, u32[]{:S(2)}, u32[]{:S(2)}) collective-permute-start(bf16[48,3072]{1,0:T(8,128)(2,1)S(1)} %get-tuple-element.66), channel_id=1, source_target_pairs={{0,16},{4,20},{8,24},{12,28},{16,0},{20,4},{24,8},{28,12},{1,17},{... | collective-permute-start | bytes 884744 | tf_op jit(solution)/shard_map/sum_gradients/ppermute | solution.py:344
  377.4 17.2 %collective-permute-start.77 = (bf16[48,3072]{1,0:T(8,128)(2,1)S(1)}, bf16[48,3072]{1,0:T(8,128)(2,1)S(1)}, u32[]{:S(2)}, u32[]{:S(2)}) collective-permute-start(bf16[48,3072]{1,0:T(8,128)(2,1)S(1)} %get-tuple-element.67), channel_id=1, source_target_pairs={{0,8},{4,12},{8,0},{12,4},{16,24},{20,28},{24,16},{28,20},{1,9},{5... | collective-permute-start | bytes 884744 | tf_op jit(solution)/shard_map/sum_gradients/ppermute | solution.py:344
  395.0 17.4 %collective-permute-start.78 = (bf16[96,3072]{1,0:T(8,128)(2,1)S(1)}, bf16[96,3072]{1,0:T(8,128)(2,1)S(1)}, u32[]{:S(2)}, u32[]{:S(2)}) collective-permute-start(bf16[96,3072]{1,0:T(8,128)(2,1)S(1)} %pad_maximum_fusion.5), channel_id=1, source_target_pairs={{0,1},{3,2},{4,5},{7,6},{8,9},{11,10},{12,13},{15,14},{16,17},{19,... | collective-permute-start | bytes 1769480 | tf_op jit(solution)/shard_map/sum_gradients/ppermute | solution.py:392
  401.0 19.0 %collective-permute-start.70 = (bf16[768,384]{1,0:T(8,128)(2,1)S(1)}, bf16[768,384]{1,0:T(8,128)(2,1)S(1)}, u32[]{:S(2)}, u32[]{:S(2)}) collective-permute-start(bf16[768,384]{1,0:T(8,128)(2,1)S(1)} %pad_maximum_fusion.2), channel_id=1, source_target_pairs={{0,1},{3,2},{4,5},{7,6},{8,9},{11,10},{12,13},{15,14},{16,17},{19,... | collective-permute-start | bytes 1769480 | tf_op jit(solution)/shard_map/sum_gradients/ppermute | solution.py:392
  414.7 17.5 %collective-permute-start.56 = (bf16[288,768]{1,0:T(8,128)(2,1)S(1)}, bf16[288,768]{1,0:T(8,128)(2,1)S(1)}, u32[]{:S(2)}, u32[]{:S(2)}) collective-permute-start(bf16[288,768]{1,0:T(8,128)(2,1)S(1)} %add_convert_fusion.4), channel_id=1, source_target_pairs={{1,0},{2,3},{5,4},{6,7},{9,8},{10,11},{13,12},{14,15},{17,16},{18,... | collective-permute-start | bytes 1327112 | tf_op jit(solution)/shard_map/sum_gradients/ppermute | solution.py:394
  421.0 22.6 %collective-permute-start.80 = (bf16[96,3072]{1,0:T(8,128)(2,1)S(1)}, bf16[96,3072]{1,0:T(8,128)(2,1)S(1)}, u32[]{:S(2)}, u32[]{:S(2)}) collective-permute-start(bf16[96,3072]{1,0:T(8,128)(2,1)S(1)} %add_convert_fusion), channel_id=1, source_target_pairs={{1,0},{2,3},{5,4},{6,7},{9,8},{10,11},{13,12},{14,15},{17,16},{18,... | collective-permute-start | bytes 1769480 | tf_op jit(solution)/shard_map/sum_gradients/ppermute | solution.py:394
  433.3 19.9 %collective-permute-start.72 = (bf16[768,384]{1,0:T(8,128)(2,1)S(1)}, bf16[768,384]{1,0:T(8,128)(2,1)S(1)}, u32[]{:S(2)}, u32[]{:S(2)}) collective-permute-start(bf16[768,384]{1,0:T(8,128)(2,1)S(1)} %add_convert_fusion.2), channel_id=1, source_target_pairs={{1,0},{2,3},{5,4},{6,7},{9,8},{10,11},{13,12},{14,15},{17,16},{18,... | collective-permute-start | bytes 1769480 | tf_op jit(solution)/shard_map/sum_gradients/ppermute | solution.py:394
  (85 other events, 898.5 us)

commit v2 on v1

v2 whole, which is shorter than its diff:
```python
import math
from functools import partial

import jax
import jax.numpy as jnp
from jax import lax
from jax.experimental import pallas as pl
from jax.experimental.pallas import tpu as pltpu
from jax.sharding import PartitionSpec as P

HEAD = 64
ROW_LEN = 1024
layer_eps = 1e-06
ema_rate = 0.75

BF = jnp.bfloat16
F32 = jnp.float32
NN = (((1,), (0,)), ((), ()))
NT = (((1,), (1,)), ((), ()))
TN = (((0,), (0,)), ((), ()))
VMEM_LIMIT = 66_000_000
GRANT = 32_000_000
COST_SCALE = 0.02

QW = 256
KW = 224
FIT = KW - 15
SMALL = 128
FIT_SMALL = SMALL - 15
KB = 128
STRIDE = 35


def mm(left, right, dims):
    return lax.dot_general(left, right, dims, preferred_element_type=F32)


def cost(flops, moved):
    return pl.CostEstimate(flops=int(flops * COST_SCALE), bytes_accessed=int(moved * COST_SCALE), transcendentals=0)


def job_table(segment_ids, rows, device):
    seg = segment_ids.reshape(rows, 1, ROW_LEN)
    ident = jnp.arange(16, dtype=jnp.int32)[None, :, None]
    real = seg >= 0
    starts = jnp.sum((real & (seg < ident)).astype(jnp.int32), axis=2)
    after = jnp.sum((real & (seg < ident + 1)).astype(jnp.int32), axis=2)
    images = jnp.max(seg, axis=2) + 1
    ends = jnp.where(jnp.arange(16, dtype=jnp.int32)[None, :] < images, after, ROW_LEN)
    valid = jnp.sum(real.astype(jnp.int32), axis=2)
    pad = ROW_LEN - valid
    fits = pad <= FIT
    jobs = images + jnp.where((pad > 0) & fits, 1, 0)
    wide = jnp.where(fits, 0, (pad + 15 + QW - 1) // QW)
    table = jnp.concatenate([starts, ends, jobs, valid, wide], axis=1).reshape(-1)
    return jnp.concatenate([table, device.astype(jnp.int32).reshape(1)])


def lane_of(count):
    return lax.broadcasted_iota(jnp.int32, (count, 128), 1)


def slot_of(count, base):
    return lax.broadcasted_iota(jnp.int32, (count, 128), 0) + base


def half_lanes(count, par):
    return (lane_of(count) < 64) if par == 0 else (lane_of(count) >= 64)


def spare_lane(count, par):
    return lane_of(count) == (64 if par == 0 else 0)


def query_side(q, par):
    n = q.shape[0]
    return jnp.where(half_lanes(n, par), q * BF(0.125), jnp.where(spare_lane(n, par), BF(1), BF(0)))


def key_side(k, par, inside):
    n = k.shape[0]
    return jnp.where(half_lanes(n, par), k, jnp.where(spare_lane(n, par) & (~inside), BF(-1e30), BF(0)))


def one_head(x, par):
    return jnp.where(half_lanes(x.shape[0], par), x, BF(0))


def each_image(tab, base, work):
    def job(j, carry):
        begin = tab[base + j]
        end = tab[base + 16 + j]
        low = lax.div(begin, 16) * 16
        small = end - begin <= FIT_SMALL
        for fits, nq, nk in ((small, SMALL, SMALL), (~small, QW, KW)):

            @pl.when(fits)
            def _():
                q0 = pl.multiple_of(jnp.minimum(low, ROW_LEN - nq), 16)
                k0 = pl.multiple_of(jnp.minimum(low, ROW_LEN - nk), 16)
                kr = slot_of(nk, k0)
                qr = slot_of(nq, q0)
                work(pl.ds(q0, nq), pl.ds(k0, nk), (qr >= begin) & (qr < end), (kr >= begin) & (kr < end))

        return carry

    lax.fori_loop(0, tab[base + 32], job, 0)


def attend_kernel(pairs, row0, tab, q_ref, k_ref, v_ref, *rest):
    o_ref, a_sc = rest[-2:]
    base = (pl.program_id(0) + row0) * STRIDE
    o_ref[...] = jnp.zeros_like(o_ref)

    def work(qs, ks, qin, inside):
        scores = []
        for p in range(pairs):
            cs = pl.ds(128 * p, 128)
            q = q_ref[qs, cs]
            k = k_ref[ks, cs]
            for par in range(2):
                scores.append(mm(key_side(k, par, inside), query_side(q, par), NT))
        probs = []
        for st in scores:
            expo = jnp.exp(st - jnp.max(st, axis=0, keepdims=True))
            total = jnp.sum(expo, axis=0, keepdims=True)
            probs.append((expo * (1.0 / total)).astype(BF))
        for p in range(pairs):
            cs = pl.ds(128 * p, 128)
            v = v_ref[ks, cs]
            o = jnp.concatenate(
                [mm(v[:, 64 * par : 64 * par + 64], probs[2 * p + par], TN) for par in range(2)], axis=0
            ).T
            o_ref[qs, cs] = jnp.where(qin, o.astype(BF), o_ref[qs, cs])

    each_image(tab, base, work)

    start = tab[base + 33]
    low = lax.div(start, 16) * 16

    def wide(i, carry):
        q0 = pl.multiple_of(jnp.minimum(low + i * QW, ROW_LEN - QW), 16)
        qin = slot_of(QW, q0) >= start
        for p in range(pairs):
            cs = pl.ds(128 * p, 128)
            q = q_ref[pl.ds(q0, QW), cs]
            for par in range(2):
                qs = query_side(q, par)

                def block(kb):
                    k0 = pl.multiple_of(kb * KB, KB)
                    k = k_ref[pl.ds(k0, KB), cs]
                    return k0, mm(key_side(k, par, slot_of(KB, k0) >= start), qs, NT)

                def take_max(kb, top):
                    return jnp.maximum(top, jnp.max(block(kb)[1], axis=0, keepdims=True))

                top = lax.fori_loop(0, ROW_LEN // KB, take_max, jnp.full((1, QW), -1e30, F32))

                def take_sum(kb, total):
                    return total + jnp.sum(jnp.exp(block(kb)[1] - top), axis=0, keepdims=True)

                total = lax.fori_loop(0, ROW_LEN // KB, take_sum, jnp.zeros((1, QW), F32))
                a_sc[...] = jnp.zeros_like(a_sc)

                def take_out(kb, c):
                    k0, st = block(kb)
                    prob = (jnp.exp(st - top) * (1.0 / total)).astype(BF)
                    a_sc[...] += mm(one_head(v_ref[pl.ds(k0, KB), cs], par), prob, TN)
                    return c

                lax.fori_loop(0, ROW_LEN // KB, take_out, 0)
                hit = qin & half_lanes(QW, par)
                o_ref[pl.ds(q0, QW), cs] = jnp.where(hit, a_sc[...].T.astype(BF), o_ref[pl.ds(q0, QW), cs])
        return carry

    lax.fori_loop(0, tab[base + 34], wide, 0)


def attend_back_kernel(pairs, row0, tab, q_ref, k_ref, v_ref, d_ref, *rest):
    dq_ref, dk_ref, dv_ref, a_sc, dk_sc, dv_sc = rest[-6:]
    base = (pl.program_id(0) + row0) * STRIDE
    dq_ref[...] = jnp.zeros_like(dq_ref)
    dk_ref[...] = jnp.zeros_like(dk_ref)
    dv_ref[...] = jnp.zeros_like(dv_ref)

    def work(qs, ks, qin, inside):
        scores = []
        grads = []
        for p in range(pairs):
            cs = pl.ds(128 * p, 128)
            q = q_ref[qs, cs]
            k = k_ref[ks, cs]
            v = v_ref[ks, cs]
            d = jnp.where(qin, d_ref[qs, cs], BF(0))
            for par in range(2):
                scores.append(mm(key_side(k, par, inside), query_side(q, par), NT))
                grads.append(mm(v, one_head(d, par), NT))
        probs = []
        dscores = []
        for st, dp in zip(scores, grads):
            expo = jnp.exp(st - jnp.max(st, axis=0, keepdims=True))
            total = jnp.sum(expo, axis=0, keepdims=True)
            prob = expo * (1.0 / total)
            center = jnp.sum(prob * dp, axis=0, keepdims=True)
            dscores.append((prob * (dp - center)).astype(BF))
            probs.append(prob.astype(BF))
        for p in range(pairs):
            cs = pl.ds(128 * p, 128)
            q = q_ref[qs, cs]
            k = k_ref[ks, cs]
            d = jnp.where(qin, d_ref[qs, cs], BF(0))
            dv = mm(probs[2 * p], one_head(d, 0), NN) + mm(probs[2 * p + 1], one_head(d, 1), NN)
            dk = mm(dscores[2 * p], one_head(q, 0), NN) + mm(dscores[2 * p + 1], one_head(q, 1), NN)
            dq = jnp.concatenate(
                [mm(k[:, 64 * par : 64 * par + 64], dscores[2 * p + par], TN) for par in range(2)], axis=0
            ).T
            dq_ref[qs, cs] = jnp.where(qin, (dq * 0.125).astype(BF), dq_ref[qs, cs])
            dk_ref[ks, cs] = jnp.where(inside, (dk * 0.125).astype(BF), dk_ref[ks, cs])
            dv_ref[ks, cs] = jnp.where(inside, dv.astype(BF), dv_ref[ks, cs])

    each_image(tab, base, work)

    start = tab[base + 33]
    low = lax.div(start, 16) * 16
    windows = tab[base + 34]
    for p in range(pairs):
        cs = pl.ds(128 * p, 128)

        @pl.when(windows > 0)
        def _():
            dk_sc[...] = jnp.zeros_like(dk_sc)
            dv_sc[...] = jnp.zeros_like(dv_sc)

        def wide(i, carry):
            first = jnp.maximum(start, low + i * QW)
            q0 = pl.multiple_of(jnp.minimum(low + i * QW, ROW_LEN - QW), 16)
            qin = slot_of(QW, q0) >= first
            q = q_ref[pl.ds(q0, QW), cs]
            d = jnp.where(qin, d_ref[pl.ds(q0, QW), cs], BF(0))
            for par in range(2):
                qh = query_side(q, par)
                dh = one_head(d, par)
                qo = one_head(q, par)

                def block(kb):
                    k0 = pl.multiple_of(kb * KB, KB)
                    k = k_ref[pl.ds(k0, KB), cs]
                    v = v_ref[pl.ds(k0, KB), cs]
                    return k0, k, mm(key_side(k, par, slot_of(KB, k0) >= start), qh, NT), mm(v, dh, NT)

                def take_max(kb, top):
                    return jnp.maximum(top, jnp.max(block(kb)[2], axis=0, keepdims=True))

                top = lax.fori_loop(0, ROW_LEN // KB, take_max, jnp.full((1, QW), -1e30, F32))

                def take_sums(kb, sums):
                    _, _, st, dp = block(kb)
                    expo = jnp.exp(st - top)
                    return (
                        sums[0] + jnp.sum(expo, axis=0, keepdims=True),
                        sums[1] + jnp.sum(expo * dp, axis=0, keepdims=True),
                    )

                none = jnp.zeros((1, QW), F32)
                total, weighted = lax.fori_loop(0, ROW_LEN // KB, take_sums, (none, none))
                scale = 1.0 / total
                center = weighted * scale
                a_sc[...] = jnp.zeros_like(a_sc)

                def take_grads(kb, c):
                    k0, k, st, dp = block(kb)
                    prob = jnp.exp(st - top) * scale
                    ds = (prob * (dp - center)).astype(BF)
                    a_sc[...] += mm(one_head(k, par), ds, TN)
                    dk_sc[pl.ds(k0, KB), :] += mm(ds, qo, NN)
                    dv_sc[pl.ds(k0, KB), :] += mm(prob.astype(BF), dh, NN)
                    return c

                lax.fori_loop(0, ROW_LEN // KB, take_grads, 0)
                hit = qin & half_lanes(QW, par)
                dq = (a_sc[...].T * 0.125).astype(BF)
                dq_ref[pl.ds(q0, QW), cs] = jnp.where(hit, dq, dq_ref[pl.ds(q0, QW), cs])
            return carry

        lax.fori_loop(0, windows, wide, 0)

        @pl.when(windows > 0)
        def _():
            kin = slot_of(ROW_LEN, 0) >= start
            dk_ref[:, cs] = jnp.where(kin, (dk_sc[...] * 0.125).astype(BF), dk_ref[:, cs])
            dv_ref[:, cs] = jnp.where(kin, dv_sc[...].astype(BF), dv_ref[:, cs])


def row_call(kernel, name, outs, scratch, qkv, extra, table, row, half, halves, before, flops, moved):
    n = qkv.shape[0]
    width = qkv.shape[1] // 3
    w = width // halves
    spec = lambda part: pl.BlockSpec((ROW_LEN, w), lambda r, t: (row, part * halves + half))
    before = [] if before is None else list(before)
    return pl.pallas_call(
        partial(kernel, w // 128, row),
        out_shape=[jax.ShapeDtypeStruct((n, width), BF)] * outs,
        grid_spec=pltpu.PrefetchScalarGridSpec(
            num_scalar_prefetch=1,
            grid=(1,),
            in_specs=[spec(0), spec(1), spec(2)]
            + [spec(0)] * len(extra)
            + [pl.BlockSpec(memory_space=pl.ANY)] * len(before),
            out_specs=[spec(0)] * outs,
            scratch_shapes=scratch,
        ),
        input_output_aliases={4 + len(extra) + i: i for i in range(len(before))},
        compiler_params=pltpu.CompilerParams(vmem_limit_bytes=GRANT),
        cost_estimate=cost(flops / halves, moved * ROW_LEN * w),
        name=name,
    )(table, qkv, qkv, qkv, *extra, *before)


def attention_forward(qkv, table, row, before):
    scratch = [pltpu.VMEM((128, QW), F32)]
    return row_call(attend_kernel, "attend", 1, scratch, qkv, [], table, row, 0, 1, before, 12e9, 8)


def attention_backward(qkv, da, table, row, half, halves, before):
    scratch = [pltpu.VMEM((128, QW), F32), pltpu.VMEM((ROW_LEN, 128), F32), pltpu.VMEM((ROW_LEN, 128), F32)]
    return row_call(attend_back_kernel, "attend_back", 3, scratch, qkv, [da], table, row, half, halves, before, 24e9, 14)


def hop(value, bit, size):
    return lax.ppermute(value, "fsdp", [(i, i ^ bit) for i in range(size)])


def gather_cross(first, second):
    first_x, second_y = hop(first, 2, 8), hop(second, 4, 8)
    first_y, second_x = hop(first, 4, 8), hop(second, 2, 8)
    return (first, first_x, first_y), (second, second_x, second_y)


def forward_cross(firsts, seconds):
    return hop(firsts[1], 4, 8), hop(seconds[2], 2, 8)


def both_cores(arrays):
    own = [(array, 2 * i) for i, array in enumerate(arrays)]
    return own + [(hop(array, 1, 8), slot + 1) for array, slot in own]


def after(value, *others):
    return lax.optimization_barrier((value, *others))[0]


def total(*terms):
    return sum(t.astype(F32) for t in terms).astype(BF)


class Scatter:
    def __init__(self, even, odd):
        self.even = even
        self.core = hop(odd, 1, 8)

    def send(self, done):
        self.core = after(self.core, done)
        self.out = [total(self.even[q], self.core[q]) for q in (1, 2, 3)]
        return self.out

    def block(self, done):
        come = after([hop(block, 2 * q, 8) for q, block in zip((1, 2, 3), self.out)], done)
        return total(self.even[0], self.core[0], *come)


def direct_sum(block, done):
    shift = lambda value, by: lax.ppermute(value, "rep", [(i, (i + by) % 4) for i in range(4)])
    z = lax.axis_index("rep")
    quarters = block.reshape(4, block.shape[0] // 4, block.shape[1])
    pick = lambda by: lax.dynamic_index_in_dim(quarters, lax.rem(z + by, 4), 0, False)
    mine = total(pick(0), *after([shift(pick(by), by) for by in (2, 1, 3)], done))
    parts = [mine] + [shift(mine, by) for by in (1, 2, 3)]
    out = jnp.zeros(quarters.shape, F32)
    for by, part in enumerate(parts):
        out = lax.dynamic_update_index_in_dim(out, part.astype(F32), lax.rem(z - by + 4, 4), 0)
    return out.reshape(block.shape)


class Weight:
    def __init__(self, pieces, per):
        self.arrays = [p[0] for p in pieces]
        self.places = [p[1:] for p in pieces]
        self.per = per

    def copies(self, refs, dst, sems, me):
        out = []
        for i, (ref, (slot, row)) in enumerate(zip(refs, self.places)):
            src, into = ref, dst
            if slot is not None:
                half = self.per // 2
                src = ref.at[pl.ds(0, half), :]
                into = dst.at[pl.ds(pl.multiple_of((me ^ slot) * self.per + row, half), half), :]
            out.append(pltpu.make_async_copy(src, into, sems.at[i]))
        return out


def norm_stats(values):
    center = values - jnp.mean(values, axis=1, keepdims=True)
    rate = lax.rsqrt(jnp.mean(center * center, axis=1, keepdims=True) + layer_eps)
    return center * rate, rate


def norm_back(unit, rate, gain, grad):
    scaled = grad * gain
    mean = jnp.mean(scaled, axis=1, keepdims=True)
    along = jnp.mean(scaled * unit, axis=1, keepdims=True)
    return rate * (scaled - mean - unit * along)


def project_kernel(weight, count, tab, x_ref, *rest):
    w_refs = rest[:count]
    h_ref, qkv_ref, nrm_ref, w_sc, n_sc, sems, n_sems = rest[-7:]
    me = tab[tab.shape[0] - 1]
    half = weight.per // 2

    @pl.when(pl.program_id(0) == 0)
    def _():
        if len(rest) - 7 > count:
            norm_copies = [pltpu.make_async_copy(rest[count], n_sc.at[0], n_sems.at[0])]
        else:
            norm_copies = [
                pltpu.make_async_copy(w_refs[i].at[pl.ds(half, 16), :], n_sc.at[i], n_sems.at[i]) for i in range(8)
            ]
        copies = weight.copies(w_refs, w_sc, sems, me)
        for c in norm_copies + copies:
            c.start()
        for c in norm_copies:
            c.wait()
        placed = sum(n_sc[i].astype(F32) for i in range(len(norm_copies)))
        nrm_ref[...] = placed[:8, :]
        for c in copies:
            c.wait()

    tb, width = x_ref.shape
    parts = [pl.ds(i, tb // 2) for i in range(0, tb, tb // 2)]
    for p in parts:
        unit, _ = norm_stats(x_ref[p, :].astype(F32))
        h_ref[p, :] = (unit * nrm_ref[0:1, :] + nrm_ref[1:2, :]).astype(BF)
    for p in parts:
        qkv_ref[p, :] = mm(h_ref[p, :], w_sc[...], NT).astype(BF)


def project(table, norm_parts, x, weight, tb=512):
    n, width = x.shape
    count = len(weight.arrays)
    anywhere = pl.BlockSpec(memory_space=pl.ANY)
    block = lambda w: pl.BlockSpec((tb, w), lambda t, tab: (t, 0))
    sds = jax.ShapeDtypeStruct
    return pl.pallas_call(
        partial(project_kernel, weight, count),
        out_shape=[sds((n, width), BF), sds((n, 3 * width), BF), sds((8, width), F32)],
        grid_spec=pltpu.PrefetchScalarGridSpec(
            num_scalar_prefetch=1,
            grid=(n // tb,),
            in_specs=[block(width)] + [anywhere] * (count + len(norm_parts)),
            out_specs=[block(width), block(3 * width), pl.BlockSpec((8, width), lambda t, tab: (0, 0))],
            scratch_shapes=[
                pltpu.VMEM((3 * width, width), BF),
                pltpu.VMEM((8, 16, width), BF),
                pltpu.SemaphoreType.DMA((count,)),
                pltpu.SemaphoreType.DMA((8,)),
            ],
        ),
        compiler_params=pltpu.CompilerParams(vmem_limit_bytes=VMEM_LIMIT),
        cost_estimate=cost(6 * n * width * width, n * width * 10 + 6 * width * width),
        name="project",
    )(table, x, *weight.arrays, *norm_parts)


def by_owner(acc, per, even_ref, odd_ref, me):
    for q in range(4):
        for parity, ref in ((0, even_ref), (1, odd_ref)):
            at = pl.multiple_of((me ^ (2 * q + parity)) * per, per)
            ref[q] = acc[pl.ds(at, per), :].astype(BF)


def project_grad_kernel(size, tab, dq_ref, dk_ref, dv_ref, h_ref, *rest):
    out_refs, acc = rest[:-1], rest[-1]
    t = pl.program_id(0)
    width = h_ref.shape[1]

    @pl.when(t == 0)
    def _():
        acc[...] = jnp.zeros_like(acc)

    for part, ref in enumerate((dq_ref, dk_ref, dv_ref)):
        acc[pl.ds(part * width, width), :] += mm(ref[...], h_ref[...], TN)

    @pl.when(t == pl.num_programs(0) - 1)
    def _():
        if size == 8:
            by_owner(acc, acc.shape[0] // 8, *out_refs, tab[tab.shape[0] - 1])
        else:
            out_refs[0][...] = acc[...].astype(BF)


def project_grad(table, dq, dk, dv, h, size, tb=512):
    n, width = h.shape
    rows = 3 * width
    block = pl.BlockSpec((tb, width), lambda t, tab: (t, 0))
    shapes = [(4, rows // 8, width)] * 2 if size == 8 else [(rows, width)]
    return pl.pallas_call(
        partial(project_grad_kernel, size),
        out_shape=[jax.ShapeDtypeStruct(s, BF) for s in shapes],
        grid_spec=pltpu.PrefetchScalarGridSpec(
            num_scalar_prefetch=1,
            grid=(n // tb,),
            in_specs=[block] * 4,
            out_specs=[pl.BlockSpec(s, lambda t, tab, k=len(s): (0,) * k) for s in shapes],
            scratch_shapes=[pltpu.VMEM((rows, width), F32)],
        ),
        compiler_params=pltpu.CompilerParams(vmem_limit_bytes=VMEM_LIMIT),
        cost_estimate=cost(6 * n * width * width, n * width * 8 + 6 * width * width),
        name="project_grad",
    )(table, dq, dk, dv, h)


def project_back_kernel(weight, count, tab, nrm_ref, dq_ref, dk_ref, dv_ref, x_ref, dx_ref, *rest):
    w_refs = rest[:count]
    out_ref, gn_ref, w_sc, sems = rest[-4:]
    t = pl.program_id(0)
    me = tab[tab.shape[0] - 1]
    width = x_ref.shape[1]

    @pl.when(t == 0)
    def _():
        copies = weight.copies(w_refs, w_sc, sems, me)
        for c in copies:
            c.start()
        gn_ref[...] = jnp.zeros_like(gn_ref)
        for c in copies:
            c.wait()

    tb = x_ref.shape[0]
    parts = [pl.ds(i, tb // 2) for i in range(0, tb, tb // 2)]
    units = [norm_stats(x_ref[p, :].astype(F32)) for p in parts]
    dgain = jnp.zeros((1, width), F32)
    dshift = jnp.zeros((1, width), F32)
    for p, (unit, rate) in zip(parts, units):
        grad = mm(dq_ref[p, :], w_sc[pl.ds(0, width), :], NN)
        grad += mm(dk_ref[p, :], w_sc[pl.ds(width, width), :], NN)
        grad += mm(dv_ref[p, :], w_sc[pl.ds(2 * width, width), :], NN)
        out_ref[p, :] = (dx_ref[p, :] + norm_back(unit, rate, nrm_ref[0:1, :], grad)).astype(BF)
        dgain += jnp.sum(grad * unit, axis=0, keepdims=True)
        dshift += jnp.sum(grad, axis=0, keepdims=True)
    gn_ref[0:1, :] += dgain
    gn_ref[1:2, :] += dshift


def project_back(table, norms, dq, dk, dv, x, dx, weight, row, before, tb=512):
    n, width = x.shape
    count = len(weight.arrays)
    anywhere = pl.BlockSpec(memory_space=pl.ANY)
    per = ROW_LEN // tb
    block = pl.BlockSpec((tb, width), lambda t, tab: (row * per + t, 0))
    fixed = pl.BlockSpec((8, width), lambda t, tab: (0, 0))
    before = [] if before is None else [before]
    return pl.pallas_call(
        partial(project_back_kernel, weight, count),
        out_shape=[jax.ShapeDtypeStruct((n, width), BF), jax.ShapeDtypeStruct((8, width), F32)],
        grid_spec=pltpu.PrefetchScalarGridSpec(
            num_scalar_prefetch=1,
            grid=(per,),
            in_specs=[fixed] + [block] * 5 + [anywhere] * (count + len(before)),
            out_specs=[block, fixed],
            scratch_shapes=[pltpu.VMEM((3 * width, width), BF), pltpu.SemaphoreType.DMA((count,))],
        ),
        input_output_aliases={7 + count: 0} if before else {},
        compiler_params=pltpu.CompilerParams(vmem_limit_bytes=VMEM_LIMIT),
        cost_estimate=cost(6 * ROW_LEN * width * width, ROW_LEN * width * 14 + 6 * width * width),
        name="project_back",
    )(table, norms, dq, dk, dv, x, dx, *weight.arrays, *before)


def gelu_both(values):
    phi = 0.5 + 0.5 * lax.erf(values * math.sqrt(0.5))
    bell = jnp.exp(values * values * -0.5) * (1.0 / math.sqrt(2.0 * math.pi))
    return values * phi, phi + values * bell


def down_copies(weight, refs, block, dst, sems, me):
    out = []
    for i, (ref, (slot, _)) in enumerate(zip(refs, weight.places)):
        src = ref.at[pl.ds(pl.multiple_of(block * weight.per, weight.per), weight.per), :]
        at = pl.multiple_of((me ^ slot) * weight.per, weight.per)
        out.append(pltpu.make_async_copy(src, dst.at[pl.ds(at, weight.per), :], sems.at[i]))
    return out


def middle_kernel(size, tb, sub, chunks, w_up, w_down, w_proj, tab, nrm_ref, att_ref, x_ref, cot_ref, *rest):
    ups, downs = len(w_up.arrays), len(w_down.arrays)
    up_refs, down_refs = rest[:ups], rest[ups : ups + downs]
    proj_refs = down_refs if size == 8 else rest[ups + downs : ups + downs + 1]
    outs = 1 if size == 8 else 3
    rest = rest[-(22 + outs) :]
    x1_ref, act_ref, dx_ref, da_ref, gn_ref = rest[:5]
    g_refs = rest[5 : 5 + outs]
    x1_sc, h_sc, ht_sc, dy_sc, dyt_sc, dh_sc, gu_sc, gd_sc, wp_sc, wu_sc, wd_sc, su_sc, sd_sc, p_sem, u_sem, d_sem, g_sem = rest[
        5 + outs :
    ]
    j = pl.program_id(0)
    t = pl.program_id(1)
    steps = pl.num_programs(1)
    me = tab[tab.shape[0] - 1]
    per = ROW_LEN // tb
    valid = tab[lax.div(t, per) * STRIDE + 33]
    ok = (lax.broadcasted_iota(jnp.int32, (tb, 1), 0) + lax.rem(t, per) * tb) < valid
    ts = pl.ds(pl.multiple_of(t * tb, tb), tb)
    width = x_ref.shape[1]
    gain = nrm_ref[2:3, :]
    shift = nrm_ref[3:4, :]
    parts = [pl.ds(pl.multiple_of(t * tb + i, sub), sub) for i in range(0, tb, sub)]
    pieces = [pl.ds(i, sub) for i in range(0, tb, sub)]

    def chunk_copies(m):
        b = m % 2
        if size != 8:
            piece = pl.ds(m * width, width)
            up = [pltpu.make_async_copy(up_refs[0].at[piece, :], wu_sc.at[b], u_sem.at[b, 0])]
            down = [pltpu.make_async_copy(down_refs[0].at[:, piece], wd_sc.at[b], d_sem.at[b, 0])]
            return up + down
        up = []
        for i, (ref, (slot, _)) in enumerate(zip(up_refs, w_up.places)):
            if slot // 2 == m:
                at = pl.multiple_of(((me & 1) ^ (slot & 1)) * w_up.per, w_up.per)
                into = wu_sc.at[b].at[pl.ds(at, w_up.per), :]
                up.append(pltpu.make_async_copy(ref, into, u_sem.at[b, len(up)]))
        return up + down_copies(w_down, down_refs, (me >> 1) ^ m, wd_sc.at[b], d_sem.at[b], me)

    def proj_copies():
        if size != 8:
            return [pltpu.make_async_copy(proj_refs[0], wp_sc, p_sem.at[0])]
        return down_copies(w_down, proj_refs, chunks, wp_sc, p_sem, me)

    def packed_copies(block, up_pair=None):
        fw, dw = w_up.per, w_down.per
        whole = fw + (chunks + 1) * dw
        out = []
        for d in range(8):
            at = pl.multiple_of(d * whole + fw + block * dw, dw)
            out.append(pltpu.make_async_copy(sd_sc.at[pl.ds(d * dw, dw), :], g_refs[0].at[pl.ds(at, dw), :], g_sem.at[d]))
        if up_pair is not None:
            for k in range(2):
                at = pl.multiple_of((2 * up_pair + k) * whole, dw)
                out.append(pltpu.make_async_copy(su_sc.at[k], g_refs[0].at[pl.ds(at, fw), :], g_sem.at[8 + k]))
        return out

    @pl.when((j == 0) & (t == 0))
    def _():
        for c in proj_copies() + chunk_copies(0):
            c.start()
        for c in proj_copies():
            c.wait()

    for m in range(chunks):

        @pl.when((j == m) & (t == 0))
        def _():
            for c in chunk_copies(m):
                c.wait()
            if m + 1 < chunks:
                for c in chunk_copies(m + 1):
                    c.start()

    @pl.when(j == 0)
    def _():
        dy = jnp.where(ok, cot_ref[...], BF(0))
        dy_sc[ts, :] = dy
        x1s = [x_ref[p, :].astype(F32) + mm(att_ref[p, :], wp_sc[...], NT) for p in pieces]
        dyt_sc[:, ts] = dy.T
        for p, full, x1 in zip(pieces, parts, x1s):
            x1_sc[full, :] = x1
            x1_ref[p, :] = x1
            unit, _ = norm_stats(x1)
            h = (unit * gain + shift).astype(BF)
            h_sc[full, :] = h
            ht_sc[:, full] = h.T
        dh_sc[ts, :] = jnp.zeros((tb, width), F32)

    @pl.when((t == 0) & (j < chunks))
    def _():
        gu_sc[...] = jnp.zeros_like(gu_sc)
        gd_sc[...] = jnp.zeros_like(gd_sc)

    @pl.when(j < chunks)
    def _():
        wu = wu_sc[lax.rem(j, 2)]
        wd = wd_sc[lax.rem(j, 2)]
        uppers = [mm(h_sc[p, :], wu, NT) for p in parts]
        acts = []
        dups = []
        for p, upper in zip(parts, uppers):
            dact = mm(dy_sc[p, :], wd, NN)
            act, slope = gelu_both(upper)
            acts.append(act.astype(BF))
            dups.append((dact * slope).astype(BF))
        for p, dup in zip(parts, dups):
            dh_sc[p, :] += mm(dup, wu, NN)
        act = jnp.concatenate(acts, axis=0)
        act_ref[...] = act
        gd_sc[...] += mm(dyt_sc[:, ts], act, NN)
        gu_sc[...] += mm(ht_sc[:, ts], jnp.concatenate(dups, axis=0), NN)

    @pl.when((t == steps - 1) & (j < chunks))
    def _():
        if size == 8:
            pair = (me >> 1) ^ j

            @pl.when(j > 0)
            def _():
                before = (me >> 1) ^ (j - 1)
                for c in packed_copies(before, before):
                    c.wait()

            fw = w_up.per
            for k in range(2):
                for i in range(2):
                    su_sc[k, :, i * fw : (i + 1) * fw] = gu_sc[i * fw : (i + 1) * fw, k * fw : (k + 1) * fw].astype(BF)
            sd_sc[...] = gd_sc[...].astype(BF)
            for c in packed_copies(pair, pair):
                c.start()
        else:
            g_refs[0][...] = gu_sc[...].astype(BF)
            g_refs[1][...] = gd_sc[...].astype(BF)

    @pl.when(j == chunks)
    def _():
        @pl.when(t == 0)
        def _():
            gu_sc[...] = jnp.zeros_like(gu_sc)
            gn_ref[...] = jnp.zeros_like(gn_ref)

        dgain = jnp.zeros((1, width), F32)
        dshift = jnp.zeros((1, width), F32)
        dbs = []
        for p, full in zip(pieces, parts):
            unit, rate = norm_stats(x1_sc[full, :])
            dh = dh_sc[full, :]
            dx = dy_sc[full, :].astype(F32) + norm_back(unit, rate, gain, dh)
            dx_ref[p, :] = dx
            dbs.append(dx.astype(BF))
            da_ref[p, :] = mm(dbs[-1], wp_sc[...], NN).astype(BF)
            dgain += jnp.sum(dh * unit, axis=0, keepdims=True)
            dshift += jnp.sum(dh, axis=0, keepdims=True)
        gu_sc[...] += mm(jnp.concatenate(dbs, axis=0), att_ref[...], TN)
        gn_ref[0:1, :] += dgain
        gn_ref[1:2, :] += dshift

        @pl.when(t == steps - 1)
        def _():
            if size == 8:
                before = (me >> 1) ^ (chunks - 1)
                for c in packed_copies(before, before):
                    c.wait()
                sd_sc[...] = gu_sc[...].astype(BF)
                for c in packed_copies(chunks):
                    c.start()
                for c in packed_copies(chunks):
                    c.wait()
            else:
                g_refs[2][...] = gu_sc[...].astype(BF)


def middle(table, norms, att, x, cot, w_up, w_down, w_proj, hidden, size, tb=512, sub=256):
    n, width = x.shape
    chunks = hidden // width
    steps = n // tb
    last = chunks - 1
    dev = table.shape[0] - 1
    first = lambda j, t, tab: (jnp.where(j == 0, t, steps - 1), 0)
    ends = lambda j, t, tab: (jnp.where((j == 0) | (j == chunks), t, steps - 1), 0)
    final = lambda j, t, tab: (jnp.where(j == chunks, t, 0), 0)
    fixed = lambda j, t, tab: (0, 0)
    anywhere = pl.BlockSpec(memory_space=pl.ANY)
    now = lambda j: jnp.minimum(j, last)
    sds = jax.ShapeDtypeStruct
    if size == 8:
        fw, dw = w_up.per, w_down.per
        pair = lambda j, tab: lax.bitwise_xor(lax.shift_right_logical(tab[dev], 1), now(j))
        assert hidden == 8 * fw and width == 2 * fw == 8 * dw
        g_shapes = [sds((8 * (fw + (chunks + 1) * dw), width), BF)]
        g_specs = [anywhere]
    else:
        pair = lambda j, tab: now(j)
        g_shapes = [sds((width, hidden), BF)] * 2 + [sds((width, width), BF)]
        g_specs = [pl.BlockSpec((width, width), lambda j, t, tab: (0, now(j)))] * 2 + [
            pl.BlockSpec((width, width), fixed)
        ]
    block = lambda index: pl.BlockSpec((tb, width), index)
    acts = lambda j, t, tab: (jnp.where(j == chunks, steps - 1, t), pair(j, tab))
    weights = w_up.arrays + w_down.arrays + w_proj.arrays
    dma = pltpu.SemaphoreType.DMA
    return pl.pallas_call(
        partial(middle_kernel, size, tb, sub, chunks, w_up, w_down, w_proj),
        out_shape=[
            sds((n, width), F32),
            sds((n, hidden), BF),
            sds((n, width), F32),
            sds((n, width), BF),
            sds((8, width), F32),
        ]
        + g_shapes,
        grid_spec=pltpu.PrefetchScalarGridSpec(
            num_scalar_prefetch=1,
            grid=(chunks + 1, steps),
            in_specs=[pl.BlockSpec((8, width), fixed), block(ends), block(first), block(first)]
            + [anywhere] * len(weights),
            out_specs=[block(first), block(acts), block(final), block(final), pl.BlockSpec((8, width), fixed)]
            + g_specs,
            scratch_shapes=[
                pltpu.VMEM((n, width), F32),
                pltpu.VMEM((n, width), BF),
                pltpu.VMEM((width, n), BF),
                pltpu.VMEM((n, width), BF),
                pltpu.VMEM((width, n), BF),
                pltpu.VMEM((n, width), F32),
                pltpu.VMEM((width, width), F32),
                pltpu.VMEM((width, width), F32),
                pltpu.VMEM((width, width), BF),
                pltpu.VMEM((2, width, width), BF),
                pltpu.VMEM((2, width, width), BF),
                pltpu.VMEM((2, width // 2, width), BF),
                pltpu.VMEM((width, width), BF),
                dma((8,)),
                dma((2, 2)),
                dma((2, 8)),
                dma((10,)),
            ],
        ),
        compiler_params=pltpu.CompilerParams(vmem_limit_bytes=VMEM_LIMIT),
        cost_estimate=cost(n * width * (10 * hidden + 6 * width), n * (width * 22 + 2 * hidden) + 8 * hidden * width),
        name="middle",
    )(table, norms, att, x, cot, *weights)


def finish_kernel(size, blocks, w_down, row, tab, x1_ref, act_ref, *rest):
    w_refs = rest[: len(w_down.arrays)]
    out_ref, w_sc, sems = rest[-3:]
    t = pl.program_id(0)
    me = tab[tab.shape[0] - 1]
    tb, width = x1_ref.shape

    def copies(b):
        if size == 8:
            return down_copies(w_down, w_refs, b, w_sc.at[:, pl.ds(b * width, width)], sems.at[b], me)
        at = pl.ds(b * width, width)
        return [pltpu.make_async_copy(w_refs[0].at[:, at], w_sc.at[:, at], sems.at[b, 0])]

    @pl.when(t == 0)
    def _():
        for b in range(blocks):
            for c in copies(b):
                c.start()
        for b in range(blocks):
            for c in copies(b):
                c.wait()

    x2 = x1_ref[...] + mm(act_ref[...], w_sc[...], NT)
    ok = (lax.broadcasted_iota(jnp.int32, (tb, 1), 0) + t * tb) < tab[row * STRIDE + 33]
    out_ref[...] = jnp.where(ok, x2, 0.0).astype(BF)


def finish(table, x1, act, w_down, row, before, size, tb=512):
    n, width = x1.shape
    hidden = act.shape[1]
    blocks = hidden // width
    per = ROW_LEN // tb
    before = [] if before is None else [before]
    count = len(w_down.arrays)
    block = lambda w: pl.BlockSpec((tb, w), lambda t, tab: (row * per + t, 0))
    return pl.pallas_call(
        partial(finish_kernel, size, blocks, w_down, row),
        out_shape=jax.ShapeDtypeStruct((n, width), BF),
        grid_spec=pltpu.PrefetchScalarGridSpec(
            num_scalar_prefetch=1,
            grid=(per,),
            in_specs=[block(width), block(hidden)] + [pl.BlockSpec(memory_space=pl.ANY)] * (count + len(before)),
            out_specs=block(width),
            scratch_shapes=[pltpu.VMEM((width, hidden), BF), pltpu.SemaphoreType.DMA((blocks, 8))],
        ),
        input_output_aliases={3 + count: 0} if before else {},
        compiler_params=pltpu.CompilerParams(vmem_limit_bytes=VMEM_LIMIT),
        cost_estimate=cost(2 * ROW_LEN * width * hidden, ROW_LEN * (width * 6 + hidden * 2) + 2 * width * hidden),
        name="finish",
    )(table, x1, act, *w_down.arrays, *before)


def per_device(
    size,
    replicas,
    tokens,
    segment_ids,
    cotangent,
    norm_params,
    qkv_weight,
    proj_weight,
    up_weight,
    down_weight,
    target_norms,
    target_qkv,
    target_proj,
    target_up,
    target_down,
):
    count, width = tokens.shape
    rows = count // ROW_LEN
    hidden = down_weight.shape[0]
    own = width // size
    blocks = hidden // width
    fast = size == 8 and replicas == 4
    size = size if fast else 0
    me = lax.axis_index("fsdp")
    table = job_table(segment_ids, rows, me)
    with jax.named_scope("gather_weights"):
        placed = lax.dynamic_update_slice(jnp.zeros((16, width), BF), norm_params, (0, me * own))
        qkv_t, up_t, down_t, proj_t = qkv_weight.T, up_weight.T, down_weight.T, proj_weight.T
        if fast:
            half = qkv_t.shape[0] // 2
            first, second = gather_cross(jnp.concatenate([qkv_t[:half], placed], axis=0), qkv_t[half:])
            far = forward_cross(first, second)
            upper = both_cores([*first, far[0]])
            lower = both_cores([*second, far[1]])
            w_qkv = Weight([(a, s, 0) for a, s in upper] + [(a, s, half) for a, s in lower], 2 * half)
            norm_parts = []
            packed = jnp.concatenate([down_t[:, b * width : (b + 1) * width] for b in range(blocks)] + [proj_t], axis=0)
            up_1, down_1 = after((up_t, packed), first[1], second[2])
            up_x, down_y = hop(up_1, 2, 8), hop(down_1, 4, 8)
            up_2, down_2 = after((up_t, packed), *far)
            up_y, down_x = hop(up_2, 4, 8), hop(down_2, 2, 8)
        else:
            whole = lambda shard: lax.all_gather(shard, "fsdp", axis=0, tiled=True)
            w_qkv, w_up, w_down, w_proj = (Weight([(whole(w), None, 0)], 0) for w in (qkv_t, up_t, down_t, proj_t))
            norm_parts = [lax.psum(placed.astype(F32), "fsdp").astype(BF)]

    keep_rate = 1.0 - ema_rate
    blend = lambda target, weight: ema_rate * target + keep_rate * weight.astype(F32)
    targets = (
        blend(target_norms, norm_params),
        blend(target_qkv, qkv_weight),
        blend(target_proj, proj_weight),
        blend(target_up, up_weight),
        blend(target_down, down_weight),
    )
    stage, *targets = lax.optimization_barrier((table, *targets))
    h1, qkv, norms = project(stage, norm_parts, tokens, w_qkv)
    attended = None
    stage = table
    if fast:
        with jax.named_scope("gather_weights"):
            up_x, down_y, up_t, packed = after((up_x, down_y, up_t, packed), qkv)
            up_far, down_far = forward_cross((None, up_x), (None, None, down_y))
            near = both_cores([up_t, up_x]), both_cores([packed])
            stage = after(table, up_x, down_y)
    for row in range(rows):
        attended = attention_forward(qkv, stage, row, attended)
        if fast and row == 0:
            with jax.named_scope("gather_weights"):
                up_y, down_x, down_y = after((up_y, down_x, down_y), attended[0])
                along = hop(up_y, 1, 8), hop(down_x, 1, 8), hop(down_y, 1, 8)
                stage = after(table, up_y, down_x, down_y)
    if fast:
        with jax.named_scope("gather_weights"):
            up_far, down_far = after((up_far, down_far), attended[0])
            ups = near[0] + [(up_y, 4), (along[0], 5), (up_far, 6), (hop(up_far, 1, 8), 7)]
            downs = near[1] + [(down_x, 2), (along[1], 3), (down_y, 4), (along[2], 5)]
            downs += [(down_far, 6), (hop(down_far, 1, 8), 7)]
            w_up = Weight([(a, s, 0) for a, s in ups], up_t.shape[0])
            w_down = Weight([(a, s, 0) for a, s in downs], own)
            w_proj = Weight([], own)
    x1, act, grad_middle, grad_attended, grad_norm2, *grads = middle(
        table, norms, attended[0], tokens, cotangent, w_up, w_down, w_proj, hidden, size
    )

    dqkv = None
    input_grad = None
    block_output = None
    norm_grads = []
    after_table = lambda *values: after(table, *values)
    if fast:
        packed_own = lax.psum_scatter(grads[0], "fsdp", scatter_dimension=0, tiled=True)
    for row in range(rows):
        dqkv = attention_backward(qkv, grad_attended, table, row, 0, 1, dqkv)
    if fast:
        grad_qkv = project_grad(table, *dqkv, h1, size)
        qkv_sum = Scatter(*grad_qkv)
        block_output = finish(after_table(grad_qkv[0]), x1, act, w_down, 0, None, size)
        stage = after_table(*qkv_sum.send(block_output))
        for row in range(1, rows):
            block_output = finish(stage, x1, act, w_down, row, block_output, size)
        packed_own = after(packed_own, block_output)
        packed_sum = lax.psum(packed_own, "rep")
        stage = after_table(packed_own)
        input_grad, part = project_back(stage, norms, *dqkv, tokens, grad_middle, w_qkv, 0, None)
        norm_grads.append(part)
        qkv_own = qkv_sum.block(part)
        stage = after_table(qkv_own)
        for row in range(1, rows):
            input_grad, part = project_back(stage, norms, *dqkv, tokens, grad_middle, w_qkv, row, input_grad)
            norm_grads.append(part)
        qkv_own = direct_sum(qkv_own, part)
        norm_sum = jnp.concatenate(
            [sum(p[:2] for p in norm_grads), grad_norm2[:2], jnp.zeros((4, width), F32)], axis=0
        )
        for bit in (1, 2, 4):
            norm_sum = norm_sum + hop(norm_sum, bit, 8)
        for bit in (1, 2):
            norm_sum = norm_sum + lax.ppermute(norm_sum, "rep", [(i, i ^ bit) for i in range(4)])
        packed_sum = packed_sum.astype(F32)
        fw = hidden // 8
        up = jnp.concatenate([packed_sum[:fw, :fw], packed_sum[:fw, fw:]], axis=0)
        down = packed_sum[fw : fw + blocks * own].reshape(blocks, own, width).transpose(1, 0, 2).reshape(own, hidden)
        proj = packed_sum[fw + blocks * own :]
    else:
        grad_qkv = project_grad(table, *dqkv, h1, size)
        for row in range(rows):
            input_grad, part = project_back(table, norms, *dqkv, tokens, grad_middle, w_qkv, row, input_grad)
            norm_grads.append(part)
            block_output = finish(table, x1, act, w_down, row, block_output, size)
        sums = lambda g, dim: lax.psum(lax.psum_scatter(g, "fsdp", scatter_dimension=dim, tiled=True), "rep").astype(F32)
        up, down, proj, qkv_own = sums(grads[0], 1), sums(grads[1], 0), sums(grads[2], 0), sums(grad_qkv[0], 0)
        norm_sum = jnp.concatenate([sum(p[:2] for p in norm_grads), grad_norm2[:2]], axis=0)
        norm_sum = lax.psum(norm_sum, ("fsdp", "rep"))
    norm_grad = lax.dynamic_slice(norm_sum, (0, me * own), (4, own))
    return (block_output, input_grad, norm_grad, qkv_own.T, proj.T, up, down.T, *targets)


def solution(mesh):
    tokens = P(("fsdp", "rep"), None)
    columns = P(None, "fsdp")
    return jax.shard_map(
        partial(per_device, mesh.shape["fsdp"], mesh.shape["rep"]),
        mesh=mesh,
        in_specs=(tokens, P(("fsdp", "rep")), tokens) + (columns,) * 10,
        out_specs=(tokens, tokens) + (columns,) * 10,
        check_vma=False,
    )
```

time: 460 us -> 378 us (0.82)
  waiting for transfers between devices: 118 us -> 47.6 us
  starting transfers between devices: 71 us -> 43.8 us
  local copies, waits for them, and re-layouts: 7.01 us -> 29.5 us
  between operations: 2 us -> 15.2 us
  other arithmetic: 27.7 us -> 16.9 us
  Pallas kernels: 229 us -> 219 us
    ppermute x65 -> x35, waiting for transfers between devices: 78.6 us -> 23.3 us  [hop(): return lax.ppermute(value, 'fsdp', [(i, i ^ bit) for i in range(size)])]
    ppermute x16 -> x8, waiting for transfers between devices: 39.2 us -> 13.8 us  [the longest x6 8.67 us: direct_sum(): lax.ppermute(value, 'rep', [(i, (i + by) % 4) for i in range(4)])]
    unnamed x73 -> x89, local copies, waits for them, and re-layouts: 4.1 us -> 21.7 us
    pallas_call x5 -> x8, Pallas kernels: 198 us -> 182 us  [the longest x1 86.6 us: middle(): pl.pallas_call(partial(middle_kernel, size, tb, sub, chunks, w_up, w_down...]
    ppermute x65 -> x35, starting transfers between devices: 44.8 us -> 29.9 us  [hop(): return lax.ppermute(value, 'fsdp', [(i, i ^ bit) for i in range(size)])]
    ppermute x16 -> x8, starting transfers between devices: 26.1 us -> 13.8 us  [the longest x6 10 us: direct_sum(): lax.ppermute(value, 'rep', [(i, (i + by) % 4) for i in range(4)])]
    psum x0 -> x1, waiting for transfers between devices: none -> 10.4 us  [per_device(): packed_sum = lax.psum(packed_own, 'rep')]
    convert_element_type x22 -> x3, other arithmetic: 11.5 us -> 4.85 us  [the longest x2 4.67 us: total(): return sum((t.astype(F32) for t in terms)).astype(BF)]
  transfers between devices with their start and end apart: 81 -> 45, of which waited for: 31 -> 12; matrix products, arithmetic and copies ran while one was open for 7% -> 6% of each run, Pallas kernels for 22% -> 36%
where the time goes in v2:
time: 378 us; the launch traced here: 372 us
  Pallas kernels  219 us (58%)
  waiting for transfers between devices  47.6 us (13%)
  starting transfers between devices  43.8 us (12%)
  local copies, waits for them, and re-layouts  29.5 us (8%)
  other arithmetic  16.9 us (4%)
  between operations  15.2 us (4%)
    pallas_call x1, Pallas kernels, middle(): pl.pallas_call(partial(middle_kernel, size, tb, sub, chunks, w_up, w_down...  86.6 us
    pallas_call x4, Pallas kernels, row_call(): pl.pallas_call(partial(kernel, w // 128, row), out_shape=[jax.ShapeDtypeS...  54.8 us
    ppermute x35, starting transfers between devices, hop(): return lax.ppermute(value, 'fsdp', [(i, i ^ bit) for i in range(size)])  29.9 us
    pallas_call x2, Pallas kernels, finish(): pl.pallas_call(partial(finish_kernel, size, blocks, w_down, row), out_sha...  25.5 us
    pallas_call x2, Pallas kernels, project_back(): pl.pallas_call(partial(project_back_kernel, weight, count), out_shape=[ja...  23.8 us
    ppermute x35, waiting for transfers between devices, hop(): return lax.ppermute(value, 'fsdp', [(i, i ^ bit) for i in range(size)])  23.3 us
    unnamed x89, local copies, waits for them, and re-layouts  21.7 us
    pallas_call x1, Pallas kernels, project(): pl.pallas_call(partial(project_kernel, weight, count), out_shape=[sds((n,...  14.7 us
  transfers between devices with their start and end apart: 45, of which 12 were waited for; matrix products, arithmetic and copies ran while one was open for 6% of the time, Pallas kernels for 36%

profile of v2, /device:TPU:0, one launch (start us, length us, event | category | flops | bytes accessed | tf_op | source)
XLA Modules:
  0.0 372.0 jit_solution(5942792036035977504)
XLA Ops:
  8.9 2.6 collective-permute-start.8
  19.0 2.6 multiply_add_fusion
  29.1 4.7 %collective-permute-done.9.rest_11_ = bf16[144,768]{1,0:T(8,128)(2,1)} collective-permute-done((bf16[144,768]{1,0:T(8,128)(2,1)}, bf16[144,768]{1,0:T(8,128)(2,1)}, u32[]{:S(2)}, u32[]{:S(2)}) %collective-permute-start.9) | collective-permute-done | bytes 221216 | tf_op jit(solution)/shard_map/gather_weights/ppermute | solution.py:331
  41.9 14.7 %project.1 = (bf16[2048,768]{1,0:T(8,128)(2,1)}, bf16[2048,2304]{1,0:T(8,128)(2,1)}, f32[8,768]{1,0:T(8,128)}) custom-call(s32[71]{0:T(128)} %pad_add_fusion.tab, bf16[2048,768]{1,0:T(8,128)(2,1)} %x_ref.7, bf16[160,768]{1,0:T(8,128)(2,1)} %copy-done.16, bf16[160,768]{1,0:T(8,128)(2,1)} %copy-done.21, bf16[160,768]{1,0:T(8,128)(2,1)} %copy-done.20, ...), custom_call_target="tpu_custom_call" | custom-call | flops 144955152 | bytes 385351 | tf_op jit(solution)/shard_map/project/pallas_call | solution.py:455
  58.5 7.5 %collective-permute-done.14.rest_4_ = bf16[384,768]{1,0:T(8,128)(2,1)} collective-permute-done((bf16[384,768]{1,0:T(8,128)(2,1)}, bf16[384,768]{1,0:T(8,128)(2,1)}, u32[]{:S(2)}, u32[]{:S(2)}) %collective-permute-start.14) | collective-permute-done | bytes 589856 | tf_op jit(solution)/shard_map/gather_weights/ppermute | solution.py:331
  66.9 3.7 copy-done
  70.5 9.4 %attend.2.rest_0_ = bf16[2048,768]{1,0:T(8,128)(2,1)S(1)} custom-call(s32[71]{0:T(128)S(1)} %copy-done.7, bf16[2048,2304]{1,0:T(8,128)(2,1)S(1)} %copy-done, bf16[2048,2304]{1,0:T(8,128)(2,1)S(1)} %copy-done, bf16[2048,2304]{1,0:T(8,128)(2,1)S(1)} %copy-done), custom_call_target="tpu_custom_call" | custom-call | flops 240000000 | bytes 125829 | tf_op jit(solution)/shard_map/attend/pallas_call | solution.py:301
  80.0 10.4 %attend.3.att_ref = bf16[2048,768]{1,0:T(8,128)(2,1)S(1)} custom-call(s32[71]{0:T(128)S(1)} %copy-done.7, bf16[2048,2304]{1,0:T(8,128)(2,1)S(1)} %copy-done, bf16[2048,2304]{1,0:T(8,128)(2,1)S(1)} %copy-done, bf16[2048,2304]{1,0:T(8,128)(2,1)S(1)} %copy-done, bf16[2048,768]{1,0:T(8,128)(2,1)S(1)} %attend.2.rest_0_), custom_call_target="tpu_custom_call", output_to_operand_aliasing={{}: (4, {})} | custom-call | flops 240000000 | bytes 125829 | tf_op jit(solution)/shard_map/attend/pallas_call | solution.py:301
  94.1 4.7 %collective-permute-done.20.rest_5_ = bf16[384,768]{1,0:T(8,128)(2,1)S(1)} collective-permute-done((bf16[384,768]{1,0:T(8,128)(2,1)}, bf16[384,768]{1,0:T(8,128)(2,1)S(1)}, u32[]{:S(2)}, u32[]{:S(2)}) %collective-permute-start.20) | collective-permute-done | bytes 589856 | tf_op jit(solution)/shard_map/gather_weights/ppermute | solution.py:331
  101.0 86.6 %middle.1 = (f32[2048,768]{1,0:T(8,128)}, bf16[2048,3072]{1,0:T(8,128)(2,1)}, f32[2048,768]{1,0:T(8,128)}, bf16[2048,768]{1,0:T(8,128)(2,1)}, f32[8,768]{1,0:T(8,128)}, /*index=5*/bf16[6912,768]{1,0:T(8,128)(2,1)}) custom-call(s32[71]{0:T(128)} %pad_add_fusion.tab, f32[8,768]{1,0:T(8,128)} %get-tuple-element.68.nrm_ref, bf16[2048,768]{1,0:T(8,128)(2,1)} %copy-done.5, ...), custom_call_target="tpu_custom_call" | custom-call | flops 1111322752 | bytes 1321205 | tf_op jit(solution)/shard_map/middle/pallas_call | solution.py:799
  187.8 1.8 copy-done.6
  189.6 3.7 copy-done.1
  193.3 15.2 %attend_back.2 = (bf16[2048,768]{1,0:T(8,128)(2,1)S(1)}, bf16[2048,768]{1,0:T(8,128)(2,1)S(1)}, bf16[2048,768]{1,0:T(8,128)(2,1)S(1)}) custom-call(s32[71]{0:T(128)S(1)} %copy-done.8, bf16[2048,2304]{1,0:T(8,128)(2,1)S(1)} %copy-done.1, bf16[2048,2304]{1,0:T(8,128)(2,1)S(1)} %copy-done.1, bf16[2048,2304]{1,0:T(8,128)(2,1)S(1)} %copy-done.1, ...), custom_call_target="tpu_custom_call" | custom-call | flops 480000000 | bytes 220200 | tf_op jit(solution)/shard_map/attend_back/pallas_call | solution.py:301
  208.5 19.8 %attend_back.3 = (bf16[2048,768]{1,0:T(8,128)(2,1)S(1)}, bf16[2048,768]{1,0:T(8,128)(2,1)S(1)}, bf16[2048,768]{1,0:T(8,128)(2,1)S(1)}) custom-call(s32[71]{0:T(128)S(1)} %copy-done.8, bf16[2048,2304]{1,0:T(8,128)(2,1)S(1)} %copy-done.1, bf16[2048,2304]{1,0:T(8,128)(2,1)S(1)} %copy-done.1, ...), custom_call_target="tpu_custom_call", output_to_operand_aliasing={{0}: (5, {}), {1}: (6, {}), {2}: (7, {})} | custom-call | flops 480000000 | bytes 220200 | tf_op jit(solution)/shard_map/attend_back/pallas_call | solution.py:301
  233.3 13.7 %project_grad.1 = (bf16[4,288,768]{2,1,0:T(8,128)(2,1)}, bf16[4,288,768]{2,1,0:T(8,128)(2,1)}) custom-call(s32[71]{0:T(128)} %pad_add_fusion.tab, bf16[2048,768]{1,0:T(8,128)(2,1)} %copy-done.2, bf16[2048,768]{1,0:T(8,128)(2,1)} %copy-done.3, bf16[2048,768]{1,0:T(8,128)(2,1)} %copy-done.4, bf16[2048,768]{1,0:T(8,128)(2,1)} %get-tuple-element.91.h_ref), custom_call_target="tpu_custom_call" | custom-call | flops 144955152 | bytes 322437 | tf_op jit(solution)/shard_map/project_grad/pallas_call | solution.py:508
  247.1 3.3 collective-permute-start.28
  250.4 13.1 %finish.2.rest_8_ = bf16[2048,768]{1,0:T(8,128)(2,1)} custom-call(s32[71]{0:T(128)} %pad_add_fusion.tab, f32[2048,768]{1,0:T(8,128)} %get-tuple-element.95.x1_ref, bf16[2048,3072]{1,0:T(8,128)(2,1)} %get-tuple-element.96.act_ref, bf16[480,768]{1,0:T(8,128)(2,1)} %copy-done.10, bf16[480,768]{1,0:T(8,128)(2,1)} %copy-done.12, ...), custom_call_target="tpu_custom_call" | custom-call | flops 96636768 | bytes 314572 | tf_op jit(solution)/shard_map/finish/pallas_call | solution.py:877
  263.6 2.9 fusion.5
  266.5 6.3 %collective-permute-start.31 = (bf16[288,768]{1,0:T(8,128)(2,1)}, bf16[288,768]{1,0:T(8,128)(2,1)S(1)}, u32[]{:S(2)}, u32[]{:S(2)}) collective-permute-start(bf16[288,768]{1,0:T(8,128)(2,1)} %get-tuple-element.124), channel_id=1, source_target_pairs={{0,24},{4,28},{8,16},{12,20},{16,8},{20,12},{24,0},{28,4},{1,25},{... | collective-permute-start | bytes 1327112 | tf_op jit(solution)/shard_map/ppermute | solution.py:331
  274.2 12.3 %finish.3 = bf16[2048,768]{1,0:T(8,128)(2,1)} custom-call(s32[71]{0:T(128)} %pad_add_fusion.tab, f32[2048,768]{1,0:T(8,128)} %get-tuple-element.95.x1_ref, bf16[2048,3072]{1,0:T(8,128)(2,1)} %get-tuple-element.96.act_ref, bf16[480,768]{1,0:T(8,128)(2,1)} %copy-done.10, bf16[480,768]{1,0:T(8,128)(2,1)} %copy-done.12, ...), custom_call_target="tpu_custom_call", output_to_operand_aliasing={{}: (11, {})} | custom-call | flops 96636768 | bytes 314572 | tf_op jit(solution)/shard_map/finish/pallas_call | solution.py:877
  286.6 11.8 %project_back.2 = (bf16[2048,768]{1,0:T(8,128)(2,1)}, f32[8,768]{1,0:T(8,128)}) custom-call(s32[71]{0:T(128)} %pad_add_fusion.tab, f32[8,768]{1,0:T(8,128)} %get-tuple-element.68.nrm_ref, bf16[2048,768]{1,0:T(8,128)(2,1)} %copy-done.2, bf16[2048,768]{1,0:T(8,128)(2,1)} %copy-done.3, bf16[2048,768]{1,0:T(8,128)(2,1)} %copy-done.4, bf16[2048,768]{1,0:T(8,128)(2,1)} %x_ref.7, ...), custom_call_target="tpu_custom_call" | custom-call | flops 72477576 | bytes 290979 | tf_op jit(solution)/shard_map/project_back/pallas_call | solution.py:564
  300.2 11.9 %project_back.3 = (bf16[2048,768]{1,0:T(8,128)(2,1)}, f32[8,768]{1,0:T(8,128)}) custom-call(s32[71]{0:T(128)} %pad_add_fusion.tab, f32[8,768]{1,0:T(8,128)} %get-tuple-element.68.nrm_ref, bf16[2048,768]{1,0:T(8,128)(2,1)} %copy-done.2, bf16[2048,768]{1,0:T(8,128)(2,1)} %copy-done.3, bf16[2048,768]{1,0:T(8,128)(2,1)} %copy-done.4, ...), custom_call_target="tpu_custom_call", output_to_operand_aliasing={{0}: (23, {})} | custom-call | flops 72477576 | bytes 290979 | tf_op jit(solution)/shard_map/project_back/pallas_call | solution.py:564
  313.1 2.6 collective-permute-start.39
  317.7 2.5 collective-permute-done.33
  321.7 2.3 collective-permute-done.34
  324.0 3.8 %collective-permute-start.35 = (f32[8,768]{1,0:T(8,128)S(1)}, f32[8,768]{1,0:T(8,128)S(1)}, u32[]{:S(2)}, u32[]{:S(2)}) collective-permute-start(f32[8,768]{1,0:T(8,128)S(1)} %add.199), channel_id=1, source_target_pairs={{0,1},{1,0},{2,3},{3,2},{4,5},{5,4},{6,7},{7,6},{8,9},{9,8},{10,11... | collective-permute-start | bytes 73736 | tf_op jit(solution)/shard_map/ppermute | solution.py:1013
  327.8 3.4 collective-permute-done.35
  331.3 3.0 collective-permute-start.41
  335.3 2.9 collective-permute-start.42
  340.6 5.8 %collective-permute-done.40 = bf16[72,768]{1,0:T(8,128)(2,1)S(1)} collective-permute-done((bf16[72,768]{1,0:T(8,128)(2,1)S(1)}, bf16[72,768]{1,0:T(8,128)(2,1)S(1)}, u32[]{:S(2)}, u32[]{:S(2)}) %collective-permute-start.40) | collective-permute-done | bytes 110624 | tf_op jit(solution)/shard_map/ppermute | solution.py:373
  346.4 2.8 collective-permute-done.41
  349.3 10.4 %all-reduce.2.cloned.1.call-done = bf16[864,768]{1,0:T(8,128)(2,1)} async-done(((bf16[864,768]{1,0:T(8,128)(2,1)}), bf16[864,768]{1,0:T(8,128)(2,1)}) %all-reduce.2.cloned.1.call-update) | async-done | bytes 1327120 | tf_op jit(solution)/shard_map/psum | solution.py:997
  (210 shorter events, 54.3 us)
Async XLA Ops:
  7.2 279.4 %reduce-scatter.2.cloned.1.call-start = ((), (), s32[]{:S(2)}) async-start(), calls=%async_computation.1 | async-start | bytes 11943936 | tf_op jit(solution)/shard_map/reduce_scatter | solution.py:986
  8.4 15.2 %collective-permute-start.10 = (bf16[144,768]{1,0:T(8,128)(2,1)S(1)}, bf16[144,768]{1,0:T(8,128)(2,1)S(1)}, u32[]{:S(2)}, u32[]{:S(2)}) collective-permute-start(bf16[144,768]{1,0:T(8,128)(2,1)S(1)} %get-tuple-element.132.rest_8_), channel_id=1, source_target_pairs={{0,4},{4,0},{8,12},{12,8},{16,20},{20,16},{24,28},{28,24},{1,5},{5... | collective-permute-start | bytes 663560 | tf_op jit(solution)/shard_map/gather_weights/ppermute | solution.py:331
  8.9 17.1 %collective-permute-start.8 = (bf16[144,768]{1,0:T(8,128)(2,1)S(1)}, bf16[144,768]{1,0:T(8,128)(2,1)}, u32[]{:S(2)}, u32[]{:S(2)}) collective-permute-start(bf16[144,768]{1,0:T(8,128)(2,1)S(1)} %get-tuple-element.132.rest_8_), channel_id=1, source_target_pairs={{0,16},{4,20},{8,24},{12,28},{16,0},{20,4},{24,8},{28,12},{1,17},{... | collective-permute-start | bytes 663560 | tf_op jit(solution)/shard_map/gather_weights/ppermute | solution.py:331
  11.5 15.9 %collective-permute-start.7 = (bf16[144,768]{1,0:T(8,128)(2,1)S(1)}, bf16[144,768]{1,0:T(8,128)(2,1)}, u32[]{:S(2)}, u32[]{:S(2)}) collective-permute-start(bf16[144,768]{1,0:T(8,128)(2,1)S(1)} %get-tuple-element.132.rest_8_), channel_id=1, source_target_pairs={{0,8},{4,12},{8,0},{12,4},{16,24},{20,28},{24,16},{28,20},{1,9},{5... | collective-permute-start | bytes 663560 | tf_op jit(solution)/shard_map/gather_weights/ppermute | solution.py:331
  14.6 12.9 %collective-permute-start.1 = (bf16[160,768]{1,0:T(8,128)(2,1)S(1)}, bf16[160,768]{1,0:T(8,128)(2,1)S(1)}, u32[]{:S(2)}, u32[]{:S(2)}) collective-permute-start(bf16[160,768]{1,0:T(8,128)(2,1)S(1)} %pad_maximum_fusion.1.rest_0_), channel_id=1, source_target_pairs={{0,16},{4,20},{8,24},{12,28},{16,0},{20,4},{24,8},{28,12},{1,17},{... | collective-permute-start | bytes 737288 | tf_op jit(solution)/shard_map/gather_weights/ppermute | solution.py:331
  15.2 9.1 %collective-permute-start = (bf16[160,768]{1,0:T(8,128)(2,1)S(1)}, bf16[160,768]{1,0:T(8,128)(2,1)S(1)}, u32[]{:S(2)}, u32[]{:S(2)}) collective-permute-start(bf16[160,768]{1,0:T(8,128)(2,1)S(1)} %pad_maximum_fusion.1.rest_0_), channel_id=1, source_target_pairs={{0,8},{4,12},{8,0},{12,4},{16,24},{20,28},{24,16},{28,20},{1,9},{5... | collective-permute-start | bytes 737288 | tf_op jit(solution)/shard_map/gather_weights/ppermute | solution.py:331
  24.3 9.6 %collective-permute-start.2 = (bf16[160,768]{1,0:T(8,128)(2,1)S(1)}, bf16[160,768]{1,0:T(8,128)(2,1)S(1)}, u32[]{:S(2)}, u32[]{:S(2)}) collective-permute-start(bf16[160,768]{1,0:T(8,128)(2,1)S(1)} %collective-permute-done.rest_1_), channel_id=1, source_target_pairs={{0,16},{4,20},{8,24},{12,28},{16,0},{20,4},{24,8},{28,12},{1,17},{... | collective-permute-start | bytes 737288 | tf_op jit(solution)/shard_map/gather_weights/ppermute | solution.py:331
  26.1 7.8 %collective-permute-start.9 = (bf16[144,768]{1,0:T(8,128)(2,1)}, bf16[144,768]{1,0:T(8,128)(2,1)}, u32[]{:S(2)}, u32[]{:S(2)}) collective-permute-start(bf16[144,768]{1,0:T(8,128)(2,1)} %collective-permute-done.8.rest_10_), channel_id=1, source_target_pairs={{0,8},{4,12},{8,0},{12,4},{16,24},{20,28},{24,16},{28,20},{1,9},{5... | collective-permute-start | bytes 663560 | tf_op jit(solution)/shard_map/gather_weights/ppermute | solution.py:331
  27.4 10.3 %collective-permute-start.4 = (bf16[160,768]{1,0:T(8,128)(2,1)S(1)}, bf16[160,768]{1,0:T(8,128)(2,1)S(1)}, u32[]{:S(2)}, u32[]{:S(2)}) collective-permute-start(bf16[160,768]{1,0:T(8,128)(2,1)S(1)} %collective-permute-done.rest_1_), channel_id=1, source_target_pairs={{0,4},{4,0},{8,12},{12,8},{16,20},{20,16},{24,28},{28,24},{1,5},{5... | collective-permute-start | bytes 737288 | tf_op jit(solution)/shard_map/gather_weights/ppermute | solution.py:331
  27.5 8.7 %collective-permute-start.5 = (bf16[160,768]{1,0:T(8,128)(2,1)S(1)}, bf16[160,768]{1,0:T(8,128)(2,1)S(1)}, u32[]{:S(2)}, u32[]{:S(2)}) collective-permute-start(bf16[160,768]{1,0:T(8,128)(2,1)S(1)} %collective-permute-done.1.rest_2_), channel_id=1, source_target_pairs={{0,4},{4,0},{8,12},{12,8},{16,20},{20,16},{24,28},{28,24},{1,5},{5... | collective-permute-start | bytes 737288 | tf_op jit(solution)/shard_map/gather_weights/ppermute | solution.py:331
  33.9 22.7 %collective-permute-start.17 = (bf16[480,768]{1,0:T(8,128)(2,1)S(1)}, bf16[480,768]{1,0:T(8,128)(2,1)}, u32[]{:S(2)}, u32[]{:S(2)}) collective-permute-start(bf16[480,768]{1,0:T(8,128)(2,1)S(1)} %bitcast_dynamic-update-slice_fusion.rest_8_.rest_0_), channel_id=1, source_target_pairs={{0,16},{4,20},{8,24},{12,28},{16,0},{20,4},{24,8},{28,12},{1,17},{... | collective-permute-start | bytes 2211848 | tf_op jit(solution)/shard_map/gather_weights/ppermute | solution.py:331
  34.5 22.1 %collective-permute-start.16 = (bf16[384,768]{1,0:T(8,128)(2,1)}, bf16[384,768]{1,0:T(8,128)(2,1)}, u32[]{:S(2)}, u32[]{:S(2)}) collective-permute-start(bf16[384,768]{1,0:T(8,128)(2,1)} %bitcast.4.rest_0_), channel_id=1, source_target_pairs={{0,8},{4,12},{8,0},{12,4},{16,24},{20,28},{24,16},{28,20},{1,9},{5... | collective-permute-start | bytes 1769480 | tf_op jit(solution)/shard_map/gather_weights/ppermute | solution.py:331
  36.2 29.8 %collective-permute-start.14 = (bf16[384,768]{1,0:T(8,128)(2,1)}, bf16[384,768]{1,0:T(8,128)(2,1)}, u32[]{:S(2)}, u32[]{:S(2)}) collective-permute-start(bf16[384,768]{1,0:T(8,128)(2,1)} %bitcast.4.rest_0_), channel_id=1, source_target_pairs={{0,16},{4,20},{8,24},{12,28},{16,0},{20,4},{24,8},{28,12},{1,17},{... | collective-permute-start | bytes 1769480 | tf_op jit(solution)/shard_map/gather_weights/ppermute | solution.py:331
  37.8 29.1 %collective-permute-start.15 = (bf16[480,768]{1,0:T(8,128)(2,1)S(1)}, bf16[480,768]{1,0:T(8,128)(2,1)}, u32[]{:S(2)}, u32[]{:S(2)}) collective-permute-start(bf16[480,768]{1,0:T(8,128)(2,1)S(1)} %bitcast_dynamic-update-slice_fusion.rest_8_.rest_0_), channel_id=1, source_target_pairs={{0,8},{4,12},{8,0},{12,4},{16,24},{20,28},{24,16},{28,20},{1,9},{5... | collective-permute-start | bytes 2211848 | tf_op jit(solution)/shard_map/gather_weights/ppermute | solution.py:331
  56.6 36.4 %collective-permute-start.22 = (bf16[480,768]{1,0:T(8,128)(2,1)}, bf16[480,768]{1,0:T(8,128)(2,1)S(1)}, u32[]{:S(2)}, u32[]{:S(2)}) collective-permute-start(bf16[480,768]{1,0:T(8,128)(2,1)} %collective-permute-done.17.rest_12_.rest_4_), channel_id=1, source_target_pairs={{0,8},{4,12},{8,0},{12,4},{16,24},{20,28},{24,16},{28,20},{1,9},{5... | collective-permute-start | bytes 2211848 | tf_op jit(solution)/shard_map/gather_weights/ppermute | solution.py:331
  58.0 34.0 %collective-permute-start.21 = (bf16[384,768]{1,0:T(8,128)(2,1)}, bf16[384,768]{1,0:T(8,128)(2,1)S(1)}, u32[]{:S(2)}, u32[]{:S(2)}) collective-permute-start(bf16[384,768]{1,0:T(8,128)(2,1)} %collective-permute-done.16.rest_1_), channel_id=1, source_target_pairs={{0,16},{4,20},{8,24},{12,28},{16,0},{20,4},{24,8},{28,12},{1,17},{... | collective-permute-start | bytes 1769480 | tf_op jit(solution)/shard_map/gather_weights/ppermute | solution.py:331
  58.5 35.1 %collective-permute-start.24 = (bf16[480,768]{1,0:T(8,128)(2,1)S(1)}, bf16[480,768]{1,0:T(8,128)(2,1)S(1)}, u32[]{:S(2)}, u32[]{:S(2)}) collective-permute-start(bf16[480,768]{1,0:T(8,128)(2,1)S(1)} %bitcast_dynamic-update-slice_fusion.rest_8_.rest_0_), channel_id=1, source_target_pairs={{0,4},{4,0},{8,12},{12,8},{16,20},{20,16},{24,28},{28,24},{1,5},{5... | collective-permute-start | bytes 2211848 | tf_op jit(solution)/shard_map/gather_weights/ppermute | solution.py:331
  66.0 27.1 %collective-permute-start.18 = (bf16[384,768]{1,0:T(8,128)(2,1)}, bf16[384,768]{1,0:T(8,128)(2,1)}, u32[]{:S(2)}, u32[]{:S(2)}) collective-permute-start(bf16[384,768]{1,0:T(8,128)(2,1)} %bitcast.4.rest_0_), channel_id=1, source_target_pairs={{0,4},{4,0},{8,12},{12,8},{16,20},{20,16},{24,28},{28,24},{1,5},{5... | collective-permute-start | bytes 1769480 | tf_op jit(solution)/shard_map/gather_weights/ppermute | solution.py:331
  66.8 26.6 %collective-permute-start.19 = (bf16[384,768]{1,0:T(8,128)(2,1)}, bf16[384,768]{1,0:T(8,128)(2,1)S(1)}, u32[]{:S(2)}, u32[]{:S(2)}) collective-permute-start(bf16[384,768]{1,0:T(8,128)(2,1)} %collective-permute-done.16.rest_1_), channel_id=1, source_target_pairs={{0,4},{4,0},{8,12},{12,8},{16,20},{20,16},{24,28},{28,24},{1,5},{5... | collective-permute-start | bytes 1769480 | tf_op jit(solution)/shard_map/gather_weights/ppermute | solution.py:331
  187.7 172.0 %all-reduce.2.cloned.1.call-start = ((), (), s32[]{:S(2)}) async-start(), calls=%async_computation.2 | async-start | bytes 2654208 | tf_op jit(solution)/shard_map/psum | solution.py:997
  247.1 16.5 %collective-permute-start.28 = (bf16[4,288,768]{2,1,0:T(8,128)(2,1)}, bf16[4,288,768]{2,1,0:T(8,128)(2,1)}, u32[]{:S(2)}, u32[]{:S(2)}) collective-permute-start(bf16[4,288,768]{2,1,0:T(8,128)(2,1)} %get-tuple-element.93), channel_id=1, source_target_pairs={{0,4},{4,0},{8,12},{12,8},{16,20},{20,16},{24,28},{28,24},{1,5},{5... | collective-permute-start | bytes 5308424 | tf_op jit(solution)/shard_map/ppermute | solution.py:331
  266.5 32.0 %collective-permute-start.31 = (bf16[288,768]{1,0:T(8,128)(2,1)}, bf16[288,768]{1,0:T(8,128)(2,1)S(1)}, u32[]{:S(2)}, u32[]{:S(2)}) collective-permute-start(bf16[288,768]{1,0:T(8,128)(2,1)} %get-tuple-element.124), channel_id=1, source_target_pairs={{0,24},{4,28},{8,16},{12,20},{16,8},{20,12},{24,0},{28,4},{1,25},{... | collective-permute-start | bytes 1327112 | tf_op jit(solution)/shard_map/ppermute | solution.py:331
  272.8 25.6 %collective-permute-start.30 = (bf16[288,768]{1,0:T(8,128)(2,1)}, bf16[288,768]{1,0:T(8,128)(2,1)}, u32[]{:S(2)}, u32[]{:S(2)}) collective-permute-start(bf16[288,768]{1,0:T(8,128)(2,1)} %get-tuple-element.125), channel_id=1, source_target_pairs={{0,16},{4,20},{8,24},{12,28},{16,0},{20,4},{24,8},{28,12},{1,17},{... | collective-permute-start | bytes 1327112 | tf_op jit(solution)/shard_map/ppermute | solution.py:331
  272.8 25.6 %collective-permute-start.29 = (bf16[288,768]{1,0:T(8,128)(2,1)S(1)}, bf16[288,768]{1,0:T(8,128)(2,1)}, u32[]{:S(2)}, u32[]{:S(2)}) collective-permute-start(bf16[288,768]{1,0:T(8,128)(2,1)S(1)} %get-tuple-element.126), channel_id=1, source_target_pairs={{0,8},{4,12},{8,0},{12,4},{16,24},{20,28},{24,16},{28,20},{1,9},{5... | collective-permute-start | bytes 1327112 | tf_op jit(solution)/shard_map/ppermute | solution.py:331
  313.1 18.1 %collective-permute-start.39 = (bf16[72,768]{1,0:T(8,128)(2,1)S(1)}, bf16[72,768]{1,0:T(8,128)(2,1)S(1)}, u32[]{:S(2)}, u32[]{:S(2)}) collective-permute-start(bf16[72,768]{1,0:T(8,128)(2,1)S(1)} %get-tuple-element.129), channel_id=1, source_target_pairs={{0,3},{1,0},{2,1},{3,2},{4,7},{5,4},{6,5},{7,6},{8,11},{9,8},{10,9... | collective-permute-start | bytes 331784 | tf_op jit(solution)/shard_map/ppermute | solution.py:373
  315.7 15.5 %collective-permute-start.38 = (bf16[72,768]{1,0:T(8,128)(2,1)S(1)}, bf16[72,768]{1,0:T(8,128)(2,1)S(1)}, u32[]{:S(2)}, u32[]{:S(2)}) collective-permute-start(bf16[72,768]{1,0:T(8,128)(2,1)S(1)} %get-tuple-element.130), channel_id=1, source_target_pairs={{0,1},{1,2},{2,3},{3,0},{4,5},{5,6},{6,7},{7,4},{8,9},{9,10},{10,1... | collective-permute-start | bytes 331784 | tf_op jit(solution)/shard_map/ppermute | solution.py:373
  315.7 15.5 %collective-permute-start.37 = (bf16[72,768]{1,0:T(8,128)(2,1)S(1)}, bf16[72,768]{1,0:T(8,128)(2,1)S(1)}, u32[]{:S(2)}, u32[]{:S(2)}) collective-permute-start(bf16[72,768]{1,0:T(8,128)(2,1)S(1)} %get-tuple-element.131), channel_id=1, source_target_pairs={{0,2},{1,3},{2,0},{3,1},{4,6},{5,7},{6,4},{7,5},{8,10},{9,11},{10,... | collective-permute-start | bytes 331784 | tf_op jit(solution)/shard_map/ppermute | solution.py:373
  324.0 7.1 %collective-permute-start.35 = (f32[8,768]{1,0:T(8,128)S(1)}, f32[8,768]{1,0:T(8,128)S(1)}, u32[]{:S(2)}, u32[]{:S(2)}) collective-permute-start(f32[8,768]{1,0:T(8,128)S(1)} %add.199), channel_id=1, source_target_pairs={{0,1},{1,0},{2,3},{3,2},{4,5},{5,4},{6,7},{7,6},{8,9},{9,8},{10,11... | collective-permute-start | bytes 73736 | tf_op jit(solution)/shard_map/ppermute | solution.py:1013
  331.2 8.7 %collective-permute-start.36 = (f32[8,768]{1,0:T(8,128)S(1)}, f32[8,768]{1,0:T(8,128)S(1)}, u32[]{:S(2)}, u32[]{:S(2)}) collective-permute-start(f32[8,768]{1,0:T(8,128)S(1)} %add.200), channel_id=1, source_target_pairs={{0,2},{1,3},{2,0},{3,1},{4,6},{5,7},{6,4},{7,5},{8,10},{9,11},{10,... | collective-permute-start | bytes 73736 | tf_op jit(solution)/shard_map/ppermute | solution.py:1013
  331.3 17.9 %collective-permute-start.41 = (bf16[72,768]{1,0:T(8,128)(2,1)S(1)}, bf16[72,768]{1,0:T(8,128)(2,1)S(1)}, u32[]{:S(2)}, u32[]{:S(2)}) collective-permute-start(bf16[72,768]{1,0:T(8,128)(2,1)S(1)} %get-tuple-element.123), channel_id=1, source_target_pairs={{0,2},{1,3},{2,0},{3,1},{4,6},{5,7},{6,4},{7,5},{8,10},{9,11},{10,... | collective-permute-start | bytes 331784 | tf_op jit(solution)/shard_map/ppermute | solution.py:373
  334.3 12.1 %collective-permute-start.40 = (bf16[72,768]{1,0:T(8,128)(2,1)S(1)}, bf16[72,768]{1,0:T(8,128)(2,1)S(1)}, u32[]{:S(2)}, u32[]{:S(2)}) collective-permute-start(bf16[72,768]{1,0:T(8,128)(2,1)S(1)} %get-tuple-element.123), channel_id=1, source_target_pairs={{0,1},{1,2},{2,3},{3,0},{4,5},{5,6},{6,7},{7,4},{8,9},{9,10},{10,1... | collective-permute-start | bytes 331784 | tf_op jit(solution)/shard_map/ppermute | solution.py:373
  335.3 14.0 %collective-permute-start.42 = (bf16[72,768]{1,0:T(8,128)(2,1)S(1)}, bf16[72,768]{1,0:T(8,128)(2,1)S(1)}, u32[]{:S(2)}, u32[]{:S(2)}) collective-permute-start(bf16[72,768]{1,0:T(8,128)(2,1)S(1)} %get-tuple-element.123), channel_id=1, source_target_pairs={{0,3},{1,0},{2,1},{3,2},{4,7},{5,4},{6,5},{7,6},{8,11},{9,8},{10,9... | collective-permute-start | bytes 331784 | tf_op jit(solution)/shard_map/ppermute | solution.py:373
  (55 other events, 299.6 us)
Sparse Core Ops, SparseCore 0:
  187.9 84.5 reduce-scatter.1
  286.7 72.9 all-reduce.1

commit v3 on v2

--- a/solution.py
+++ b/solution.py
@@ -107,9 +107,8 @@
     lax.fori_loop(0, tab[base + 32], job, 0)
 
 
-def attend_kernel(pairs, row0, tab, q_ref, k_ref, v_ref, *rest):
-    o_ref, a_sc = rest[-2:]
-    base = (pl.program_id(0) + row0) * STRIDE
+def attend_kernel(pairs, tab, q_ref, k_ref, v_ref, o_ref, a_sc):
+    base = pl.program_id(0) * STRIDE
     o_ref[...] = jnp.zeros_like(o_ref)
 
     def work(qs, ks, qin, inside):
@@ -141,8 +140,9 @@
     def wide(i, carry):
         q0 = pl.multiple_of(jnp.minimum(low + i * QW, ROW_LEN - QW), 16)
         qin = slot_of(QW, q0) >= start
-        for p in range(pairs):
-            cs = pl.ds(128 * p, 128)
+
+        def pair(p, none):
+            cs = pl.ds(pl.multiple_of(128 * p, 128), 128)
             q = q_ref[pl.ds(q0, QW), cs]
             for par in range(2):
                 qs = query_side(q, par)
@@ -172,14 +172,17 @@
                 lax.fori_loop(0, ROW_LEN // KB, take_out, 0)
                 hit = qin & half_lanes(QW, par)
                 o_ref[pl.ds(q0, QW), cs] = jnp.where(hit, a_sc[...].T.astype(BF), o_ref[pl.ds(q0, QW), cs])
+            return none
+
+        lax.fori_loop(0, pairs, pair, 0)
         return carry
 
     lax.fori_loop(0, tab[base + 34], wide, 0)
 
 
-def attend_back_kernel(pairs, row0, tab, q_ref, k_ref, v_ref, d_ref, *rest):
+def attend_back_kernel(pairs, tab, q_ref, k_ref, v_ref, d_ref, *rest):
     dq_ref, dk_ref, dv_ref, a_sc, dk_sc, dv_sc = rest[-6:]
-    base = (pl.program_id(0) + row0) * STRIDE
+    base = pl.program_id(0) * STRIDE
     dq_ref[...] = jnp.zeros_like(dq_ref)
     dk_ref[...] = jnp.zeros_like(dk_ref)
     dv_ref[...] = jnp.zeros_like(dv_ref)
@@ -224,8 +227,9 @@
     start = tab[base + 33]
     low = lax.div(start, 16) * 16
     windows = tab[base + 34]
-    for p in range(pairs):
-        cs = pl.ds(128 * p, 128)
+
+    def pair(p, none):
+        cs = pl.ds(pl.multiple_of(128 * p, 128), 128)
 
         @pl.when(windows > 0)
         def _():
@@ -291,40 +295,39 @@
             dk_ref[:, cs] = jnp.where(kin, (dk_sc[...] * 0.125).astype(BF), dk_ref[:, cs])
             dv_ref[:, cs] = jnp.where(kin, dv_sc[...].astype(BF), dv_ref[:, cs])
 
-
-def row_call(kernel, name, outs, scratch, qkv, extra, table, row, half, halves, before, flops, moved):
+        return none
+
+    lax.fori_loop(0, jnp.where(windows > 0, pairs, 0), pair, 0)
+
+
+def attention_call(kernel, name, outs, scratch, qkv, extra, table, rows, flops, moved):
     n = qkv.shape[0]
     width = qkv.shape[1] // 3
-    w = width // halves
-    spec = lambda part: pl.BlockSpec((ROW_LEN, w), lambda r, t: (row, part * halves + half))
-    before = [] if before is None else list(before)
+    spec = lambda part: pl.BlockSpec((ROW_LEN, width), lambda r, t: (r, part))
     return pl.pallas_call(
-        partial(kernel, w // 128, row),
+        partial(kernel, width // 128),
         out_shape=[jax.ShapeDtypeStruct((n, width), BF)] * outs,
         grid_spec=pltpu.PrefetchScalarGridSpec(
             num_scalar_prefetch=1,
-            grid=(1,),
-            in_specs=[spec(0), spec(1), spec(2)]
-            + [spec(0)] * len(extra)
-            + [pl.BlockSpec(memory_space=pl.ANY)] * len(before),
+            grid=(rows,),
+            in_specs=[spec(0), spec(1), spec(2)] + [spec(0)] * len(extra),
             out_specs=[spec(0)] * outs,
             scratch_shapes=scratch,
         ),
-        input_output_aliases={4 + len(extra) + i: i for i in range(len(before))},
-        compiler_params=pltpu.CompilerParams(vmem_limit_bytes=GRANT),
-        cost_estimate=cost(flops / halves, moved * ROW_LEN * w),
+        compiler_params=pltpu.CompilerParams(vmem_limit_bytes=VMEM_LIMIT),
+        cost_estimate=cost(rows * flops, rows * moved * ROW_LEN * width),
         name=name,
-    )(table, qkv, qkv, qkv, *extra, *before)
-
-
-def attention_forward(qkv, table, row, before):
+    )(table, qkv, qkv, qkv, *extra)
+
+
+def attention_forward(qkv, table, rows):
     scratch = [pltpu.VMEM((128, QW), F32)]
-    return row_call(attend_kernel, "attend", 1, scratch, qkv, [], table, row, 0, 1, before, 12e9, 8)
-
-
-def attention_backward(qkv, da, table, row, half, halves, before):
+    return attention_call(attend_kernel, "attend", 1, scratch, qkv, [], table, rows, 12e9, 8)[0]
+
+
+def attention_backward(qkv, da, table, rows):
     scratch = [pltpu.VMEM((128, QW), F32), pltpu.VMEM((ROW_LEN, 128), F32), pltpu.VMEM((ROW_LEN, 128), F32)]
-    return row_call(attend_back_kernel, "attend_back", 3, scratch, qkv, [da], table, row, half, halves, before, 24e9, 14)
+    return attention_call(attend_back_kernel, "attend_back", 3, scratch, qkv, [da], table, rows, 24e9, 14)
 
 
 def hop(value, bit, size):
@@ -333,7 +336,8 @@
 
 def gather_cross(first, second):
     first_x, second_y = hop(first, 2, 8), hop(second, 4, 8)
-    first_y, second_x = hop(first, 4, 8), hop(second, 2, 8)
+    first_late, second_late = after((first, second), hop(second[:16], 1, 8))
+    first_y, second_x = hop(first_late, 4, 8), hop(second_late, 2, 8)
     return (first, first_x, first_y), (second, second_x, second_y)
 
 
@@ -359,8 +363,7 @@
         self.even = even
         self.core = hop(odd, 1, 8)
 
-    def send(self, done):
-        self.core = after(self.core, done)
+    def send(self):
         self.out = [total(self.even[q], self.core[q]) for q in (1, 2, 3)]
         return self.out
 
@@ -369,17 +372,24 @@
         return total(self.even[0], self.core[0], *come)
 
 
-def direct_sum(block, done):
-    shift = lambda value, by: lax.ppermute(value, "rep", [(i, (i + by) % 4) for i in range(4)])
+def shift(value, by):
+    return lax.ppermute(value, "rep", [(i, (i + by) % 4) for i in range(4)])
+
+
+def quarter_sum(block, done):
     z = lax.axis_index("rep")
     quarters = block.reshape(4, block.shape[0] // 4, block.shape[1])
     pick = lambda by: lax.dynamic_index_in_dim(quarters, lax.rem(z + by, 4), 0, False)
-    mine = total(pick(0), *after([shift(pick(by), by) for by in (2, 1, 3)], done))
+    return total(pick(0), *after([shift(pick(by), by) for by in (2, 1, 3)], done))
+
+
+def all_quarters(mine):
+    z = lax.axis_index("rep")
     parts = [mine] + [shift(mine, by) for by in (1, 2, 3)]
-    out = jnp.zeros(quarters.shape, F32)
+    out = jnp.zeros((4, *mine.shape), F32)
     for by, part in enumerate(parts):
         out = lax.dynamic_update_index_in_dim(out, part.astype(F32), lax.rem(z - by + 4, 4), 0)
-    return out.reshape(block.shape)
+    return out.reshape(4 * mine.shape[0], mine.shape[1])
 
 
 class Weight:
@@ -434,14 +444,18 @@
             c.wait()
         placed = sum(n_sc[i].astype(F32) for i in range(len(norm_copies)))
         nrm_ref[...] = placed[:8, :]
-        for c in copies:
-            c.wait()
 
     tb, width = x_ref.shape
     parts = [pl.ds(i, tb // 2) for i in range(0, tb, tb // 2)]
     for p in parts:
         unit, _ = norm_stats(x_ref[p, :].astype(F32))
         h_ref[p, :] = (unit * nrm_ref[0:1, :] + nrm_ref[1:2, :]).astype(BF)
+
+    @pl.when(pl.program_id(0) == 0)
+    def _():
+        for c in weight.copies(w_refs, w_sc, sems, me):
+            c.wait()
+
     for p in parts:
         qkv_ref[p, :] = mm(h_ref[p, :], w_sc[...], NT).astype(BF)
 
@@ -481,7 +495,7 @@
 
 
 def project_grad_kernel(size, tab, dq_ref, dk_ref, dv_ref, h_ref, *rest):
-    out_refs, acc = rest[:-1], rest[-1]
+    acc = rest[-1]
     t = pl.program_id(0)
     width = h_ref.shape[1]
 
@@ -495,30 +509,34 @@
     @pl.when(t == pl.num_programs(0) - 1)
     def _():
         if size == 8:
-            by_owner(acc, acc.shape[0] // 8, *out_refs, tab[tab.shape[0] - 1])
+            per = acc.shape[0] // 8
+            by_owner(acc, per, *(ref.at[:, pl.ds(0, per), :] for ref in rest[2:4]), tab[tab.shape[0] - 1])
+            for src, dst in zip(rest[0:2], rest[2:4]):
+                dst[:, pl.ds(per, src.shape[1]), :] = src[...]
         else:
-            out_refs[0][...] = acc[...].astype(BF)
-
-
-def project_grad(table, dq, dk, dv, h, size, tb=512):
+            rest[0][...] = acc[...].astype(BF)
+
+
+def project_grad(table, dq, dk, dv, h, proj, size, tb=512):
     n, width = h.shape
     rows = 3 * width
     block = pl.BlockSpec((tb, width), lambda t, tab: (t, 0))
-    shapes = [(4, rows // 8, width)] * 2 if size == 8 else [(rows, width)]
+    whole = lambda s: pl.BlockSpec(s, lambda t, tab, k=len(s): (0,) * k)
+    shapes = [(4, rows // 8 + proj[0].shape[1], width)] * 2 if size == 8 else [(rows, width)]
     return pl.pallas_call(
         partial(project_grad_kernel, size),
         out_shape=[jax.ShapeDtypeStruct(s, BF) for s in shapes],
         grid_spec=pltpu.PrefetchScalarGridSpec(
             num_scalar_prefetch=1,
             grid=(n // tb,),
-            in_specs=[block] * 4,
-            out_specs=[pl.BlockSpec(s, lambda t, tab, k=len(s): (0,) * k) for s in shapes],
+            in_specs=[block] * 4 + [whole(p.shape) for p in proj],
+            out_specs=[whole(s) for s in shapes],
             scratch_shapes=[pltpu.VMEM((rows, width), F32)],
         ),
         compiler_params=pltpu.CompilerParams(vmem_limit_bytes=VMEM_LIMIT),
         cost_estimate=cost(6 * n * width * width, n * width * 8 + 6 * width * width),
         name="project_grad",
-    )(table, dq, dk, dv, h)
+    )(table, dq, dk, dv, h, *proj)
 
 
 def project_back_kernel(weight, count, tab, nrm_ref, dq_ref, dk_ref, dv_ref, x_ref, dx_ref, *rest):
@@ -553,29 +571,26 @@
     gn_ref[1:2, :] += dshift
 
 
-def project_back(table, norms, dq, dk, dv, x, dx, weight, row, before, tb=512):
+def project_back(table, norms, dq, dk, dv, x, dx, weight, tb=256):
     n, width = x.shape
     count = len(weight.arrays)
     anywhere = pl.BlockSpec(memory_space=pl.ANY)
-    per = ROW_LEN // tb
-    block = pl.BlockSpec((tb, width), lambda t, tab: (row * per + t, 0))
+    block = pl.BlockSpec((tb, width), lambda t, tab: (t, 0))
     fixed = pl.BlockSpec((8, width), lambda t, tab: (0, 0))
-    before = [] if before is None else [before]
     return pl.pallas_call(
         partial(project_back_kernel, weight, count),
         out_shape=[jax.ShapeDtypeStruct((n, width), BF), jax.ShapeDtypeStruct((8, width), F32)],
         grid_spec=pltpu.PrefetchScalarGridSpec(
             num_scalar_prefetch=1,
-            grid=(per,),
-            in_specs=[fixed] + [block] * 5 + [anywhere] * (count + len(before)),
+            grid=(n // tb,),
+            in_specs=[fixed] + [block] * 5 + [anywhere] * count,
             out_specs=[block, fixed],
             scratch_shapes=[pltpu.VMEM((3 * width, width), BF), pltpu.SemaphoreType.DMA((count,))],
         ),
-        input_output_aliases={7 + count: 0} if before else {},
         compiler_params=pltpu.CompilerParams(vmem_limit_bytes=VMEM_LIMIT),
-        cost_estimate=cost(6 * ROW_LEN * width * width, ROW_LEN * width * 14 + 6 * width * width),
+        cost_estimate=cost(6 * n * width * width, n * width * 14 + 6 * width * width),
         name="project_back",
-    )(table, norms, dq, dk, dv, x, dx, *weight.arrays, *before)
+    )(table, norms, dq, dk, dv, x, dx, *weight.arrays)
 
 
 def gelu_both(values):
@@ -597,13 +612,11 @@
     ups, downs = len(w_up.arrays), len(w_down.arrays)
     up_refs, down_refs = rest[:ups], rest[ups : ups + downs]
     proj_refs = down_refs if size == 8 else rest[ups + downs : ups + downs + 1]
-    outs = 1 if size == 8 else 3
-    rest = rest[-(22 + outs) :]
-    x1_ref, act_ref, dx_ref, da_ref, gn_ref = rest[:5]
-    g_refs = rest[5 : 5 + outs]
-    x1_sc, h_sc, ht_sc, dy_sc, dyt_sc, dh_sc, gu_sc, gd_sc, wp_sc, wu_sc, wd_sc, su_sc, sd_sc, p_sem, u_sem, d_sem, g_sem = rest[
-        5 + outs :
-    ]
+    outs = 1 if size == 8 else 2
+    rest = rest[-(19 + outs) :]
+    x1_ref, act_ref, dh_ref = rest[:3]
+    g_refs = rest[3 : 3 + outs]
+    h_sc, ht_sc, dy_sc, dyt_sc, dh_sc, gu_sc, gd_sc, wp_sc, wu_sc, wd_sc, su_sc, sd_sc, p_sem, u_sem, d_sem, g_sem = rest[3 + outs :]
     j = pl.program_id(0)
     t = pl.program_id(1)
     steps = pl.num_programs(1)
@@ -638,17 +651,16 @@
             return [pltpu.make_async_copy(proj_refs[0], wp_sc, p_sem.at[0])]
         return down_copies(w_down, proj_refs, chunks, wp_sc, p_sem, me)
 
-    def packed_copies(block, up_pair=None):
+    def packed_copies(pair):
         fw, dw = w_up.per, w_down.per
-        whole = fw + (chunks + 1) * dw
+        whole = fw + chunks * dw
         out = []
         for d in range(8):
-            at = pl.multiple_of(d * whole + fw + block * dw, dw)
+            at = pl.multiple_of(d * whole + fw + pair * dw, dw)
             out.append(pltpu.make_async_copy(sd_sc.at[pl.ds(d * dw, dw), :], g_refs[0].at[pl.ds(at, dw), :], g_sem.at[d]))
-        if up_pair is not None:
-            for k in range(2):
-                at = pl.multiple_of((2 * up_pair + k) * whole, dw)
-                out.append(pltpu.make_async_copy(su_sc.at[k], g_refs[0].at[pl.ds(at, fw), :], g_sem.at[8 + k]))
+        for k in range(2):
+            at = pl.multiple_of((2 * pair + k) * whole, dw)
+            out.append(pltpu.make_async_copy(su_sc.at[k], g_refs[0].at[pl.ds(at, fw), :], g_sem.at[8 + k]))
         return out
 
     @pl.when((j == 0) & (t == 0))
@@ -675,7 +687,6 @@
         x1s = [x_ref[p, :].astype(F32) + mm(att_ref[p, :], wp_sc[...], NT) for p in pieces]
         dyt_sc[:, ts] = dy.T
         for p, full, x1 in zip(pieces, parts, x1s):
-            x1_sc[full, :] = x1
             x1_ref[p, :] = x1
             unit, _ = norm_stats(x1)
             h = (unit * gain + shift).astype(BF)
@@ -683,39 +694,40 @@
             ht_sc[:, full] = h.T
         dh_sc[ts, :] = jnp.zeros((tb, width), F32)
 
-    @pl.when((t == 0) & (j < chunks))
+    @pl.when(t == 0)
     def _():
         gu_sc[...] = jnp.zeros_like(gu_sc)
         gd_sc[...] = jnp.zeros_like(gd_sc)
 
-    @pl.when(j < chunks)
-    def _():
-        wu = wu_sc[lax.rem(j, 2)]
-        wd = wd_sc[lax.rem(j, 2)]
-        uppers = [mm(h_sc[p, :], wu, NT) for p in parts]
-        acts = []
-        dups = []
-        for p, upper in zip(parts, uppers):
-            dact = mm(dy_sc[p, :], wd, NN)
-            act, slope = gelu_both(upper)
-            acts.append(act.astype(BF))
-            dups.append((dact * slope).astype(BF))
-        for p, dup in zip(parts, dups):
-            dh_sc[p, :] += mm(dup, wu, NN)
-        act = jnp.concatenate(acts, axis=0)
-        act_ref[...] = act
-        gd_sc[...] += mm(dyt_sc[:, ts], act, NN)
-        gu_sc[...] += mm(ht_sc[:, ts], jnp.concatenate(dups, axis=0), NN)
-
-    @pl.when((t == steps - 1) & (j < chunks))
+    wu = wu_sc[lax.rem(j, 2)]
+    wd = wd_sc[lax.rem(j, 2)]
+    uppers = [mm(h_sc[p, :], wu, NT) for p in parts]
+    acts = []
+    dups = []
+    for p, upper in zip(parts, uppers):
+        dact = mm(dy_sc[p, :], wd, NN)
+        act, slope = gelu_both(upper)
+        acts.append(act.astype(BF))
+        dups.append((dact * slope).astype(BF))
+    for p, dup in zip(parts, dups):
+        dh_sc[p, :] += mm(dup, wu, NN)
+    act = jnp.concatenate(acts, axis=0)
+    act_ref[...] = act
+    gd_sc[...] += mm(dyt_sc[:, ts], act, NN)
+    gu_sc[...] += mm(ht_sc[:, ts], jnp.concatenate(dups, axis=0), NN)
+
+    @pl.when(j == chunks - 1)
+    def _():
+        dh_ref[...] = dh_sc[ts, :]
+
+    @pl.when(t == steps - 1)
     def _():
         if size == 8:
             pair = (me >> 1) ^ j
 
             @pl.when(j > 0)
             def _():
-                before = (me >> 1) ^ (j - 1)
-                for c in packed_copies(before, before):
+                for c in packed_copies((me >> 1) ^ (j - 1)):
                     c.wait()
 
             fw = w_up.per
@@ -723,98 +735,50 @@
                 for i in range(2):
                     su_sc[k, :, i * fw : (i + 1) * fw] = gu_sc[i * fw : (i + 1) * fw, k * fw : (k + 1) * fw].astype(BF)
             sd_sc[...] = gd_sc[...].astype(BF)
-            for c in packed_copies(pair, pair):
+            for c in packed_copies(pair):
                 c.start()
+
+            @pl.when(j == chunks - 1)
+            def _():
+                for c in packed_copies(pair):
+                    c.wait()
         else:
             g_refs[0][...] = gu_sc[...].astype(BF)
             g_refs[1][...] = gd_sc[...].astype(BF)
-
-    @pl.when(j == chunks)
-    def _():
-        @pl.when(t == 0)
-        def _():
-            gu_sc[...] = jnp.zeros_like(gu_sc)
-            gn_ref[...] = jnp.zeros_like(gn_ref)
-
-        dgain = jnp.zeros((1, width), F32)
-        dshift = jnp.zeros((1, width), F32)
-        dbs = []
-        for p, full in zip(pieces, parts):
-            unit, rate = norm_stats(x1_sc[full, :])
-            dh = dh_sc[full, :]
-            dx = dy_sc[full, :].astype(F32) + norm_back(unit, rate, gain, dh)
-            dx_ref[p, :] = dx
-            dbs.append(dx.astype(BF))
-            da_ref[p, :] = mm(dbs[-1], wp_sc[...], NN).astype(BF)
-            dgain += jnp.sum(dh * unit, axis=0, keepdims=True)
-            dshift += jnp.sum(dh, axis=0, keepdims=True)
-        gu_sc[...] += mm(jnp.concatenate(dbs, axis=0), att_ref[...], TN)
-        gn_ref[0:1, :] += dgain
-        gn_ref[1:2, :] += dshift
-
-        @pl.when(t == steps - 1)
-        def _():
-            if size == 8:
-                before = (me >> 1) ^ (chunks - 1)
-                for c in packed_copies(before, before):
-                    c.wait()
-                sd_sc[...] = gu_sc[...].astype(BF)
-                for c in packed_copies(chunks):
-                    c.start()
-                for c in packed_copies(chunks):
-                    c.wait()
-            else:
-                g_refs[2][...] = gu_sc[...].astype(BF)
 
 
 def middle(table, norms, att, x, cot, w_up, w_down, w_proj, hidden, size, tb=512, sub=256):
     n, width = x.shape
     chunks = hidden // width
     steps = n // tb
-    last = chunks - 1
     dev = table.shape[0] - 1
     first = lambda j, t, tab: (jnp.where(j == 0, t, steps - 1), 0)
-    ends = lambda j, t, tab: (jnp.where((j == 0) | (j == chunks), t, steps - 1), 0)
-    final = lambda j, t, tab: (jnp.where(j == chunks, t, 0), 0)
+    final = lambda j, t, tab: (jnp.where(j == chunks - 1, t, 0), 0)
     fixed = lambda j, t, tab: (0, 0)
     anywhere = pl.BlockSpec(memory_space=pl.ANY)
-    now = lambda j: jnp.minimum(j, last)
     sds = jax.ShapeDtypeStruct
     if size == 8:
         fw, dw = w_up.per, w_down.per
-        pair = lambda j, tab: lax.bitwise_xor(lax.shift_right_logical(tab[dev], 1), now(j))
         assert hidden == 8 * fw and width == 2 * fw == 8 * dw
-        g_shapes = [sds((8 * (fw + (chunks + 1) * dw), width), BF)]
+        pair = lambda j, tab: lax.bitwise_xor(lax.shift_right_logical(tab[dev], 1), j)
+        g_shapes = [sds((8 * (fw + chunks * dw), width), BF)]
         g_specs = [anywhere]
     else:
-        pair = lambda j, tab: now(j)
-        g_shapes = [sds((width, hidden), BF)] * 2 + [sds((width, width), BF)]
-        g_specs = [pl.BlockSpec((width, width), lambda j, t, tab: (0, now(j)))] * 2 + [
-            pl.BlockSpec((width, width), fixed)
-        ]
+        pair = lambda j, tab: j
+        g_shapes = [sds((width, hidden), BF)] * 2
+        g_specs = [pl.BlockSpec((width, width), lambda j, t, tab: (0, j))] * 2
     block = lambda index: pl.BlockSpec((tb, width), index)
-    acts = lambda j, t, tab: (jnp.where(j == chunks, steps - 1, t), pair(j, tab))
     weights = w_up.arrays + w_down.arrays + w_proj.arrays
     dma = pltpu.SemaphoreType.DMA
     return pl.pallas_call(
         partial(middle_kernel, size, tb, sub, chunks, w_up, w_down, w_proj),
-        out_shape=[
-            sds((n, width), F32),
-            sds((n, hidden), BF),
-            sds((n, width), F32),
-            sds((n, width), BF),
-            sds((8, width), F32),
-        ]
-        + g_shapes,
+        out_shape=[sds((n, width), F32), sds((n, hidden), BF), sds((n, width), F32)] + g_shapes,
         grid_spec=pltpu.PrefetchScalarGridSpec(
             num_scalar_prefetch=1,
-            grid=(chunks + 1, steps),
-            in_specs=[pl.BlockSpec((8, width), fixed), block(ends), block(first), block(first)]
-            + [anywhere] * len(weights),
-            out_specs=[block(first), block(acts), block(final), block(final), pl.BlockSpec((8, width), fixed)]
-            + g_specs,
+            grid=(chunks, steps),
+            in_specs=[pl.BlockSpec((8, width), fixed)] + [block(first)] * 3 + [anywhere] * len(weights),
+            out_specs=[block(first), block(lambda j, t, tab: (t, pair(j, tab))), block(final)] + g_specs,
             scratch_shapes=[
-                pltpu.VMEM((n, width), F32),
                 pltpu.VMEM((n, width), BF),
                 pltpu.VMEM((width, n), BF),
                 pltpu.VMEM((n, width), BF),
@@ -834,12 +798,88 @@
             ],
         ),
         compiler_params=pltpu.CompilerParams(vmem_limit_bytes=VMEM_LIMIT),
-        cost_estimate=cost(n * width * (10 * hidden + 6 * width), n * (width * 22 + 2 * hidden) + 8 * hidden * width),
+        cost_estimate=cost(n * width * (10 * hidden + 2 * width), n * (width * 22 + 2 * hidden) + 8 * hidden * width),
         name="middle",
     )(table, norms, att, x, cot, *weights)
 
 
-def finish_kernel(size, blocks, w_down, row, tab, x1_ref, act_ref, *rest):
+def attended_back_kernel(size, tb, sub, block, w_down, w_proj, tab, nrm_ref, x1_ref, dh_ref, cot_ref, att_ref, *rest):
+    count = len(w_down.arrays) if size == 8 else 1
+    w_refs = rest[:count]
+    dx_ref, da_ref, gn_ref, *g_refs, acc, wp_sc, sems = rest[count:]
+    t = pl.program_id(0)
+    me = tab[tab.shape[0] - 1]
+    per = ROW_LEN // tb
+    valid = tab[lax.div(t, per) * STRIDE + 33] - lax.rem(t, per) * tb
+    width = x1_ref.shape[1]
+
+    @pl.when(t == 0)
+    def _():
+        if size == 8:
+            copies = down_copies(w_down, w_refs, block, wp_sc, sems, me)
+        else:
+            copies = [pltpu.make_async_copy(w_refs[0], wp_sc, sems.at[0])]
+        for c in copies:
+            c.start()
+        acc[...] = jnp.zeros_like(acc)
+        gn_ref[...] = jnp.zeros_like(gn_ref)
+        for c in copies:
+            c.wait()
+
+    dgain = jnp.zeros((1, width), F32)
+    dshift = jnp.zeros((1, width), F32)
+    dbs = []
+    for i in range(0, tb, sub):
+        p = pl.ds(i, sub)
+        unit, rate = norm_stats(x1_ref[p, :])
+        dh = dh_ref[p, :]
+        ok = lax.broadcasted_iota(jnp.int32, (sub, 1), 0) + i < valid
+        dx = jnp.where(ok, cot_ref[p, :].astype(F32), 0.0) + norm_back(unit, rate, nrm_ref[2:3, :], dh)
+        dx_ref[p, :] = dx
+        dbs.append(dx.astype(BF))
+        da_ref[p, :] = mm(dbs[-1], wp_sc[...], NN).astype(BF)
+        dgain += jnp.sum(dh * unit, axis=0, keepdims=True)
+        dshift += jnp.sum(dh, axis=0, keepdims=True)
+    acc[...] += mm(jnp.concatenate(dbs, axis=0), att_ref[...], TN)
+    gn_ref[0:1, :] += dgain
+    gn_ref[1:2, :] += dshift
+
+    @pl.when(t == pl.num_programs(0) - 1)
+    def _():
+        if size == 8:
+            by_owner(acc, w_down.per, *g_refs, me)
+        else:
+            g_refs[0][...] = acc[...].astype(BF)
+
+
+def attended_back(table, norms, x1, dh, cot, att, w_down, w_proj, size, tb=256, sub=256):
+    n, width = x1.shape
+    weights = w_down.arrays if size == 8 else w_proj.arrays
+    block = pl.BlockSpec((tb, width), lambda t, tab: (t, 0))
+    fixed = pl.BlockSpec((8, width), lambda t, tab: (0, 0))
+    sds = jax.ShapeDtypeStruct
+    g_shapes = [(4, w_down.per, width)] * 2 if size == 8 else [(width, width)]
+    return pl.pallas_call(
+        partial(attended_back_kernel, size, tb, sub, 4, w_down, w_proj),
+        out_shape=[sds((n, width), F32), sds((n, width), BF), sds((8, width), F32)] + [sds(g, BF) for g in g_shapes],
+        grid_spec=pltpu.PrefetchScalarGridSpec(
+            num_scalar_prefetch=1,
+            grid=(n // tb,),
+            in_specs=[fixed] + [block] * 4 + [pl.BlockSpec(memory_space=pl.ANY)] * len(weights),
+            out_specs=[block, block, fixed] + [pl.BlockSpec(g, lambda t, tab, k=len(g): (0,) * k) for g in g_shapes],
+            scratch_shapes=[
+                pltpu.VMEM((width, width), F32),
+                pltpu.VMEM((width, width), BF),
+                pltpu.SemaphoreType.DMA((8,)),
+            ],
+        ),
+        compiler_params=pltpu.CompilerParams(vmem_limit_bytes=VMEM_LIMIT),
+        cost_estimate=cost(4 * n * width * width, n * width * 18),
+        name="attended_back",
+    )(table, norms, x1, dh, cot, att, *weights)
+
+
+def finish_kernel(size, blocks, w_down, tab, x1_ref, act_ref, *rest):
     w_refs = rest[: len(w_down.arrays)]
     out_ref, w_sc, sems = rest[-3:]
     t = pl.program_id(0)
@@ -862,33 +902,32 @@
                 c.wait()
 
     x2 = x1_ref[...] + mm(act_ref[...], w_sc[...], NT)
-    ok = (lax.broadcasted_iota(jnp.int32, (tb, 1), 0) + t * tb) < tab[row * STRIDE + 33]
+    per = ROW_LEN // tb
+    valid = tab[lax.div(t, per) * STRIDE + 33] - lax.rem(t, per) * tb
+    ok = lax.broadcasted_iota(jnp.int32, (tb, 1), 0) < valid
     out_ref[...] = jnp.where(ok, x2, 0.0).astype(BF)
 
 
-def finish(table, x1, act, w_down, row, before, size, tb=512):
+def finish(table, x1, act, w_down, size, tb=256):
     n, width = x1.shape
     hidden = act.shape[1]
     blocks = hidden // width
-    per = ROW_LEN // tb
-    before = [] if before is None else [before]
     count = len(w_down.arrays)
-    block = lambda w: pl.BlockSpec((tb, w), lambda t, tab: (row * per + t, 0))
+    block = lambda w: pl.BlockSpec((tb, w), lambda t, tab: (t, 0))
     return pl.pallas_call(
-        partial(finish_kernel, size, blocks, w_down, row),
+        partial(finish_kernel, size, blocks, w_down),
         out_shape=jax.ShapeDtypeStruct((n, width), BF),
         grid_spec=pltpu.PrefetchScalarGridSpec(
             num_scalar_prefetch=1,
-            grid=(per,),
-            in_specs=[block(width), block(hidden)] + [pl.BlockSpec(memory_space=pl.ANY)] * (count + len(before)),
+            grid=(n // tb,),
+            in_specs=[block(width), block(hidden)] + [pl.BlockSpec(memory_space=pl.ANY)] * count,
             out_specs=block(width),
             scratch_shapes=[pltpu.VMEM((width, hidden), BF), pltpu.SemaphoreType.DMA((blocks, 8))],
         ),
-        input_output_aliases={3 + count: 0} if before else {},
         compiler_params=pltpu.CompilerParams(vmem_limit_bytes=VMEM_LIMIT),
-        cost_estimate=cost(2 * ROW_LEN * width * hidden, ROW_LEN * (width * 6 + hidden * 2) + 2 * width * hidden),
+        cost_estimate=cost(2 * n * width * hidden, n * (width * 6 + hidden * 2) + 2 * width * hidden),
         name="finish",
-    )(table, x1, act, *w_down.arrays, *before)
+    )(table, x1, act, *w_down.arrays)
 
 
 def per_device(
@@ -949,82 +988,64 @@
     )
     stage, *targets = lax.optimization_barrier((table, *targets))
     h1, qkv, norms = project(stage, norm_parts, tokens, w_qkv)
-    attended = None
     stage = table
     if fast:
         with jax.named_scope("gather_weights"):
             up_x, down_y, up_t, packed = after((up_x, down_y, up_t, packed), qkv)
-            up_far, down_far = forward_cross((None, up_x), (None, None, down_y))
+            up_far, down_far = hop(up_x, 4, 8), hop(down_y, 2, 8)
             near = both_cores([up_t, up_x]), both_cores([packed])
             stage = after(table, up_x, down_y)
-    for row in range(rows):
-        attended = attention_forward(qkv, stage, row, attended)
-        if fast and row == 0:
-            with jax.named_scope("gather_weights"):
-                up_y, down_x, down_y = after((up_y, down_x, down_y), attended[0])
-                along = hop(up_y, 1, 8), hop(down_x, 1, 8), hop(down_y, 1, 8)
-                stage = after(table, up_y, down_x, down_y)
+    attended = attention_forward(qkv, stage, rows)
     if fast:
         with jax.named_scope("gather_weights"):
-            up_far, down_far = after((up_far, down_far), attended[0])
+            up_y, down_x, down_y, up_far, down_far = after((up_y, down_x, down_y, up_far, down_far), attended)
+            along = hop(up_y, 1, 8), hop(down_x, 1, 8), hop(down_y, 1, 8)
             ups = near[0] + [(up_y, 4), (along[0], 5), (up_far, 6), (hop(up_far, 1, 8), 7)]
             downs = near[1] + [(down_x, 2), (along[1], 3), (down_y, 4), (along[2], 5)]
             downs += [(down_far, 6), (hop(down_far, 1, 8), 7)]
             w_up = Weight([(a, s, 0) for a, s in ups], up_t.shape[0])
             w_down = Weight([(a, s, 0) for a, s in downs], own)
             w_proj = Weight([], own)
-    x1, act, grad_middle, grad_attended, grad_norm2, *grads = middle(
-        table, norms, attended[0], tokens, cotangent, w_up, w_down, w_proj, hidden, size
+    x1, act, grad_second, *grads = middle(
+        table, norms, attended, tokens, cotangent, w_up, w_down, w_proj, hidden, size
     )
-
-    dqkv = None
-    input_grad = None
-    block_output = None
-    norm_grads = []
+    grad_middle, grad_attended, grad_norm2, *grad_proj = attended_back(
+        table, norms, x1, grad_second, cotangent, attended, w_down, w_proj, size
+    )
+
     after_table = lambda *values: after(table, *values)
     if fast:
         packed_own = lax.psum_scatter(grads[0], "fsdp", scatter_dimension=0, tiled=True)
-    for row in range(rows):
-        dqkv = attention_backward(qkv, grad_attended, table, row, 0, 1, dqkv)
+    dqkv = attention_backward(qkv, grad_attended, table, rows)
     if fast:
-        grad_qkv = project_grad(table, *dqkv, h1, size)
+        grad_qkv = project_grad(table, *dqkv, h1, grad_proj, size)
         qkv_sum = Scatter(*grad_qkv)
-        block_output = finish(after_table(grad_qkv[0]), x1, act, w_down, 0, None, size)
-        stage = after_table(*qkv_sum.send(block_output))
-        for row in range(1, rows):
-            block_output = finish(stage, x1, act, w_down, row, block_output, size)
-        packed_own = after(packed_own, block_output)
+        fw = hidden // 8
+        packed_own = after(packed_own, grad_qkv[0])
         packed_sum = lax.psum(packed_own, "rep")
-        stage = after_table(packed_own)
-        input_grad, part = project_back(stage, norms, *dqkv, tokens, grad_middle, w_qkv, 0, None)
-        norm_grads.append(part)
-        qkv_own = qkv_sum.block(part)
-        stage = after_table(qkv_own)
-        for row in range(1, rows):
-            input_grad, part = project_back(stage, norms, *dqkv, tokens, grad_middle, w_qkv, row, input_grad)
-            norm_grads.append(part)
-        qkv_own = direct_sum(qkv_own, part)
-        norm_sum = jnp.concatenate(
-            [sum(p[:2] for p in norm_grads), grad_norm2[:2], jnp.zeros((4, width), F32)], axis=0
-        )
+        stage = after_table(packed_own, *qkv_sum.send())
+        block_output = finish(stage, x1, act, w_down, size)
+        qkv_own = qkv_sum.block(block_output)
+        input_grad, grad_norm1 = project_back(after_table(qkv_own), norms, *dqkv, tokens, grad_middle, w_qkv)
+        norm_sum = jnp.concatenate([grad_norm1[:2], grad_norm2[:2], jnp.zeros((4, width), F32)], axis=0)
+        quarter = quarter_sum(qkv_own, grad_norm1)
+        quarter = after(quarter, packed_sum)
         for bit in (1, 2, 4):
             norm_sum = norm_sum + hop(norm_sum, bit, 8)
         for bit in (1, 2):
             norm_sum = norm_sum + lax.ppermute(norm_sum, "rep", [(i, i ^ bit) for i in range(4)])
+        qkv_own = all_quarters(quarter)
         packed_sum = packed_sum.astype(F32)
-        fw = hidden // 8
         up = jnp.concatenate([packed_sum[:fw, :fw], packed_sum[:fw, fw:]], axis=0)
-        down = packed_sum[fw : fw + blocks * own].reshape(blocks, own, width).transpose(1, 0, 2).reshape(own, hidden)
-        proj = packed_sum[fw + blocks * own :]
+        down = packed_sum[fw:].reshape(blocks, own, width).transpose(1, 0, 2).reshape(own, hidden)
+        qkv_own, proj = qkv_own[: 3 * own], qkv_own[3 * own :]
     else:
-        grad_qkv = project_grad(table, *dqkv, h1, size)
-        for row in range(rows):
-            input_grad, part = project_back(table, norms, *dqkv, tokens, grad_middle, w_qkv, row, input_grad)
-            norm_grads.append(part)
-            block_output = finish(table, x1, act, w_down, row, block_output, size)
+        grad_qkv = project_grad(table, *dqkv, h1, [], size)
+        input_grad, grad_norm1 = project_back(table, norms, *dqkv, tokens, grad_middle, w_qkv)
+        block_output = finish(table, x1, act, w_down, size)
         sums = lambda g, dim: lax.psum(lax.psum_scatter(g, "fsdp", scatter_dimension=dim, tiled=True), "rep").astype(F32)
-        up, down, proj, qkv_own = sums(grads[0], 1), sums(grads[1], 0), sums(grads[2], 0), sums(grad_qkv[0], 0)
-        norm_sum = jnp.concatenate([sum(p[:2] for p in norm_grads), grad_norm2[:2]], axis=0)
+        up, down, proj, qkv_own = sums(grads[0], 1), sums(grads[1], 0), sums(grad_proj[0], 0), sums(grad_qkv[0], 0)
+        norm_sum = jnp.concatenate([grad_norm1[:2], grad_norm2[:2]], axis=0)
         norm_sum = lax.psum(norm_sum, ("fsdp", "rep"))
     norm_grad = lax.dynamic_slice(norm_sum, (0, me * own), (4, own))
     return (block_output, input_grad, norm_grad, qkv_own.T, proj.T, up, down.T, *targets)

time: 378 us -> 361 us (0.955); the launches traced: 372 us -> 359 us
  local copies, waits for them, and re-layouts: 29.5 us -> 15.3 us
    pallas_call x6 -> x4, Pallas kernels: 80.3 us -> 95.8 us  [the longest x2 57.3 us: attention_call(): pl.pallas_call(partial(kernel, width // 128), out_shape=[jax.ShapeDtypeSt...]
    unnamed x89 -> x57, local copies, waits for them, and re-layouts: 21.7 us -> 6.42 us
    ppermute x35, waiting for transfers between devices: 23.3 us -> 35.6 us  [hop(): return lax.ppermute(value, 'fsdp', [(i, i ^ bit) for i in range(size)])]
    pallas_call x1, Pallas kernels: 86.6 us -> 75.6 us  [middle(): pl.pallas_call(partial(middle_kernel, size, tb, sub, chunks, w_up, w_down...]
    psum x1, waiting for transfers between devices: 10.4 us -> 0.02 us  [per_device(): packed_sum = lax.psum(packed_own, 'rep')]
    pallas_call x2 -> x1, Pallas kernels: 23.8 us -> 18 us  [project_back(): pl.pallas_call(partial(project_back_kernel, weight, count), out_shape=[ja...]
    ppermute x6, waiting for transfers between devices: 8.67 us -> 3.85 us  [shift(): return lax.ppermute(value, 'rep', [(i, (i + by) % 4) for i in range(4)])]
    ppermute x35, starting transfers between devices: 29.9 us -> 33.9 us  [hop(): return lax.ppermute(value, 'fsdp', [(i, i ^ bit) for i in range(size)])]
  transfers between devices with their start and end apart: 45 -> 45, of which waited for: 12 -> 15; matrix products, arithmetic and copies ran while one was open for 6% -> 6% of each run, Pallas kernels for 36% -> 40%
where the time goes in v3:
time: 361 us; the launch traced here: 359 us
  Pallas kernels  220 us (61%)
  waiting for transfers between devices  48.6 us (13%)
  starting transfers between devices  44.6 us (12%)
  other arithmetic  16.3 us (5%)
  local copies, waits for them, and re-layouts  15.3 us (4%)
  between operations  14.6 us (4%)
    pallas_call x1, Pallas kernels, middle(): pl.pallas_call(partial(middle_kernel, size, tb, sub, chunks, w_up, w_down...  75.6 us
    pallas_call x2, Pallas kernels, attention_call(): pl.pallas_call(partial(kernel, width // 128), out_shape=[jax.ShapeDtypeSt...  57.3 us
    ppermute x35, waiting for transfers between devices, hop(): return lax.ppermute(value, 'fsdp', [(i, i ^ bit) for i in range(size)])  35.6 us
    ppermute x35, starting transfers between devices, hop(): return lax.ppermute(value, 'fsdp', [(i, i ^ bit) for i in range(size)])  33.9 us
    pallas_call x1, Pallas kernels, attended_back(): pl.pallas_call(partial(attended_back_kernel, size, tb, sub, 4, w_down, w_...  20 us
    pallas_call x1, Pallas kernels, finish(): pl.pallas_call(partial(finish_kernel, size, blocks, w_down), out_shape=ja...  18.6 us
    pallas_call x1, Pallas kernels, project_back(): pl.pallas_call(partial(project_back_kernel, weight, count), out_shape=[ja...  18 us
    pallas_call x1, Pallas kernels, project(): pl.pallas_call(partial(project_kernel, weight, count), out_shape=[sds((n,...  15.7 us
  transfers between devices with their start and end apart: 45, of which 15 were waited for; matrix products, arithmetic and copies ran while one was open for 6% of the time, Pallas kernels for 40%

profile of v3, /device:TPU:0, one launch (start us, length us, event | category | flops | bytes accessed | tf_op | source)
XLA Modules:
  0.0 359.3 jit_solution(9326729097682808271)
XLA Ops:
  8.4 1.6 dynamic_update_slice.16
  10.0 3.1 collective-permute-start
  15.4 2.2 multiply_add_fusion.2
  22.0 1.9 collective-permute-done.7.rest_9_
  24.6 1.8 collective-permute-start.2
  29.8 4.0 %collective-permute-done.9.rest_11_ = bf16[144,768]{1,0:T(8,128)(2,1)S(1)} collective-permute-done((bf16[144,768]{1,0:T(8,128)(2,1)}, bf16[144,768]{1,0:T(8,128)(2,1)S(1)}, u32[]{:S(2)}, u32[]{:S(2)}) %collective-permute-start.9) | collective-permute-done | bytes 221216 | tf_op jit(solution)/shard_map/gather_weights/ppermute | solution.py:334
  39.4 1.8 multiply_add_fusion.3
  42.0 15.7 %project.1 = (bf16[2048,768]{1,0:T(8,128)(2,1)}, bf16[2048,2304]{1,0:T(8,128)(2,1)}, f32[8,768]{1,0:T(8,128)}) custom-call(s32[71]{0:T(128)} %pad_add_fusion.tab, bf16[2048,768]{1,0:T(8,128)(2,1)} %x_ref.5, bf16[160,768]{1,0:T(8,128)(2,1)} %copy-done.5, bf16[160,768]{1,0:T(8,128)(2,1)} %collective-permute-done.rest_1_, ...), custom_call_target="tpu_custom_call" | custom-call | flops 144955152 | bytes 385351 | tf_op jit(solution)/shard_map/project/pallas_call | solution.py:469
  60.3 5.6 %collective-permute-done.18.rest_4_ = bf16[384,768]{1,0:T(8,128)(2,1)} collective-permute-done((bf16[384,768]{1,0:T(8,128)(2,1)}, bf16[384,768]{1,0:T(8,128)(2,1)}, u32[]{:S(2)}, u32[]{:S(2)}) %collective-permute-start.18) | collective-permute-done | bytes 589856 | tf_op jit(solution)/shard_map/gather_weights/ppermute | solution.py:334
  66.0 1.6 collective-permute-done.19.rest_10_.rest_2_
  67.6 21.0 %attend.1.att_ref = bf16[2048,768]{1,0:T(8,128)(2,1)} custom-call(s32[71]{0:T(128)} %pad_add_fusion.tab, bf16[2048,2304]{1,0:T(8,128)(2,1)} %get-tuple-element.69.q_ref.k_ref.v_ref, bf16[2048,2304]{1,0:T(8,128)(2,1)} %get-tuple-element.69.q_ref.k_ref.v_ref, bf16[2048,2304]{1,0:T(8,128)(2,1)} %get-tuple-element.69.q_ref.k_ref.v_ref), custom_call_target="tpu_custom_call" | custom-call | flops 480000000 | bytes 251658 | tf_op jit(solution)/shard_map/attend/pallas_call | solution.py:307
  90.7 4.9 %collective-permute-done.22.rest_5_ = bf16[384,768]{1,0:T(8,128)(2,1)} collective-permute-done((bf16[384,768]{1,0:T(8,128)(2,1)}, bf16[384,768]{1,0:T(8,128)(2,1)}, u32[]{:S(2)}, u32[]{:S(2)}) %collective-permute-start.22) | collective-permute-done | bytes 589856 | tf_op jit(solution)/shard_map/gather_weights/ppermute | solution.py:334
  96.5 75.6 %middle.1 = (f32[2048,768]{1,0:T(8,128)}, bf16[2048,3072]{1,0:T(8,128)(2,1)}, f32[2048,768]{1,0:T(8,128)}, bf16[6144,768]{1,0:T(8,128)(2,1)}) custom-call(s32[71]{0:T(128)} %pad_add_fusion.tab, f32[8,768]{1,0:T(8,128)} %get-tuple-element.66.nrm_ref, bf16[2048,768]{1,0:T(8,128)(2,1)} %attend.1.att_ref, bf16[2048,768]{1,0:T(8,128)(2,1)} %x_ref.5, ...), custom_call_target="tpu_custom_call" | custom-call | flops 1014686016 | bytes 1321205 | tf_op jit(solution)/shard_map/middle/pallas_call | solution.py:773
  172.2 20.0 %attended_back.1 = (f32[2048,768]{1,0:T(8,128)}, bf16[2048,768]{1,0:T(8,128)(2,1)}, f32[8,768]{1,0:T(8,128)}, bf16[4,96,768]{2,1,0:T(8,128)(2,1)}, bf16[4,96,768]{2,1,0:T(8,128)(2,1)}) custom-call(s32[71]{0:T(128)} %pad_add_fusion.tab, f32[8,768]{1,0:T(8,128)} %get-tuple-element.66.nrm_ref, f32[2048,768]{1,0:T(8,128)} %get-tuple-element.83.x1_ref, ...), custom_call_target="tpu_custom_call" | custom-call | flops 96636768 | bytes 566231 | tf_op jit(solution)/shard_map/attended_back/pallas_call | solution.py:862
  192.2 36.3 %attend_back.1 = (bf16[2048,768]{1,0:T(8,128)(2,1)}, bf16[2048,768]{1,0:T(8,128)(2,1)}, bf16[2048,768]{1,0:T(8,128)(2,1)}) custom-call(s32[71]{0:T(128)} %pad_add_fusion.tab, bf16[2048,2304]{1,0:T(8,128)(2,1)} %get-tuple-element.69.q_ref.k_ref.v_ref, bf16[2048,2304]{1,0:T(8,128)(2,1)} %get-tuple-element.69.q_ref.k_ref.v_ref, ...), custom_call_target="tpu_custom_call" | custom-call | flops 960000000 | bytes 440401 | tf_op jit(solution)/shard_map/attend_back/pallas_call | solution.py:307
  228.4 14.7 %project_grad.1 = (bf16[4,384,768]{2,1,0:T(8,128)(2,1)}, bf16[4,384,768]{2,1,0:T(8,128)(2,1)}) custom-call(s32[71]{0:T(128)} %pad_add_fusion.tab, bf16[2048,768]{1,0:T(8,128)(2,1)} %get-tuple-element.86.dq_ref, bf16[2048,768]{1,0:T(8,128)(2,1)} %get-tuple-element.87.dk_ref, bf16[2048,768]{1,0:T(8,128)(2,1)} %get-tuple-element.88.dv_ref, ...), custom_call_target="tpu_custom_call" | custom-call | flops 144955152 | bytes 322437 | tf_op jit(solution)/shard_map/project_grad/pallas_call | solution.py:526
  243.1 5.6 %collective-permute-start.28 = (bf16[4,384,768]{2,1,0:T(8,128)(2,1)}, bf16[4,384,768]{2,1,0:T(8,128)(2,1)S(1)}, u32[]{:S(2)}, u32[]{:S(2)}) collective-permute-start(bf16[4,384,768]{2,1,0:T(8,128)(2,1)} %get-tuple-element.94), channel_id=1, source_target_pairs={{0,4},{4,0},{8,12},{12,8},{16,20},{20,16},{24,28},{28,24},{1,5},{5... | collective-permute-start | bytes 7077896 | tf_op jit(solution)/shard_map/ppermute | solution.py:334
  248.7 4.4 %collective-permute-done.28 = bf16[4,384,768]{2,1,0:T(8,128)(2,1)S(1)} collective-permute-done((bf16[4,384,768]{2,1,0:T(8,128)(2,1)}, bf16[4,384,768]{2,1,0:T(8,128)(2,1)S(1)}, u32[]{:S(2)}, u32[]{:S(2)}) %collective-permute-start.28) | collective-permute-done | bytes 2359328 | tf_op jit(solution)/shard_map/ppermute | solution.py:334
  253.1 3.8 %fusion.5 = (bf16[384,768]{1,0:T(8,128)(2,1)}, bf16[384,768]{1,0:T(8,128)(2,1)}, bf16[384,768]{1,0:T(8,128)(2,1)}) fusion(bf16[4,384,768]{2,1,0:T(8,128)(2,1)S(1)} %collective-permute-done.28, bf16[4,384,768]{2,1,0:T(8,128)(2,1)} %get-tuple-element.92), kind=kLoop, calls=%fused_computation.13 | loop fusion | flops 3538944 | bytes 5308416 | tf_op jit(solution)/shard_map/convert_element_type | solution.py:358
  256.9 5.1 %collective-permute-start.29 = (bf16[384,768]{1,0:T(8,128)(2,1)}, bf16[384,768]{1,0:T(8,128)(2,1)}, u32[]{:S(2)}, u32[]{:S(2)}) collective-permute-start(bf16[384,768]{1,0:T(8,128)(2,1)} %get-tuple-element.118), channel_id=1, source_target_pairs={{0,8},{4,12},{8,0},{12,4},{16,24},{20,28},{24,16},{28,20},{1,9},{5... | collective-permute-start | bytes 1769480 | tf_op jit(solution)/shard_map/ppermute | solution.py:334
  261.9 1.8 collective-permute-start.30
  266.0 18.6 %finish.1 = bf16[2048,768]{1,0:T(8,128)(2,1)} custom-call(s32[71]{0:T(128)} %pad_add_fusion.tab, f32[2048,768]{1,0:T(8,128)} %get-tuple-element.83.x1_ref, bf16[2048,3072]{1,0:T(8,128)(2,1)} %get-tuple-element.96.act_ref, bf16[480,768]{1,0:T(8,128)(2,1)} %copy-done, bf16[480,768]{1,0:T(8,128)(2,1)} %collective-permute-done.24.rest_9_.rest_1_, ...), custom_call_target="tpu_custom_call" | custom-call | flops 193273536 | bytes 534773 | tf_op jit(solution)/shard_map/finish/pallas_call | solution.py:917
  284.6 4.9 %collective-permute-done.30 = bf16[384,768]{1,0:T(8,128)(2,1)S(1)} collective-permute-done((bf16[384,768]{1,0:T(8,128)(2,1)}, bf16[384,768]{1,0:T(8,128)(2,1)S(1)}, u32[]{:S(2)}, u32[]{:S(2)}) %collective-permute-start.30) | collective-permute-done | bytes 589856 | tf_op jit(solution)/shard_map/ppermute | solution.py:334
  291.5 2.2 fusion.2
  293.7 18.0 %project_back.1 = (bf16[2048,768]{1,0:T(8,128)(2,1)}, f32[8,768]{1,0:T(8,128)}) custom-call(s32[71]{0:T(128)} %pad_add_fusion.tab, f32[8,768]{1,0:T(8,128)} %get-tuple-element.66.nrm_ref, bf16[2048,768]{1,0:T(8,128)(2,1)} %get-tuple-element.86.dq_ref, bf16[2048,768]{1,0:T(8,128)(2,1)} %get-tuple-element.87.dk_ref, ...), custom_call_target="tpu_custom_call" | custom-call | flops 144955152 | bytes 511180 | tf_op jit(solution)/shard_map/project_back/pallas_call | solution.py:580
  315.1 2.5 collective-permute-done.33
  318.9 2.5 collective-permute-done.34
  321.5 2.9 collective-permute-start.37
  324.6 3.6 %collective-permute-start.39 = (bf16[96,768]{1,0:T(8,128)(2,1)S(1)}, bf16[96,768]{1,0:T(8,128)(2,1)S(1)}, u32[]{:S(2)}, u32[]{:S(2)}) collective-permute-start(bf16[96,768]{1,0:T(8,128)(2,1)S(1)} %get-tuple-element.121), channel_id=1, source_target_pairs={{0,3},{1,0},{2,1},{3,2},{4,7},{5,4},{6,5},{7,6},{8,11},{9,8},{10,9... | collective-permute-start | bytes 442376 | tf_op jit(solution)/shard_map/ppermute | solution.py:376
  328.3 9.1 %collective-permute-done.36 = f32[8,768]{1,0:T(8,128)S(1)} collective-permute-done((f32[8,768]{1,0:T(8,128)S(1)}, f32[8,768]{1,0:T(8,128)S(1)}, u32[]{:S(2)}, u32[]{:S(2)}) %collective-permute-start.36) | collective-permute-done | bytes 24608 | tf_op jit(solution)/shard_map/ppermute | solution.py:1036
  338.3 2.8 collective-permute-start.41
  347.0 3.7 %collective-permute-done.41 = bf16[96,768]{1,0:T(8,128)(2,1)S(1)} collective-permute-done((bf16[96,768]{1,0:T(8,128)(2,1)S(1)}, bf16[96,768]{1,0:T(8,128)(2,1)S(1)}, u32[]{:S(2)}, u32[]{:S(2)}) %collective-permute-start.41) | collective-permute-done | bytes 147488 | tf_op jit(solution)/shard_map/ppermute | solution.py:376
  (176 shorter events, 41.3 us)
Async XLA Ops:
  7.2 258.8 %reduce-scatter.2.cloned.1.call-start = ((), (), s32[]{:S(2)}) async-start(), calls=%async_computation.1 | async-start | bytes 10616832 | tf_op jit(solution)/shard_map/reduce_scatter | solution.py:1018
  10.0 14.5 %collective-permute-start = (bf16[160,768]{1,0:T(8,128)(2,1)S(1)}, bf16[160,768]{1,0:T(8,128)(2,1)}, u32[]{:S(2)}, u32[]{:S(2)}) collective-permute-start(bf16[160,768]{1,0:T(8,128)(2,1)S(1)} %pad_maximum_fusion.1.rest_0_), channel_id=1, source_target_pairs={{0,8},{4,12},{8,0},{12,4},{16,24},{20,28},{24,16},{28,20},{1,9},{5... | collective-permute-start | bytes 737288 | tf_op jit(solution)/shard_map/gather_weights/ppermute | solution.py:334
  13.2 16.6 %collective-permute-start.3 = (bf16[160,768]{1,0:T(8,128)(2,1)S(1)}, bf16[160,768]{1,0:T(8,128)(2,1)}, u32[]{:S(2)}, u32[]{:S(2)}) collective-permute-start(bf16[160,768]{1,0:T(8,128)(2,1)S(1)} %pad_maximum_fusion.1.rest_0_), channel_id=1, source_target_pairs={{0,4},{4,0},{8,12},{12,8},{16,20},{20,16},{24,28},{28,24},{1,5},{5... | collective-permute-start | bytes 737288 | tf_op jit(solution)/shard_map/gather_weights/ppermute | solution.py:334
  13.2 13.5 %collective-permute-start.8 = (bf16[144,768]{1,0:T(8,128)(2,1)S(1)}, bf16[144,768]{1,0:T(8,128)(2,1)}, u32[]{:S(2)}, u32[]{:S(2)}) collective-permute-start(bf16[144,768]{1,0:T(8,128)(2,1)S(1)} %get-tuple-element.65.rest_8_), channel_id=1, source_target_pairs={{0,16},{4,20},{8,24},{12,28},{16,0},{20,4},{24,8},{28,12},{1,17},{... | collective-permute-start | bytes 663560 | tf_op jit(solution)/shard_map/gather_weights/ppermute | solution.py:334
  14.7 13.4 %collective-permute-start.1 = (bf16[160,768]{1,0:T(8,128)(2,1)S(1)}, bf16[160,768]{1,0:T(8,128)(2,1)}, u32[]{:S(2)}, u32[]{:S(2)}) collective-permute-start(bf16[160,768]{1,0:T(8,128)(2,1)S(1)} %pad_maximum_fusion.1.rest_0_), channel_id=1, source_target_pairs={{0,16},{4,20},{8,24},{12,28},{16,0},{20,4},{24,8},{28,12},{1,17},{... | collective-permute-start | bytes 737288 | tf_op jit(solution)/shard_map/gather_weights/ppermute | solution.py:334
  15.2 8.7 %collective-permute-start.7 = (bf16[144,768]{1,0:T(8,128)(2,1)S(1)}, bf16[144,768]{1,0:T(8,128)(2,1)S(1)}, u32[]{:S(2)}, u32[]{:S(2)}) collective-permute-start(bf16[144,768]{1,0:T(8,128)(2,1)S(1)} %get-tuple-element.65.rest_8_), channel_id=1, source_target_pairs={{0,8},{4,12},{8,0},{12,4},{16,24},{20,28},{24,16},{28,20},{1,9},{5... | collective-permute-start | bytes 663560 | tf_op jit(solution)/shard_map/gather_weights/ppermute | solution.py:334
  24.6 9.3 %collective-permute-start.2 = (bf16[160,768]{1,0:T(8,128)(2,1)}, bf16[160,768]{1,0:T(8,128)(2,1)S(1)}, u32[]{:S(2)}, u32[]{:S(2)}) collective-permute-start(bf16[160,768]{1,0:T(8,128)(2,1)} %collective-permute-done.rest_1_), channel_id=1, source_target_pairs={{0,16},{4,20},{8,24},{12,28},{16,0},{20,4},{24,8},{28,12},{1,17},{... | collective-permute-start | bytes 737288 | tf_op jit(solution)/shard_map/gather_weights/ppermute | solution.py:334
  26.7 7.2 %collective-permute-start.9 = (bf16[144,768]{1,0:T(8,128)(2,1)}, bf16[144,768]{1,0:T(8,128)(2,1)S(1)}, u32[]{:S(2)}, u32[]{:S(2)}) collective-permute-start(bf16[144,768]{1,0:T(8,128)(2,1)} %collective-permute-done.8.rest_10_), channel_id=1, source_target_pairs={{0,8},{4,12},{8,0},{12,4},{16,24},{20,28},{24,16},{28,20},{1,9},{5... | collective-permute-start | bytes 663560 | tf_op jit(solution)/shard_map/gather_weights/ppermute | solution.py:334
  28.2 8.6 %collective-permute-start.4 = (bf16[160,768]{1,0:T(8,128)(2,1)}, bf16[160,768]{1,0:T(8,128)(2,1)S(1)}, u32[]{:S(2)}, u32[]{:S(2)}) collective-permute-start(bf16[160,768]{1,0:T(8,128)(2,1)} %collective-permute-done.rest_1_), channel_id=1, source_target_pairs={{0,4},{4,0},{8,12},{12,8},{16,20},{20,16},{24,28},{28,24},{1,5},{5... | collective-permute-start | bytes 737288 | tf_op jit(solution)/shard_map/gather_weights/ppermute | solution.py:334
  28.2 9.7 %collective-permute-start.5 = (bf16[160,768]{1,0:T(8,128)(2,1)}, bf16[160,768]{1,0:T(8,128)(2,1)S(1)}, u32[]{:S(2)}, u32[]{:S(2)}) collective-permute-start(bf16[160,768]{1,0:T(8,128)(2,1)} %collective-permute-done.1.rest_2_), channel_id=1, source_target_pairs={{0,4},{4,0},{8,12},{12,8},{16,20},{20,16},{24,28},{28,24},{1,5},{5... | collective-permute-start | bytes 737288 | tf_op jit(solution)/shard_map/gather_weights/ppermute | solution.py:334
  33.9 23.8 %collective-permute-start.15 = (bf16[480,768]{1,0:T(8,128)(2,1)S(1)}, bf16[480,768]{1,0:T(8,128)(2,1)}, u32[]{:S(2)}, u32[]{:S(2)}) collective-permute-start(bf16[480,768]{1,0:T(8,128)(2,1)S(1)} %bitcast_dynamic-update-slice_fusion.rest_8_.rest_0_), channel_id=1, source_target_pairs={{0,16},{4,20},{8,24},{12,28},{16,0},{20,4},{24,8},{28,12},{1,17},{... | collective-permute-start | bytes 2211848 | tf_op jit(solution)/shard_map/gather_weights/ppermute | solution.py:334
  35.3 22.4 %collective-permute-start.14 = (bf16[384,768]{1,0:T(8,128)(2,1)}, bf16[384,768]{1,0:T(8,128)(2,1)}, u32[]{:S(2)}, u32[]{:S(2)}) collective-permute-start(bf16[384,768]{1,0:T(8,128)(2,1)} %bitcast.4.rest_0_), channel_id=1, source_target_pairs={{0,8},{4,12},{8,0},{12,4},{16,24},{20,28},{24,16},{28,20},{1,9},{5... | collective-permute-start | bytes 1769480 | tf_op jit(solution)/shard_map/gather_weights/ppermute | solution.py:334
  36.8 29.1 %collective-permute-start.18 = (bf16[384,768]{1,0:T(8,128)(2,1)}, bf16[384,768]{1,0:T(8,128)(2,1)}, u32[]{:S(2)}, u32[]{:S(2)}) collective-permute-start(bf16[384,768]{1,0:T(8,128)(2,1)} %bitcast.4.rest_0_), channel_id=1, source_target_pairs={{0,16},{4,20},{8,24},{12,28},{16,0},{20,4},{24,8},{28,12},{1,17},{... | collective-permute-start | bytes 1769480 | tf_op jit(solution)/shard_map/gather_weights/ppermute | solution.py:334
  37.8 29.8 %collective-permute-start.19 = (bf16[480,768]{1,0:T(8,128)(2,1)S(1)}, bf16[480,768]{1,0:T(8,128)(2,1)}, u32[]{:S(2)}, u32[]{:S(2)}) collective-permute-start(bf16[480,768]{1,0:T(8,128)(2,1)S(1)} %bitcast_dynamic-update-slice_fusion.rest_8_.rest_0_), channel_id=1, source_target_pairs={{0,8},{4,12},{8,0},{12,4},{16,24},{20,28},{24,16},{28,20},{1,9},{5... | collective-permute-start | bytes 2211848 | tf_op jit(solution)/shard_map/gather_weights/ppermute | solution.py:334
  57.7 30.9 %collective-permute-start.21 = (bf16[480,768]{1,0:T(8,128)(2,1)}, bf16[480,768]{1,0:T(8,128)(2,1)}, u32[]{:S(2)}, u32[]{:S(2)}) collective-permute-start(bf16[480,768]{1,0:T(8,128)(2,1)} %collective-permute-done.15.rest_12_.rest_4_), channel_id=1, source_target_pairs={{0,8},{4,12},{8,0},{12,4},{16,24},{20,28},{24,16},{28,20},{1,9},{5... | collective-permute-start | bytes 2211848 | tf_op jit(solution)/shard_map/gather_weights/ppermute | solution.py:334
  59.2 29.4 %collective-permute-start.20 = (bf16[384,768]{1,0:T(8,128)(2,1)}, bf16[384,768]{1,0:T(8,128)(2,1)}, u32[]{:S(2)}, u32[]{:S(2)}) collective-permute-start(bf16[384,768]{1,0:T(8,128)(2,1)} %collective-permute-done.14.rest_1_), channel_id=1, source_target_pairs={{0,16},{4,20},{8,24},{12,28},{16,0},{20,4},{24,8},{28,12},{1,17},{... | collective-permute-start | bytes 1769480 | tf_op jit(solution)/shard_map/gather_weights/ppermute | solution.py:334
  60.3 30.0 %collective-permute-start.24 = (bf16[480,768]{1,0:T(8,128)(2,1)S(1)}, bf16[480,768]{1,0:T(8,128)(2,1)}, u32[]{:S(2)}, u32[]{:S(2)}) collective-permute-start(bf16[480,768]{1,0:T(8,128)(2,1)S(1)} %bitcast_dynamic-update-slice_fusion.rest_8_.rest_0_), channel_id=1, source_target_pairs={{0,4},{4,0},{8,12},{12,8},{16,20},{20,16},{24,28},{28,24},{1,5},{5... | collective-permute-start | bytes 2211848 | tf_op jit(solution)/shard_map/gather_weights/ppermute | solution.py:334
  66.0 23.8 %collective-permute-start.16 = (bf16[384,768]{1,0:T(8,128)(2,1)}, bf16[384,768]{1,0:T(8,128)(2,1)}, u32[]{:S(2)}, u32[]{:S(2)}) collective-permute-start(bf16[384,768]{1,0:T(8,128)(2,1)} %bitcast.4.rest_0_), channel_id=1, source_target_pairs={{0,4},{4,0},{8,12},{12,8},{16,20},{20,16},{24,28},{28,24},{1,5},{5... | collective-permute-start | bytes 1769480 | tf_op jit(solution)/shard_map/gather_weights/ppermute | solution.py:334
  67.6 22.6 %collective-permute-start.17 = (bf16[384,768]{1,0:T(8,128)(2,1)}, bf16[384,768]{1,0:T(8,128)(2,1)}, u32[]{:S(2)}, u32[]{:S(2)}) collective-permute-start(bf16[384,768]{1,0:T(8,128)(2,1)} %collective-permute-done.14.rest_1_), channel_id=1, source_target_pairs={{0,4},{4,0},{8,12},{12,8},{16,20},{20,16},{24,28},{28,24},{1,5},{5... | collective-permute-start | bytes 1769480 | tf_op jit(solution)/shard_map/gather_weights/ppermute | solution.py:334
  88.6 7.0 %collective-permute-start.25 = (bf16[480,768]{1,0:T(8,128)(2,1)}, bf16[480,768]{1,0:T(8,128)(2,1)}, u32[]{:S(2)}, u32[]{:S(2)}) collective-permute-start(bf16[480,768]{1,0:T(8,128)(2,1)} %collective-permute-done.19.rest_10_.rest_2_), channel_id=1, source_target_pairs={{0,4},{4,0},{8,12},{12,8},{16,20},{20,16},{24,28},{28,24},{1,5},{5... | collective-permute-start | bytes 2211848 | tf_op jit(solution)/shard_map/gather_weights/ppermute | solution.py:334
  172.2 166.1 %all-reduce.2.cloned.1.call-start = ((), (), s32[]{:S(2)}) async-start(), calls=%async_computation.2 | async-start | bytes 2359296 | tf_op jit(solution)/shard_map/psum | solution.py:1025
  243.1 9.9 %collective-permute-start.28 = (bf16[4,384,768]{2,1,0:T(8,128)(2,1)}, bf16[4,384,768]{2,1,0:T(8,128)(2,1)S(1)}, u32[]{:S(2)}, u32[]{:S(2)}) collective-permute-start(bf16[4,384,768]{2,1,0:T(8,128)(2,1)} %get-tuple-element.94), channel_id=1, source_target_pairs={{0,4},{4,0},{8,12},{12,8},{16,20},{20,16},{24,28},{28,24},{1,5},{5... | collective-permute-start | bytes 7077896 | tf_op jit(solution)/shard_map/ppermute | solution.py:334
  256.9 27.8 %collective-permute-start.29 = (bf16[384,768]{1,0:T(8,128)(2,1)}, bf16[384,768]{1,0:T(8,128)(2,1)}, u32[]{:S(2)}, u32[]{:S(2)}) collective-permute-start(bf16[384,768]{1,0:T(8,128)(2,1)} %get-tuple-element.118), channel_id=1, source_target_pairs={{0,8},{4,12},{8,0},{12,4},{16,24},{20,28},{24,16},{28,20},{1,9},{5... | collective-permute-start | bytes 1769480 | tf_op jit(solution)/shard_map/ppermute | solution.py:334
  261.9 27.6 %collective-permute-start.30 = (bf16[384,768]{1,0:T(8,128)(2,1)}, bf16[384,768]{1,0:T(8,128)(2,1)S(1)}, u32[]{:S(2)}, u32[]{:S(2)}) collective-permute-start(bf16[384,768]{1,0:T(8,128)(2,1)} %get-tuple-element.117), channel_id=1, source_target_pairs={{0,16},{4,20},{8,24},{12,28},{16,0},{20,4},{24,8},{28,12},{1,17},{... | collective-permute-start | bytes 1769480 | tf_op jit(solution)/shard_map/ppermute | solution.py:334
  263.7 27.8 %collective-permute-start.31 = (bf16[384,768]{1,0:T(8,128)(2,1)}, bf16[384,768]{1,0:T(8,128)(2,1)}, u32[]{:S(2)}, u32[]{:S(2)}) collective-permute-start(bf16[384,768]{1,0:T(8,128)(2,1)} %get-tuple-element.116), channel_id=1, source_target_pairs={{0,24},{4,28},{8,16},{12,20},{16,8},{20,12},{24,0},{28,4},{1,25},{... | collective-permute-start | bytes 1769480 | tf_op jit(solution)/shard_map/ppermute | solution.py:334
  321.5 16.6 %collective-permute-start.37 = (bf16[96,768]{1,0:T(8,128)(2,1)S(1)}, bf16[96,768]{1,0:T(8,128)(2,1)S(1)}, u32[]{:S(2)}, u32[]{:S(2)}) collective-permute-start(bf16[96,768]{1,0:T(8,128)(2,1)S(1)} %get-tuple-element.123), channel_id=1, source_target_pairs={{0,2},{1,3},{2,0},{3,1},{4,6},{5,7},{6,4},{7,5},{8,10},{9,11},{10,... | collective-permute-start | bytes 442376 | tf_op jit(solution)/shard_map/ppermute | solution.py:376
  324.4 13.7 %collective-permute-start.38 = (bf16[96,768]{1,0:T(8,128)(2,1)S(1)}, bf16[96,768]{1,0:T(8,128)(2,1)S(1)}, u32[]{:S(2)}, u32[]{:S(2)}) collective-permute-start(bf16[96,768]{1,0:T(8,128)(2,1)S(1)} %get-tuple-element.122), channel_id=1, source_target_pairs={{0,1},{1,2},{2,3},{3,0},{4,5},{5,6},{6,7},{7,4},{8,9},{9,10},{10,1... | collective-permute-start | bytes 442376 | tf_op jit(solution)/shard_map/ppermute | solution.py:376
  324.6 13.5 %collective-permute-start.39 = (bf16[96,768]{1,0:T(8,128)(2,1)S(1)}, bf16[96,768]{1,0:T(8,128)(2,1)S(1)}, u32[]{:S(2)}, u32[]{:S(2)}) collective-permute-start(bf16[96,768]{1,0:T(8,128)(2,1)S(1)} %get-tuple-element.121), channel_id=1, source_target_pairs={{0,3},{1,0},{2,1},{3,2},{4,7},{5,4},{6,5},{7,6},{8,11},{9,8},{10,9... | collective-permute-start | bytes 442376 | tf_op jit(solution)/shard_map/ppermute | solution.py:376
  328.3 9.2 %collective-permute-start.36 = (f32[8,768]{1,0:T(8,128)S(1)}, f32[8,768]{1,0:T(8,128)S(1)}, u32[]{:S(2)}, u32[]{:S(2)}) collective-permute-start(f32[8,768]{1,0:T(8,128)S(1)} %add.196), channel_id=1, source_target_pairs={{0,2},{1,3},{2,0},{3,1},{4,6},{5,7},{6,4},{7,5},{8,10},{9,11},{10,... | collective-permute-start | bytes 73736 | tf_op jit(solution)/shard_map/ppermute | solution.py:1036
  338.2 8.7 %collective-permute-start.40 = (bf16[96,768]{1,0:T(8,128)(2,1)S(1)}, bf16[96,768]{1,0:T(8,128)(2,1)S(1)}, u32[]{:S(2)}, u32[]{:S(2)}) collective-permute-start(bf16[96,768]{1,0:T(8,128)(2,1)S(1)} %fusion.8), channel_id=1, source_target_pairs={{0,1},{1,2},{2,3},{3,0},{4,5},{5,6},{6,7},{7,4},{8,9},{9,10},{10,1... | collective-permute-start | bytes 442376 | tf_op jit(solution)/shard_map/ppermute | solution.py:376
  338.3 12.4 %collective-permute-start.41 = (bf16[96,768]{1,0:T(8,128)(2,1)S(1)}, bf16[96,768]{1,0:T(8,128)(2,1)S(1)}, u32[]{:S(2)}, u32[]{:S(2)}) collective-permute-start(bf16[96,768]{1,0:T(8,128)(2,1)S(1)} %fusion.8), channel_id=1, source_target_pairs={{0,2},{1,3},{2,0},{3,1},{4,6},{5,7},{6,4},{7,5},{8,10},{9,11},{10,... | collective-permute-start | bytes 442376 | tf_op jit(solution)/shard_map/ppermute | solution.py:376
  341.1 9.6 %collective-permute-start.42 = (bf16[96,768]{1,0:T(8,128)(2,1)S(1)}, bf16[96,768]{1,0:T(8,128)(2,1)S(1)}, u32[]{:S(2)}, u32[]{:S(2)}) collective-permute-start(bf16[96,768]{1,0:T(8,128)(2,1)S(1)} %fusion.8), channel_id=1, source_target_pairs={{0,3},{1,0},{2,1},{3,2},{4,7},{5,4},{6,5},{7,6},{8,11},{9,8},{10,9... | collective-permute-start | bytes 442376 | tf_op jit(solution)/shard_map/ppermute | solution.py:376
  (39 other events, 200.7 us)
Sparse Core Ops, SparseCore 0:
  172.3 78.3 reduce-scatter.1
  266.2 55.3 all-reduce.1

commit v4 on v3

--- a/solution.py
+++ b/solution.py
@@ -747,7 +747,7 @@
             g_refs[1][...] = gd_sc[...].astype(BF)
 
 
-def middle(table, norms, att, x, cot, w_up, w_down, w_proj, hidden, size, tb=512, sub=256):
+def middle(table, norms, att, x, cot, w_up, w_down, w_proj, hidden, size, tb=512, sub=512):
     n, width = x.shape
     chunks = hidden // width
     steps = n // tb
@@ -1029,8 +1029,11 @@
         input_grad, grad_norm1 = project_back(after_table(qkv_own), norms, *dqkv, tokens, grad_middle, w_qkv)
         norm_sum = jnp.concatenate([grad_norm1[:2], grad_norm2[:2], jnp.zeros((4, width), F32)], axis=0)
         quarter = quarter_sum(qkv_own, grad_norm1)
-        quarter = after(quarter, packed_sum)
-        for bit in (1, 2, 4):
+        norm_sum = after(norm_sum, quarter)
+        for bit in (1, 2):
+            norm_sum = norm_sum + hop(norm_sum, bit, 8)
+        quarter, norm_sum = after((quarter, norm_sum), packed_sum)
+        for bit in (4,):
             norm_sum = norm_sum + hop(norm_sum, bit, 8)
         for bit in (1, 2):
             norm_sum = norm_sum + lax.ppermute(norm_sum, "rep", [(i, i ^ bit) for i in range(4)])

time: 361 us -> 356 us (0.986)
    psum x1, waiting for transfers between devices: 0.02 us -> 4.61 us  [per_device(): packed_sum = lax.psum(packed_own, 'rep')]
    ppermute x6, waiting for transfers between devices: 3.85 us -> 0.02 us  [shift(): return lax.ppermute(value, 'rep', [(i, (i + by) % 4) for i in range(4)])]
    ppermute x35, starting transfers between devices: 33.9 us -> 30.2 us  [hop(): return lax.ppermute(value, 'fsdp', [(i, i ^ bit) for i in range(size)])]
  transfers between devices with their start and end apart: 45 -> 45, of which waited for: 15 -> 14; matrix products, arithmetic and copies ran while one was open for 6% -> 7% of each run, Pallas kernels for 40% -> 41%
where the time goes in v4:
time: 356 us; the launch traced here: 353 us
  Pallas kernels  219 us (62%)
  waiting for transfers between devices  45.5 us (13%)
  starting transfers between devices  41.7 us (12%)
  other arithmetic  16.9 us (5%)
  local copies, waits for them, and re-layouts  16 us (4%)
  between operations  14.6 us (4%)
    pallas_call x1, Pallas kernels, middle(): pl.pallas_call(partial(middle_kernel, size, tb, sub, chunks, w_up, w_down...  74.8 us
    pallas_call x2, Pallas kernels, attention_call(): pl.pallas_call(partial(kernel, width // 128), out_shape=[jax.ShapeDtypeSt...  57.4 us
    ppermute x35, waiting for transfers between devices, hop(): return lax.ppermute(value, 'fsdp', [(i, i ^ bit) for i in range(size)])  35.2 us
    ppermute x35, starting transfers between devices, hop(): return lax.ppermute(value, 'fsdp', [(i, i ^ bit) for i in range(size)])  30.2 us
    pallas_call x1, Pallas kernels, attended_back(): pl.pallas_call(partial(attended_back_kernel, size, tb, sub, 4, w_down, w_...  19.9 us
    pallas_call x1, Pallas kernels, finish(): pl.pallas_call(partial(finish_kernel, size, blocks, w_down), out_shape=ja...  18.5 us
    pallas_call x1, Pallas kernels, project_back(): pl.pallas_call(partial(project_back_kernel, weight, count), out_shape=[ja...  17.8 us
    pallas_call x1, Pallas kernels, project(): pl.pallas_call(partial(project_kernel, weight, count), out_shape=[sds((n,...  15.7 us
  transfers between devices with their start and end apart: 45, of which 14 were waited for; matrix products, arithmetic and copies ran while one was open for 7% of the time, Pallas kernels for 41%

profile of v4, /device:TPU:0, one launch (start us, length us, event | category | flops | bytes accessed | tf_op | source)
XLA Modules:
  0.0 353.5 jit_solution(3500656803057619924)
XLA Ops:
  8.4 1.6 dynamic_update_slice.16
  10.0 3.1 collective-permute-start
  15.4 2.2 multiply_add_fusion.2
  22.0 1.9 collective-permute-done.7.rest_9_
  24.6 1.8 collective-permute-start.2
  29.8 4.0 %collective-permute-done.9.rest_11_ = bf16[144,768]{1,0:T(8,128)(2,1)S(1)} collective-permute-done((bf16[144,768]{1,0:T(8,128)(2,1)}, bf16[144,768]{1,0:T(8,128)(2,1)S(1)}, u32[]{:S(2)}, u32[]{:S(2)}) %collective-permute-start.9) | collective-permute-done | bytes 221216 | tf_op jit(solution)/shard_map/gather_weights/ppermute | solution.py:334
  39.4 1.8 multiply_add_fusion.3
  42.0 15.7 %project.1 = (bf16[2048,768]{1,0:T(8,128)(2,1)}, bf16[2048,2304]{1,0:T(8,128)(2,1)}, f32[8,768]{1,0:T(8,128)}) custom-call(s32[71]{0:T(128)} %pad_add_fusion.tab, bf16[2048,768]{1,0:T(8,128)(2,1)} %x_ref.5, bf16[160,768]{1,0:T(8,128)(2,1)} %copy-done.5, bf16[160,768]{1,0:T(8,128)(2,1)} %collective-permute-done.rest_1_, ...), custom_call_target="tpu_custom_call" | custom-call | flops 144955152 | bytes 385351 | tf_op jit(solution)/shard_map/project/pallas_call | solution.py:469
  60.3 5.6 %collective-permute-done.18.rest_4_ = bf16[384,768]{1,0:T(8,128)(2,1)} collective-permute-done((bf16[384,768]{1,0:T(8,128)(2,1)}, bf16[384,768]{1,0:T(8,128)(2,1)}, u32[]{:S(2)}, u32[]{:S(2)}) %collective-permute-start.18) | collective-permute-done | bytes 589856 | tf_op jit(solution)/shard_map/gather_weights/ppermute | solution.py:334
  66.0 1.6 collective-permute-done.19.rest_10_.rest_2_
  67.6 21.0 %attend.1.att_ref = bf16[2048,768]{1,0:T(8,128)(2,1)} custom-call(s32[71]{0:T(128)} %pad_add_fusion.tab, bf16[2048,2304]{1,0:T(8,128)(2,1)} %get-tuple-element.71.q_ref.k_ref.v_ref, bf16[2048,2304]{1,0:T(8,128)(2,1)} %get-tuple-element.71.q_ref.k_ref.v_ref, bf16[2048,2304]{1,0:T(8,128)(2,1)} %get-tuple-element.71.q_ref.k_ref.v_ref), custom_call_target="tpu_custom_call" | custom-call | flops 480000000 | bytes 251658 | tf_op jit(solution)/shard_map/attend/pallas_call | solution.py:307
  90.2 4.9 %collective-permute-done.22.rest_5_ = bf16[384,768]{1,0:T(8,128)(2,1)} collective-permute-done((bf16[384,768]{1,0:T(8,128)(2,1)}, bf16[384,768]{1,0:T(8,128)(2,1)}, u32[]{:S(2)}, u32[]{:S(2)}) %collective-permute-start.22) | collective-permute-done | bytes 589856 | tf_op jit(solution)/shard_map/gather_weights/ppermute | solution.py:334
  96.0 74.8 %middle.1 = (f32[2048,768]{1,0:T(8,128)}, bf16[2048,3072]{1,0:T(8,128)(2,1)}, f32[2048,768]{1,0:T(8,128)}, bf16[6144,768]{1,0:T(8,128)(2,1)}) custom-call(s32[71]{0:T(128)} %pad_add_fusion.tab, f32[8,768]{1,0:T(8,128)} %get-tuple-element.68.nrm_ref, bf16[2048,768]{1,0:T(8,128)(2,1)} %attend.1.att_ref, bf16[2048,768]{1,0:T(8,128)(2,1)} %x_ref.5, ...), custom_call_target="tpu_custom_call" | custom-call | flops 1014686016 | bytes 1321205 | tf_op jit(solution)/shard_map/middle/pallas_call | solution.py:773
  170.9 19.9 %attended_back.1 = (f32[2048,768]{1,0:T(8,128)}, bf16[2048,768]{1,0:T(8,128)(2,1)}, f32[8,768]{1,0:T(8,128)}, bf16[4,96,768]{2,1,0:T(8,128)(2,1)}, bf16[4,96,768]{2,1,0:T(8,128)(2,1)}) custom-call(s32[71]{0:T(128)} %pad_add_fusion.tab, f32[8,768]{1,0:T(8,128)} %get-tuple-element.68.nrm_ref, f32[2048,768]{1,0:T(8,128)} %get-tuple-element.85.x1_ref, ...), custom_call_target="tpu_custom_call" | custom-call | flops 96636768 | bytes 566231 | tf_op jit(solution)/shard_map/attended_back/pallas_call | solution.py:862
  190.8 36.4 %attend_back.1 = (bf16[2048,768]{1,0:T(8,128)(2,1)}, bf16[2048,768]{1,0:T(8,128)(2,1)}, bf16[2048,768]{1,0:T(8,128)(2,1)}) custom-call(s32[71]{0:T(128)} %pad_add_fusion.tab, bf16[2048,2304]{1,0:T(8,128)(2,1)} %get-tuple-element.71.q_ref.k_ref.v_ref, bf16[2048,2304]{1,0:T(8,128)(2,1)} %get-tuple-element.71.q_ref.k_ref.v_ref, ...), custom_call_target="tpu_custom_call" | custom-call | flops 960000000 | bytes 440401 | tf_op jit(solution)/shard_map/attend_back/pallas_call | solution.py:307
  227.1 14.7 %project_grad.1 = (bf16[4,384,768]{2,1,0:T(8,128)(2,1)}, bf16[4,384,768]{2,1,0:T(8,128)(2,1)}) custom-call(s32[71]{0:T(128)} %pad_add_fusion.tab, bf16[2048,768]{1,0:T(8,128)(2,1)} %get-tuple-element.88.dq_ref, bf16[2048,768]{1,0:T(8,128)(2,1)} %get-tuple-element.89.dk_ref, bf16[2048,768]{1,0:T(8,128)(2,1)} %get-tuple-element.90.dv_ref, ...), custom_call_target="tpu_custom_call" | custom-call | flops 144955152 | bytes 322437 | tf_op jit(solution)/shard_map/project_grad/pallas_call | solution.py:526
  241.8 2.7 collective-permute-start.28
  244.5 4.4 %collective-permute-done.28 = bf16[4,384,768]{2,1,0:T(8,128)(2,1)S(1)} collective-permute-done((bf16[4,384,768]{2,1,0:T(8,128)(2,1)}, bf16[4,384,768]{2,1,0:T(8,128)(2,1)S(1)}, u32[]{:S(2)}, u32[]{:S(2)}) %collective-permute-start.28) | collective-permute-done | bytes 2359328 | tf_op jit(solution)/shard_map/ppermute | solution.py:334
  248.9 3.8 %fusion.5 = (bf16[384,768]{1,0:T(8,128)(2,1)}, bf16[384,768]{1,0:T(8,128)(2,1)}, bf16[384,768]{1,0:T(8,128)(2,1)}) fusion(bf16[4,384,768]{2,1,0:T(8,128)(2,1)S(1)} %collective-permute-done.28, bf16[4,384,768]{2,1,0:T(8,128)(2,1)} %get-tuple-element.94), kind=kLoop, calls=%fused_computation.13 | loop fusion | flops 3538944 | bytes 5308416 | tf_op jit(solution)/shard_map/convert_element_type | solution.py:358
  252.7 6.7 %collective-permute-start.29 = (bf16[384,768]{1,0:T(8,128)(2,1)}, bf16[384,768]{1,0:T(8,128)(2,1)}, u32[]{:S(2)}, u32[]{:S(2)}) collective-permute-start(bf16[384,768]{1,0:T(8,128)(2,1)} %get-tuple-element.122), channel_id=1, source_target_pairs={{0,8},{4,12},{8,0},{12,4},{16,24},{20,28},{24,16},{28,20},{1,9},{5... | collective-permute-start | bytes 1769480 | tf_op jit(solution)/shard_map/ppermute | solution.py:334
  262.3 18.5 %finish.1 = bf16[2048,768]{1,0:T(8,128)(2,1)} custom-call(s32[71]{0:T(128)} %pad_add_fusion.tab, f32[2048,768]{1,0:T(8,128)} %get-tuple-element.85.x1_ref, bf16[2048,3072]{1,0:T(8,128)(2,1)} %get-tuple-element.98.act_ref, bf16[480,768]{1,0:T(8,128)(2,1)} %copy-done, bf16[480,768]{1,0:T(8,128)(2,1)} %collective-permute-done.24.rest_9_.rest_1_, ...), custom_call_target="tpu_custom_call" | custom-call | flops 193273536 | bytes 534773 | tf_op jit(solution)/shard_map/finish/pallas_call | solution.py:917
  280.8 6.5 %collective-permute-done.30 = bf16[384,768]{1,0:T(8,128)(2,1)S(1)} collective-permute-done((bf16[384,768]{1,0:T(8,128)(2,1)}, bf16[384,768]{1,0:T(8,128)(2,1)S(1)}, u32[]{:S(2)}, u32[]{:S(2)}) %collective-permute-start.30) | collective-permute-done | bytes 589856 | tf_op jit(solution)/shard_map/ppermute | solution.py:334
  288.2 2.2 fusion.2
  292.3 2.3 collective-permute-start.33
  296.2 17.8 %project_back.1 = (bf16[2048,768]{1,0:T(8,128)(2,1)}, f32[8,768]{1,0:T(8,128)}) custom-call(s32[71]{0:T(128)} %pad_add_fusion.tab, f32[8,768]{1,0:T(8,128)} %get-tuple-element.68.nrm_ref, bf16[2048,768]{1,0:T(8,128)(2,1)} %get-tuple-element.88.dq_ref, bf16[2048,768]{1,0:T(8,128)(2,1)} %get-tuple-element.89.dk_ref, ...), custom_call_target="tpu_custom_call" | custom-call | flops 144955152 | bytes 511180 | tf_op jit(solution)/shard_map/project_back/pallas_call | solution.py:580
  318.2 2.4 collective-permute-done.36
  320.7 4.6 %all-reduce.2.cloned.1.call-done = bf16[768,768]{1,0:T(8,128)(2,1)} async-done(((bf16[768,768]{1,0:T(8,128)(2,1)}), bf16[768,768]{1,0:T(8,128)(2,1)}) %all-reduce.2.cloned.1.call-update) | async-done | bytes 1179664 | tf_op jit(solution)/shard_map/psum | solution.py:1025
  325.3 1.8 collective-permute-start.40
  327.1 1.7 collective-permute-start.41
  328.8 1.6 collective-permute-start.42
  332.5 1.8 collective-permute-done.37
  334.8 4.7 %collective-permute-done.38 = f32[8,768]{1,0:T(8,128)S(1)} collective-permute-done((f32[8,768]{1,0:T(8,128)S(1)}, f32[8,768]{1,0:T(8,128)S(1)}, u32[]{:S(2)}, u32[]{:S(2)}) %collective-permute-start.38) | collective-permute-done | bytes 24608 | tf_op jit(solution)/shard_map/ppermute | solution.py:1039
  (176 shorter events, 44.2 us)
Async XLA Ops:
  7.2 253.7 %reduce-scatter.2.cloned.1.call-start = ((), (), s32[]{:S(2)}) async-start(), calls=%async_computation.1 | async-start | bytes 10616832 | tf_op jit(solution)/shard_map/reduce_scatter | solution.py:1018
  10.0 14.5 %collective-permute-start = (bf16[160,768]{1,0:T(8,128)(2,1)S(1)}, bf16[160,768]{1,0:T(8,128)(2,1)}, u32[]{:S(2)}, u32[]{:S(2)}) collective-permute-start(bf16[160,768]{1,0:T(8,128)(2,1)S(1)} %pad_maximum_fusion.1.rest_0_), channel_id=1, source_target_pairs={{0,8},{4,12},{8,0},{12,4},{16,24},{20,28},{24,16},{28,20},{1,9},{5... | collective-permute-start | bytes 737288 | tf_op jit(solution)/shard_map/gather_weights/ppermute | solution.py:334
  13.2 16.6 %collective-permute-start.3 = (bf16[160,768]{1,0:T(8,128)(2,1)S(1)}, bf16[160,768]{1,0:T(8,128)(2,1)}, u32[]{:S(2)}, u32[]{:S(2)}) collective-permute-start(bf16[160,768]{1,0:T(8,128)(2,1)S(1)} %pad_maximum_fusion.1.rest_0_), channel_id=1, source_target_pairs={{0,4},{4,0},{8,12},{12,8},{16,20},{20,16},{24,28},{28,24},{1,5},{5... | collective-permute-start | bytes 737288 | tf_op jit(solution)/shard_map/gather_weights/ppermute | solution.py:334
  13.2 13.5 %collective-permute-start.8 = (bf16[144,768]{1,0:T(8,128)(2,1)S(1)}, bf16[144,768]{1,0:T(8,128)(2,1)}, u32[]{:S(2)}, u32[]{:S(2)}) collective-permute-start(bf16[144,768]{1,0:T(8,128)(2,1)S(1)} %get-tuple-element.67.rest_8_), channel_id=1, source_target_pairs={{0,16},{4,20},{8,24},{12,28},{16,0},{20,4},{24,8},{28,12},{1,17},{... | collective-permute-start | bytes 663560 | tf_op jit(solution)/shard_map/gather_weights/ppermute | solution.py:334
  14.7 13.4 %collective-permute-start.1 = (bf16[160,768]{1,0:T(8,128)(2,1)S(1)}, bf16[160,768]{1,0:T(8,128)(2,1)}, u32[]{:S(2)}, u32[]{:S(2)}) collective-permute-start(bf16[160,768]{1,0:T(8,128)(2,1)S(1)} %pad_maximum_fusion.1.rest_0_), channel_id=1, source_target_pairs={{0,16},{4,20},{8,24},{12,28},{16,0},{20,4},{24,8},{28,12},{1,17},{... | collective-permute-start | bytes 737288 | tf_op jit(solution)/shard_map/gather_weights/ppermute | solution.py:334
  15.2 8.7 %collective-permute-start.7 = (bf16[144,768]{1,0:T(8,128)(2,1)S(1)}, bf16[144,768]{1,0:T(8,128)(2,1)S(1)}, u32[]{:S(2)}, u32[]{:S(2)}) collective-permute-start(bf16[144,768]{1,0:T(8,128)(2,1)S(1)} %get-tuple-element.67.rest_8_), channel_id=1, source_target_pairs={{0,8},{4,12},{8,0},{12,4},{16,24},{20,28},{24,16},{28,20},{1,9},{5... | collective-permute-start | bytes 663560 | tf_op jit(solution)/shard_map/gather_weights/ppermute | solution.py:334
  24.6 9.3 %collective-permute-start.2 = (bf16[160,768]{1,0:T(8,128)(2,1)}, bf16[160,768]{1,0:T(8,128)(2,1)S(1)}, u32[]{:S(2)}, u32[]{:S(2)}) collective-permute-start(bf16[160,768]{1,0:T(8,128)(2,1)} %collective-permute-done.rest_1_), channel_id=1, source_target_pairs={{0,16},{4,20},{8,24},{12,28},{16,0},{20,4},{24,8},{28,12},{1,17},{... | collective-permute-start | bytes 737288 | tf_op jit(solution)/shard_map/gather_weights/ppermute | solution.py:334
  26.7 7.2 %collective-permute-start.9 = (bf16[144,768]{1,0:T(8,128)(2,1)}, bf16[144,768]{1,0:T(8,128)(2,1)S(1)}, u32[]{:S(2)}, u32[]{:S(2)}) collective-permute-start(bf16[144,768]{1,0:T(8,128)(2,1)} %collective-permute-done.8.rest_10_), channel_id=1, source_target_pairs={{0,8},{4,12},{8,0},{12,4},{16,24},{20,28},{24,16},{28,20},{1,9},{5... | collective-permute-start | bytes 663560 | tf_op jit(solution)/shard_map/gather_weights/ppermute | solution.py:334
  28.2 8.6 %collective-permute-start.4 = (bf16[160,768]{1,0:T(8,128)(2,1)}, bf16[160,768]{1,0:T(8,128)(2,1)S(1)}, u32[]{:S(2)}, u32[]{:S(2)}) collective-permute-start(bf16[160,768]{1,0:T(8,128)(2,1)} %collective-permute-done.rest_1_), channel_id=1, source_target_pairs={{0,4},{4,0},{8,12},{12,8},{16,20},{20,16},{24,28},{28,24},{1,5},{5... | collective-permute-start | bytes 737288 | tf_op jit(solution)/shard_map/gather_weights/ppermute | solution.py:334
  28.2 9.7 %collective-permute-start.5 = (bf16[160,768]{1,0:T(8,128)(2,1)}, bf16[160,768]{1,0:T(8,128)(2,1)S(1)}, u32[]{:S(2)}, u32[]{:S(2)}) collective-permute-start(bf16[160,768]{1,0:T(8,128)(2,1)} %collective-permute-done.1.rest_2_), channel_id=1, source_target_pairs={{0,4},{4,0},{8,12},{12,8},{16,20},{20,16},{24,28},{28,24},{1,5},{5... | collective-permute-start | bytes 737288 | tf_op jit(solution)/shard_map/gather_weights/ppermute | solution.py:334
  29.8 7.0 %collective-permute-start.12 = (bf16[144,768]{1,0:T(8,128)(2,1)}, bf16[144,768]{1,0:T(8,128)(2,1)S(1)}, u32[]{:S(2)}, u32[]{:S(2)}) collective-permute-start(bf16[144,768]{1,0:T(8,128)(2,1)} %collective-permute-done.8.rest_10_), channel_id=1, source_target_pairs={{0,4},{4,0},{8,12},{12,8},{16,20},{20,16},{24,28},{28,24},{1,5},{5... | collective-permute-start | bytes 663560 | tf_op jit(solution)/shard_map/gather_weights/ppermute | solution.py:334
  33.9 23.8 %collective-permute-start.15 = (bf16[480,768]{1,0:T(8,128)(2,1)S(1)}, bf16[480,768]{1,0:T(8,128)(2,1)}, u32[]{:S(2)}, u32[]{:S(2)}) collective-permute-start(bf16[480,768]{1,0:T(8,128)(2,1)S(1)} %bitcast_dynamic-update-slice_fusion.rest_8_.rest_0_), channel_id=1, source_target_pairs={{0,16},{4,20},{8,24},{12,28},{16,0},{20,4},{24,8},{28,12},{1,17},{... | collective-permute-start | bytes 2211848 | tf_op jit(solution)/shard_map/gather_weights/ppermute | solution.py:334
  35.3 22.4 %collective-permute-start.14 = (bf16[384,768]{1,0:T(8,128)(2,1)}, bf16[384,768]{1,0:T(8,128)(2,1)}, u32[]{:S(2)}, u32[]{:S(2)}) collective-permute-start(bf16[384,768]{1,0:T(8,128)(2,1)} %bitcast.4.rest_0_), channel_id=1, source_target_pairs={{0,8},{4,12},{8,0},{12,4},{16,24},{20,28},{24,16},{28,20},{1,9},{5... | collective-permute-start | bytes 1769480 | tf_op jit(solution)/shard_map/gather_weights/ppermute | solution.py:334
  36.8 29.1 %collective-permute-start.18 = (bf16[384,768]{1,0:T(8,128)(2,1)}, bf16[384,768]{1,0:T(8,128)(2,1)}, u32[]{:S(2)}, u32[]{:S(2)}) collective-permute-start(bf16[384,768]{1,0:T(8,128)(2,1)} %bitcast.4.rest_0_), channel_id=1, source_target_pairs={{0,16},{4,20},{8,24},{12,28},{16,0},{20,4},{24,8},{28,12},{1,17},{... | collective-permute-start | bytes 1769480 | tf_op jit(solution)/shard_map/gather_weights/ppermute | solution.py:334
  37.8 29.8 %collective-permute-start.19 = (bf16[480,768]{1,0:T(8,128)(2,1)S(1)}, bf16[480,768]{1,0:T(8,128)(2,1)}, u32[]{:S(2)}, u32[]{:S(2)}) collective-permute-start(bf16[480,768]{1,0:T(8,128)(2,1)S(1)} %bitcast_dynamic-update-slice_fusion.rest_8_.rest_0_), channel_id=1, source_target_pairs={{0,8},{4,12},{8,0},{12,4},{16,24},{20,28},{24,16},{28,20},{1,9},{5... | collective-permute-start | bytes 2211848 | tf_op jit(solution)/shard_map/gather_weights/ppermute | solution.py:334
  57.7 30.9 %collective-permute-start.21 = (bf16[480,768]{1,0:T(8,128)(2,1)}, bf16[480,768]{1,0:T(8,128)(2,1)}, u32[]{:S(2)}, u32[]{:S(2)}) collective-permute-start(bf16[480,768]{1,0:T(8,128)(2,1)} %collective-permute-done.15.rest_12_.rest_4_), channel_id=1, source_target_pairs={{0,8},{4,12},{8,0},{12,4},{16,24},{20,28},{24,16},{28,20},{1,9},{5... | collective-permute-start | bytes 2211848 | tf_op jit(solution)/shard_map/gather_weights/ppermute | solution.py:334
  59.2 29.4 %collective-permute-start.20 = (bf16[384,768]{1,0:T(8,128)(2,1)}, bf16[384,768]{1,0:T(8,128)(2,1)}, u32[]{:S(2)}, u32[]{:S(2)}) collective-permute-start(bf16[384,768]{1,0:T(8,128)(2,1)} %collective-permute-done.14.rest_1_), channel_id=1, source_target_pairs={{0,16},{4,20},{8,24},{12,28},{16,0},{20,4},{24,8},{28,12},{1,17},{... | collective-permute-start | bytes 1769480 | tf_op jit(solution)/shard_map/gather_weights/ppermute | solution.py:334
  60.3 29.5 %collective-permute-start.24 = (bf16[480,768]{1,0:T(8,128)(2,1)S(1)}, bf16[480,768]{1,0:T(8,128)(2,1)}, u32[]{:S(2)}, u32[]{:S(2)}) collective-permute-start(bf16[480,768]{1,0:T(8,128)(2,1)S(1)} %bitcast_dynamic-update-slice_fusion.rest_8_.rest_0_), channel_id=1, source_target_pairs={{0,4},{4,0},{8,12},{12,8},{16,20},{20,16},{24,28},{28,24},{1,5},{5... | collective-permute-start | bytes 2211848 | tf_op jit(solution)/shard_map/gather_weights/ppermute | solution.py:334
  66.0 23.3 %collective-permute-start.16 = (bf16[384,768]{1,0:T(8,128)(2,1)}, bf16[384,768]{1,0:T(8,128)(2,1)}, u32[]{:S(2)}, u32[]{:S(2)}) collective-permute-start(bf16[384,768]{1,0:T(8,128)(2,1)} %bitcast.4.rest_0_), channel_id=1, source_target_pairs={{0,4},{4,0},{8,12},{12,8},{16,20},{20,16},{24,28},{28,24},{1,5},{5... | collective-permute-start | bytes 1769480 | tf_op jit(solution)/shard_map/gather_weights/ppermute | solution.py:334
  67.6 22.1 %collective-permute-start.17 = (bf16[384,768]{1,0:T(8,128)(2,1)}, bf16[384,768]{1,0:T(8,128)(2,1)}, u32[]{:S(2)}, u32[]{:S(2)}) collective-permute-start(bf16[384,768]{1,0:T(8,128)(2,1)} %collective-permute-done.14.rest_1_), channel_id=1, source_target_pairs={{0,4},{4,0},{8,12},{12,8},{16,20},{20,16},{24,28},{28,24},{1,5},{5... | collective-permute-start | bytes 1769480 | tf_op jit(solution)/shard_map/gather_weights/ppermute | solution.py:334
  88.6 6.5 %collective-permute-start.25 = (bf16[480,768]{1,0:T(8,128)(2,1)}, bf16[480,768]{1,0:T(8,128)(2,1)}, u32[]{:S(2)}, u32[]{:S(2)}) collective-permute-start(bf16[480,768]{1,0:T(8,128)(2,1)} %collective-permute-done.19.rest_10_.rest_2_), channel_id=1, source_target_pairs={{0,4},{4,0},{8,12},{12,8},{16,20},{20,16},{24,28},{28,24},{1,5},{5... | collective-permute-start | bytes 2211848 | tf_op jit(solution)/shard_map/gather_weights/ppermute | solution.py:334
  170.8 154.5 %all-reduce.2.cloned.1.call-start = ((), (), s32[]{:S(2)}) async-start(), calls=%async_computation.2 | async-start | bytes 2359296 | tf_op jit(solution)/shard_map/psum | solution.py:1025
  241.8 7.1 %collective-permute-start.28 = (bf16[4,384,768]{2,1,0:T(8,128)(2,1)}, bf16[4,384,768]{2,1,0:T(8,128)(2,1)S(1)}, u32[]{:S(2)}, u32[]{:S(2)}) collective-permute-start(bf16[4,384,768]{2,1,0:T(8,128)(2,1)} %get-tuple-element.96), channel_id=1, source_target_pairs={{0,4},{4,0},{8,12},{12,8},{16,20},{20,16},{24,28},{28,24},{1,5},{5... | collective-permute-start | bytes 7077896 | tf_op jit(solution)/shard_map/ppermute | solution.py:334
  252.7 28.1 %collective-permute-start.29 = (bf16[384,768]{1,0:T(8,128)(2,1)}, bf16[384,768]{1,0:T(8,128)(2,1)}, u32[]{:S(2)}, u32[]{:S(2)}) collective-permute-start(bf16[384,768]{1,0:T(8,128)(2,1)} %get-tuple-element.122), channel_id=1, source_target_pairs={{0,8},{4,12},{8,0},{12,4},{16,24},{20,28},{24,16},{28,20},{1,9},{5... | collective-permute-start | bytes 1769480 | tf_op jit(solution)/shard_map/ppermute | solution.py:334
  259.4 27.9 %collective-permute-start.30 = (bf16[384,768]{1,0:T(8,128)(2,1)}, bf16[384,768]{1,0:T(8,128)(2,1)S(1)}, u32[]{:S(2)}, u32[]{:S(2)}) collective-permute-start(bf16[384,768]{1,0:T(8,128)(2,1)} %get-tuple-element.121), channel_id=1, source_target_pairs={{0,16},{4,20},{8,24},{12,28},{16,0},{20,4},{24,8},{28,12},{1,17},{... | collective-permute-start | bytes 1769480 | tf_op jit(solution)/shard_map/ppermute | solution.py:334
  259.7 28.5 %collective-permute-start.31 = (bf16[384,768]{1,0:T(8,128)(2,1)}, bf16[384,768]{1,0:T(8,128)(2,1)}, u32[]{:S(2)}, u32[]{:S(2)}) collective-permute-start(bf16[384,768]{1,0:T(8,128)(2,1)} %get-tuple-element.120), channel_id=1, source_target_pairs={{0,24},{4,28},{8,16},{12,20},{16,8},{20,12},{24,0},{28,4},{1,25},{... | collective-permute-start | bytes 1769480 | tf_op jit(solution)/shard_map/ppermute | solution.py:334
  291.1 24.3 %collective-permute-start.32 = (bf16[96,768]{1,0:T(8,128)(2,1)}, bf16[96,768]{1,0:T(8,128)(2,1)S(1)}, u32[]{:S(2)}, u32[]{:S(2)}) collective-permute-start(bf16[96,768]{1,0:T(8,128)(2,1)} %get-tuple-element.127), channel_id=1, source_target_pairs={{0,2},{1,3},{2,0},{3,1},{4,6},{5,7},{6,4},{7,5},{8,10},{9,11},{10,... | collective-permute-start | bytes 442376 | tf_op jit(solution)/shard_map/ppermute | solution.py:376
  292.3 23.1 %collective-permute-start.33 = (bf16[96,768]{1,0:T(8,128)(2,1)}, bf16[96,768]{1,0:T(8,128)(2,1)S(1)}, u32[]{:S(2)}, u32[]{:S(2)}) collective-permute-start(bf16[96,768]{1,0:T(8,128)(2,1)} %get-tuple-element.126), channel_id=1, source_target_pairs={{0,1},{1,2},{2,3},{3,0},{4,5},{5,6},{6,7},{7,4},{8,9},{9,10},{10,1... | collective-permute-start | bytes 442376 | tf_op jit(solution)/shard_map/ppermute | solution.py:376
  294.7 20.8 %collective-permute-start.34 = (bf16[96,768]{1,0:T(8,128)(2,1)}, bf16[96,768]{1,0:T(8,128)(2,1)S(1)}, u32[]{:S(2)}, u32[]{:S(2)}) collective-permute-start(bf16[96,768]{1,0:T(8,128)(2,1)} %get-tuple-element.125), channel_id=1, source_target_pairs={{0,3},{1,0},{2,1},{3,2},{4,7},{5,4},{6,5},{7,6},{8,11},{9,8},{10,9... | collective-permute-start | bytes 442376 | tf_op jit(solution)/shard_map/ppermute | solution.py:376
  325.3 19.6 %collective-permute-start.40 = (bf16[96,768]{1,0:T(8,128)(2,1)S(1)}, bf16[96,768]{1,0:T(8,128)(2,1)S(1)}, u32[]{:S(2)}, u32[]{:S(2)}) collective-permute-start(bf16[96,768]{1,0:T(8,128)(2,1)S(1)} %fusion.8), channel_id=1, source_target_pairs={{0,1},{1,2},{2,3},{3,0},{4,5},{5,6},{6,7},{7,4},{8,9},{9,10},{10,1... | collective-permute-start | bytes 442376 | tf_op jit(solution)/shard_map/ppermute | solution.py:376
  327.1 17.8 %collective-permute-start.41 = (bf16[96,768]{1,0:T(8,128)(2,1)S(1)}, bf16[96,768]{1,0:T(8,128)(2,1)S(1)}, u32[]{:S(2)}, u32[]{:S(2)}) collective-permute-start(bf16[96,768]{1,0:T(8,128)(2,1)S(1)} %fusion.8), channel_id=1, source_target_pairs={{0,2},{1,3},{2,0},{3,1},{4,6},{5,7},{6,4},{7,5},{8,10},{9,11},{10,... | collective-permute-start | bytes 442376 | tf_op jit(solution)/shard_map/ppermute | solution.py:376
  328.8 16.1 %collective-permute-start.42 = (bf16[96,768]{1,0:T(8,128)(2,1)S(1)}, bf16[96,768]{1,0:T(8,128)(2,1)S(1)}, u32[]{:S(2)}, u32[]{:S(2)}) collective-permute-start(bf16[96,768]{1,0:T(8,128)(2,1)S(1)} %fusion.8), channel_id=1, source_target_pairs={{0,3},{1,0},{2,1},{3,2},{4,7},{5,4},{6,5},{7,6},{8,11},{9,8},{10,9... | collective-permute-start | bytes 442376 | tf_op jit(solution)/shard_map/ppermute | solution.py:376
  (39 other events, 197.3 us)
Sparse Core Ops, SparseCore 0:
  170.9 78.2 reduce-scatter.1
  261.0 64.1 all-reduce.1

commit v5 on v4

--- a/solution.py
+++ b/solution.py
@@ -442,7 +442,13 @@
             c.start()
         for c in norm_copies:
             c.wait()
-        placed = sum(n_sc[i].astype(F32) for i in range(len(norm_copies)))
+        if len(norm_copies) == 1:
+            placed = n_sc[0].astype(F32)
+        else:
+            own = n_sc.shape[2] // 8
+            placed = sum(
+                pltpu.roll(n_sc[i].astype(F32), (me ^ weight.places[i][0]) * own, 1) for i in range(len(norm_copies))
+            )
         nrm_ref[...] = placed[:8, :]
 
     tb, width = x_ref.shape
@@ -957,11 +963,11 @@
     me = lax.axis_index("fsdp")
     table = job_table(segment_ids, rows, me)
     with jax.named_scope("gather_weights"):
-        placed = lax.dynamic_update_slice(jnp.zeros((16, width), BF), norm_params, (0, me * own))
+        padded = jnp.pad(norm_params, ((0, 12), (0, width - own)))
         qkv_t, up_t, down_t, proj_t = qkv_weight.T, up_weight.T, down_weight.T, proj_weight.T
         if fast:
             half = qkv_t.shape[0] // 2
-            first, second = gather_cross(jnp.concatenate([qkv_t[:half], placed], axis=0), qkv_t[half:])
+            first, second = gather_cross(jnp.concatenate([qkv_t[:half], padded], axis=0), qkv_t[half:])
             far = forward_cross(first, second)
             upper = both_cores([*first, far[0]])
             lower = both_cores([*second, far[1]])
@@ -975,7 +981,8 @@
         else:
             whole = lambda shard: lax.all_gather(shard, "fsdp", axis=0, tiled=True)
             w_qkv, w_up, w_down, w_proj = (Weight([(whole(w), None, 0)], 0) for w in (qkv_t, up_t, down_t, proj_t))
-            norm_parts = [lax.psum(placed.astype(F32), "fsdp").astype(BF)]
+            placed = lax.dynamic_update_slice(jnp.zeros((16, width), F32), norm_params.astype(F32), (0, me * own))
+            norm_parts = [lax.psum(placed, "fsdp").astype(BF)]
 
     keep_rate = 1.0 - ema_rate
     blend = lambda target, weight: ema_rate * target + keep_rate * weight.astype(F32)

time: 356 us -> 355 us (level)
  transfers between devices with their start and end apart: 45 -> 45, of which waited for: 14 -> 13; matrix products, arithmetic and copies ran while one was open for 7% -> 7% of each run, Pallas kernels for 41% -> 41%
where the time goes in v5:
time: 355 us; the launch traced here: 353 us
  Pallas kernels  220 us (62%)
  starting transfers between devices  44.7 us (13%)
  waiting for transfers between devices  42 us (12%)
  other arithmetic  17.6 us (5%)
  between operations  14.5 us (4%)
  local copies, waits for them, and re-layouts  14.4 us (4%)
    pallas_call x1, Pallas kernels, middle(): pl.pallas_call(partial(middle_kernel, size, tb, sub, chunks, w_up, w_down...  74.6 us
    pallas_call x2, Pallas kernels, attention_call(): pl.pallas_call(partial(kernel, width // 128), out_shape=[jax.ShapeDtypeSt...  57.4 us
    ppermute x35, waiting for transfers between devices, hop(): return lax.ppermute(value, 'fsdp', [(i, i ^ bit) for i in range(size)])  34.5 us
    ppermute x35, starting transfers between devices, hop(): return lax.ppermute(value, 'fsdp', [(i, i ^ bit) for i in range(size)])  28.6 us
    pallas_call x1, Pallas kernels, attended_back(): pl.pallas_call(partial(attended_back_kernel, size, tb, sub, 4, w_down, w_...  21 us
    pallas_call x1, Pallas kernels, finish(): pl.pallas_call(partial(finish_kernel, size, blocks, w_down), out_shape=ja...  18.7 us
    pallas_call x1, Pallas kernels, project_back(): pl.pallas_call(partial(project_back_kernel, weight, count), out_shape=[ja...  17.8 us
    pallas_call x1, Pallas kernels, project(): pl.pallas_call(partial(project_kernel, weight, count), out_shape=[sds((n,...  16.1 us
  transfers between devices with their start and end apart: 45, of which 13 were waited for; matrix products, arithmetic and copies ran while one was open for 7% of the time, Pallas kernels for 41%

profile of v5, /device:TPU:0, one launch (start us, length us, event | category | flops | bytes accessed | tf_op | source)
XLA Modules:
  0.0 353.4 jit_solution(3884685424165308674)
XLA Ops:
  9.1 3.0 collective-permute-start
  14.4 2.2 multiply_add_fusion.2
  21.0 1.9 collective-permute-done.7.rest_9_
  23.5 1.8 collective-permute-start.2
  28.8 4.0 %collective-permute-done.9.rest_11_ = bf16[144,768]{1,0:T(8,128)(2,1)S(1)} collective-permute-done((bf16[144,768]{1,0:T(8,128)(2,1)}, bf16[144,768]{1,0:T(8,128)(2,1)S(1)}, u32[]{:S(2)}, u32[]{:S(2)}) %collective-permute-start.9) | collective-permute-done | bytes 221216 | tf_op jit(solution)/shard_map/gather_weights/ppermute | solution.py:334
  38.4 1.8 multiply_add_fusion.3
  40.9 16.1 %project.1 = (bf16[2048,768]{1,0:T(8,128)(2,1)}, bf16[2048,2304]{1,0:T(8,128)(2,1)}, f32[8,768]{1,0:T(8,128)}) custom-call(s32[71]{0:T(128)} %pad_add_fusion.tab, bf16[2048,768]{1,0:T(8,128)(2,1)} %x_ref.5, bf16[160,768]{1,0:T(8,128)(2,1)} %copy-done.5, bf16[160,768]{1,0:T(8,128)(2,1)} %collective-permute-done.rest_1_, ...), custom_call_target="tpu_custom_call" | custom-call | flops 144955152 | bytes 385351 | tf_op jit(solution)/shard_map/project/pallas_call | solution.py:475
  59.6 5.3 %collective-permute-done.18.rest_4_ = bf16[384,768]{1,0:T(8,128)(2,1)} collective-permute-done((bf16[384,768]{1,0:T(8,128)(2,1)}, bf16[384,768]{1,0:T(8,128)(2,1)}, u32[]{:S(2)}, u32[]{:S(2)}) %collective-permute-start.18) | collective-permute-done | bytes 589856 | tf_op jit(solution)/shard_map/gather_weights/ppermute | solution.py:334
  64.9 1.6 collective-permute-done.19.rest_10_.rest_2_
  66.6 21.0 %attend.1.att_ref = bf16[2048,768]{1,0:T(8,128)(2,1)} custom-call(s32[71]{0:T(128)} %pad_add_fusion.tab, bf16[2048,2304]{1,0:T(8,128)(2,1)} %get-tuple-element.71.q_ref.k_ref.v_ref, bf16[2048,2304]{1,0:T(8,128)(2,1)} %get-tuple-element.71.q_ref.k_ref.v_ref, bf16[2048,2304]{1,0:T(8,128)(2,1)} %get-tuple-element.71.q_ref.k_ref.v_ref), custom_call_target="tpu_custom_call" | custom-call | flops 480000000 | bytes 251658 | tf_op jit(solution)/shard_map/attend/pallas_call | solution.py:307
  89.8 4.9 %collective-permute-done.22.rest_5_ = bf16[384,768]{1,0:T(8,128)(2,1)} collective-permute-done((bf16[384,768]{1,0:T(8,128)(2,1)}, bf16[384,768]{1,0:T(8,128)(2,1)}, u32[]{:S(2)}, u32[]{:S(2)}) %collective-permute-start.22) | collective-permute-done | bytes 589856 | tf_op jit(solution)/shard_map/gather_weights/ppermute | solution.py:334
  95.6 74.6 %middle.1 = (f32[2048,768]{1,0:T(8,128)}, bf16[2048,3072]{1,0:T(8,128)(2,1)}, f32[2048,768]{1,0:T(8,128)}, bf16[6144,768]{1,0:T(8,128)(2,1)}) custom-call(s32[71]{0:T(128)} %pad_add_fusion.tab, f32[8,768]{1,0:T(8,128)} %get-tuple-element.68.nrm_ref, bf16[2048,768]{1,0:T(8,128)(2,1)} %attend.1.att_ref, bf16[2048,768]{1,0:T(8,128)(2,1)} %x_ref.5, ...), custom_call_target="tpu_custom_call" | custom-call | flops 1014686016 | bytes 1321205 | tf_op jit(solution)/shard_map/middle/pallas_call | solution.py:779
  170.3 21.0 %attended_back.1 = (f32[2048,768]{1,0:T(8,128)}, bf16[2048,768]{1,0:T(8,128)(2,1)}, f32[8,768]{1,0:T(8,128)}, bf16[4,96,768]{2,1,0:T(8,128)(2,1)}, bf16[4,96,768]{2,1,0:T(8,128)(2,1)}) custom-call(s32[71]{0:T(128)} %pad_add_fusion.tab, f32[8,768]{1,0:T(8,128)} %get-tuple-element.68.nrm_ref, f32[2048,768]{1,0:T(8,128)} %get-tuple-element.85.x1_ref, ...), custom_call_target="tpu_custom_call" | custom-call | flops 96636768 | bytes 566231 | tf_op jit(solution)/shard_map/attended_back/pallas_call | solution.py:868
  191.3 36.4 %attend_back.1 = (bf16[2048,768]{1,0:T(8,128)(2,1)}, bf16[2048,768]{1,0:T(8,128)(2,1)}, bf16[2048,768]{1,0:T(8,128)(2,1)}) custom-call(s32[71]{0:T(128)} %pad_add_fusion.tab, bf16[2048,2304]{1,0:T(8,128)(2,1)} %get-tuple-element.71.q_ref.k_ref.v_ref, bf16[2048,2304]{1,0:T(8,128)(2,1)} %get-tuple-element.71.q_ref.k_ref.v_ref, ...), custom_call_target="tpu_custom_call" | custom-call | flops 960000000 | bytes 440401 | tf_op jit(solution)/shard_map/attend_back/pallas_call | solution.py:307
  227.7 14.7 %project_grad.1 = (bf16[4,384,768]{2,1,0:T(8,128)(2,1)}, bf16[4,384,768]{2,1,0:T(8,128)(2,1)}) custom-call(s32[71]{0:T(128)} %pad_add_fusion.tab, bf16[2048,768]{1,0:T(8,128)(2,1)} %get-tuple-element.88.dq_ref, bf16[2048,768]{1,0:T(8,128)(2,1)} %get-tuple-element.89.dk_ref, bf16[2048,768]{1,0:T(8,128)(2,1)} %get-tuple-element.90.dv_ref, ...), custom_call_target="tpu_custom_call" | custom-call | flops 144955152 | bytes 322437 | tf_op jit(solution)/shard_map/project_grad/pallas_call | solution.py:532
  242.4 4.1 %collective-permute-start.28 = (bf16[4,384,768]{2,1,0:T(8,128)(2,1)}, bf16[4,384,768]{2,1,0:T(8,128)(2,1)S(1)}, u32[]{:S(2)}, u32[]{:S(2)}) collective-permute-start(bf16[4,384,768]{2,1,0:T(8,128)(2,1)} %get-tuple-element.96), channel_id=1, source_target_pairs={{0,4},{4,0},{8,12},{12,8},{16,20},{20,16},{24,28},{28,24},{1,5},{5... | collective-permute-start | bytes 7077896 | tf_op jit(solution)/shard_map/ppermute | solution.py:334
  246.5 4.4 %collective-permute-done.28 = bf16[4,384,768]{2,1,0:T(8,128)(2,1)S(1)} collective-permute-done((bf16[4,384,768]{2,1,0:T(8,128)(2,1)}, bf16[4,384,768]{2,1,0:T(8,128)(2,1)S(1)}, u32[]{:S(2)}, u32[]{:S(2)}) %collective-permute-start.28) | collective-permute-done | bytes 2359328 | tf_op jit(solution)/shard_map/ppermute | solution.py:334
  250.8 3.8 %fusion.5 = (bf16[384,768]{1,0:T(8,128)(2,1)}, bf16[384,768]{1,0:T(8,128)(2,1)}, bf16[384,768]{1,0:T(8,128)(2,1)}) fusion(bf16[4,384,768]{2,1,0:T(8,128)(2,1)S(1)} %collective-permute-done.28, bf16[4,384,768]{2,1,0:T(8,128)(2,1)} %get-tuple-element.94), kind=kLoop, calls=%fused_computation.13 | loop fusion | flops 3538944 | bytes 5308416 | tf_op jit(solution)/shard_map/convert_element_type | solution.py:358
  254.6 1.9 collective-permute-start.29
  256.5 2.8 collective-permute-start.30
  260.7 18.7 %finish.1 = bf16[2048,768]{1,0:T(8,128)(2,1)} custom-call(s32[71]{0:T(128)} %pad_add_fusion.tab, f32[2048,768]{1,0:T(8,128)} %get-tuple-element.85.x1_ref, bf16[2048,3072]{1,0:T(8,128)(2,1)} %get-tuple-element.98.act_ref, bf16[480,768]{1,0:T(8,128)(2,1)} %copy-done, bf16[480,768]{1,0:T(8,128)(2,1)} %collective-permute-done.24.rest_9_.rest_1_, ...), custom_call_target="tpu_custom_call" | custom-call | flops 193273536 | bytes 534773 | tf_op jit(solution)/shard_map/finish/pallas_call | solution.py:923
  279.4 6.1 %collective-permute-done.30 = bf16[384,768]{1,0:T(8,128)(2,1)S(1)} collective-permute-done((bf16[384,768]{1,0:T(8,128)(2,1)}, bf16[384,768]{1,0:T(8,128)(2,1)S(1)}, u32[]{:S(2)}, u32[]{:S(2)}) %collective-permute-start.30) | collective-permute-done | bytes 589856 | tf_op jit(solution)/shard_map/ppermute | solution.py:334
  286.3 2.1 fusion.2
  289.3 5.7 %collective-permute-start.32 = (bf16[96,768]{1,0:T(8,128)(2,1)}, bf16[96,768]{1,0:T(8,128)(2,1)S(1)}, u32[]{:S(2)}, u32[]{:S(2)}) collective-permute-start(bf16[96,768]{1,0:T(8,128)(2,1)} %get-tuple-element.127), channel_id=1, source_target_pairs={{0,2},{1,3},{2,0},{3,1},{4,6},{5,7},{6,4},{7,5},{8,10},{9,11},{10,... | collective-permute-start | bytes 442376 | tf_op jit(solution)/shard_map/ppermute | solution.py:376
  295.0 3.8 %collective-permute-start.34 = (bf16[96,768]{1,0:T(8,128)(2,1)}, bf16[96,768]{1,0:T(8,128)(2,1)S(1)}, u32[]{:S(2)}, u32[]{:S(2)}) collective-permute-start(bf16[96,768]{1,0:T(8,128)(2,1)} %get-tuple-element.125), channel_id=1, source_target_pairs={{0,3},{1,0},{2,1},{3,2},{4,7},{5,4},{6,5},{7,6},{8,11},{9,8},{10,9... | collective-permute-start | bytes 442376 | tf_op jit(solution)/shard_map/ppermute | solution.py:376
  298.8 17.8 %project_back.1 = (bf16[2048,768]{1,0:T(8,128)(2,1)}, f32[8,768]{1,0:T(8,128)}) custom-call(s32[71]{0:T(128)} %pad_add_fusion.tab, f32[8,768]{1,0:T(8,128)} %get-tuple-element.68.nrm_ref, bf16[2048,768]{1,0:T(8,128)(2,1)} %get-tuple-element.88.dq_ref, bf16[2048,768]{1,0:T(8,128)(2,1)} %get-tuple-element.89.dk_ref, ...), custom_call_target="tpu_custom_call" | custom-call | flops 144955152 | bytes 511180 | tf_op jit(solution)/shard_map/project_back/pallas_call | solution.py:586
  320.7 2.5 collective-permute-done.36
  323.2 2.8 all-reduce.3.cloned.1.call-done
  326.9 3.0 collective-permute-start.42
  332.0 1.7 collective-permute-done.37
  334.4 4.7 %collective-permute-done.38 = f32[8,768]{1,0:T(8,128)S(1)} collective-permute-done((f32[8,768]{1,0:T(8,128)S(1)}, f32[8,768]{1,0:T(8,128)S(1)}, u32[]{:S(2)}, u32[]{:S(2)}) %collective-permute-start.38) | collective-permute-done | bytes 24608 | tf_op jit(solution)/shard_map/ppermute | solution.py:1046
  339.1 2.1 collective-permute-start.39
  (174 shorter events, 40.7 us)
Async XLA Ops:
  7.2 252.1 %reduce-scatter.2.cloned.1.call-start = ((), (), s32[]{:S(2)}) async-start(), calls=%async_computation.1 | async-start | bytes 10616832 | tf_op jit(solution)/shard_map/reduce_scatter | solution.py:1025
  9.1 14.4 %collective-permute-start = (bf16[160,768]{1,0:T(8,128)(2,1)S(1)}, bf16[160,768]{1,0:T(8,128)(2,1)}, u32[]{:S(2)}, u32[]{:S(2)}) collective-permute-start(bf16[160,768]{1,0:T(8,128)(2,1)S(1)} %fusion.10.rest_0_), channel_id=1, source_target_pairs={{0,8},{4,12},{8,0},{12,4},{16,24},{20,28},{24,16},{28,20},{1,9},{5... | collective-permute-start | bytes 737288 | tf_op jit(solution)/shard_map/gather_weights/ppermute | solution.py:334
  12.1 16.6 %collective-permute-start.3 = (bf16[160,768]{1,0:T(8,128)(2,1)S(1)}, bf16[160,768]{1,0:T(8,128)(2,1)}, u32[]{:S(2)}, u32[]{:S(2)}) collective-permute-start(bf16[160,768]{1,0:T(8,128)(2,1)S(1)} %fusion.10.rest_0_), channel_id=1, source_target_pairs={{0,4},{4,0},{8,12},{12,8},{16,20},{20,16},{24,28},{28,24},{1,5},{5... | collective-permute-start | bytes 737288 | tf_op jit(solution)/shard_map/gather_weights/ppermute | solution.py:334
  12.1 13.5 %collective-permute-start.8 = (bf16[144,768]{1,0:T(8,128)(2,1)S(1)}, bf16[144,768]{1,0:T(8,128)(2,1)}, u32[]{:S(2)}, u32[]{:S(2)}) collective-permute-start(bf16[144,768]{1,0:T(8,128)(2,1)S(1)} %get-tuple-element.67.rest_8_), channel_id=1, source_target_pairs={{0,16},{4,20},{8,24},{12,28},{16,0},{20,4},{24,8},{28,12},{1,17},{... | collective-permute-start | bytes 663560 | tf_op jit(solution)/shard_map/gather_weights/ppermute | solution.py:334
  13.7 13.5 %collective-permute-start.1 = (bf16[160,768]{1,0:T(8,128)(2,1)S(1)}, bf16[160,768]{1,0:T(8,128)(2,1)}, u32[]{:S(2)}, u32[]{:S(2)}) collective-permute-start(bf16[160,768]{1,0:T(8,128)(2,1)S(1)} %fusion.10.rest_0_), channel_id=1, source_target_pairs={{0,16},{4,20},{8,24},{12,28},{16,0},{20,4},{24,8},{28,12},{1,17},{... | collective-permute-start | bytes 737288 | tf_op jit(solution)/shard_map/gather_weights/ppermute | solution.py:334
  14.2 8.7 %collective-permute-start.7 = (bf16[144,768]{1,0:T(8,128)(2,1)S(1)}, bf16[144,768]{1,0:T(8,128)(2,1)S(1)}, u32[]{:S(2)}, u32[]{:S(2)}) collective-permute-start(bf16[144,768]{1,0:T(8,128)(2,1)S(1)} %get-tuple-element.67.rest_8_), channel_id=1, source_target_pairs={{0,8},{4,12},{8,0},{12,4},{16,24},{20,28},{24,16},{28,20},{1,9},{5... | collective-permute-start | bytes 663560 | tf_op jit(solution)/shard_map/gather_weights/ppermute | solution.py:334
  23.5 9.3 %collective-permute-start.2 = (bf16[160,768]{1,0:T(8,128)(2,1)}, bf16[160,768]{1,0:T(8,128)(2,1)S(1)}, u32[]{:S(2)}, u32[]{:S(2)}) collective-permute-start(bf16[160,768]{1,0:T(8,128)(2,1)} %collective-permute-done.rest_1_), channel_id=1, source_target_pairs={{0,16},{4,20},{8,24},{12,28},{16,0},{20,4},{24,8},{28,12},{1,17},{... | collective-permute-start | bytes 737288 | tf_op jit(solution)/shard_map/gather_weights/ppermute | solution.py:334
  25.6 7.2 %collective-permute-start.9 = (bf16[144,768]{1,0:T(8,128)(2,1)}, bf16[144,768]{1,0:T(8,128)(2,1)S(1)}, u32[]{:S(2)}, u32[]{:S(2)}) collective-permute-start(bf16[144,768]{1,0:T(8,128)(2,1)} %collective-permute-done.8.rest_10_), channel_id=1, source_target_pairs={{0,8},{4,12},{8,0},{12,4},{16,24},{20,28},{24,16},{28,20},{1,9},{5... | collective-permute-start | bytes 663560 | tf_op jit(solution)/shard_map/gather_weights/ppermute | solution.py:334
  27.1 8.6 %collective-permute-start.4 = (bf16[160,768]{1,0:T(8,128)(2,1)}, bf16[160,768]{1,0:T(8,128)(2,1)S(1)}, u32[]{:S(2)}, u32[]{:S(2)}) collective-permute-start(bf16[160,768]{1,0:T(8,128)(2,1)} %collective-permute-done.rest_1_), channel_id=1, source_target_pairs={{0,4},{4,0},{8,12},{12,8},{16,20},{20,16},{24,28},{28,24},{1,5},{5... | collective-permute-start | bytes 737288 | tf_op jit(solution)/shard_map/gather_weights/ppermute | solution.py:334
  27.1 9.7 %collective-permute-start.5 = (bf16[160,768]{1,0:T(8,128)(2,1)}, bf16[160,768]{1,0:T(8,128)(2,1)S(1)}, u32[]{:S(2)}, u32[]{:S(2)}) collective-permute-start(bf16[160,768]{1,0:T(8,128)(2,1)} %collective-permute-done.1.rest_2_), channel_id=1, source_target_pairs={{0,4},{4,0},{8,12},{12,8},{16,20},{20,16},{24,28},{28,24},{1,5},{5... | collective-permute-start | bytes 737288 | tf_op jit(solution)/shard_map/gather_weights/ppermute | solution.py:334
  28.7 7.0 %collective-permute-start.12 = (bf16[144,768]{1,0:T(8,128)(2,1)}, bf16[144,768]{1,0:T(8,128)(2,1)S(1)}, u32[]{:S(2)}, u32[]{:S(2)}) collective-permute-start(bf16[144,768]{1,0:T(8,128)(2,1)} %collective-permute-done.8.rest_10_), channel_id=1, source_target_pairs={{0,4},{4,0},{8,12},{12,8},{16,20},{20,16},{24,28},{28,24},{1,5},{5... | collective-permute-start | bytes 663560 | tf_op jit(solution)/shard_map/gather_weights/ppermute | solution.py:334
  32.8 24.2 %collective-permute-start.15 = (bf16[480,768]{1,0:T(8,128)(2,1)S(1)}, bf16[480,768]{1,0:T(8,128)(2,1)}, u32[]{:S(2)}, u32[]{:S(2)}) collective-permute-start(bf16[480,768]{1,0:T(8,128)(2,1)S(1)} %bitcast_dynamic-update-slice_fusion.rest_8_.rest_0_), channel_id=1, source_target_pairs={{0,16},{4,20},{8,24},{12,28},{16,0},{20,4},{24,8},{28,12},{1,17},{... | collective-permute-start | bytes 2211848 | tf_op jit(solution)/shard_map/gather_weights/ppermute | solution.py:334
  34.3 22.7 %collective-permute-start.14 = (bf16[384,768]{1,0:T(8,128)(2,1)}, bf16[384,768]{1,0:T(8,128)(2,1)}, u32[]{:S(2)}, u32[]{:S(2)}) collective-permute-start(bf16[384,768]{1,0:T(8,128)(2,1)} %bitcast.4.rest_0_), channel_id=1, source_target_pairs={{0,8},{4,12},{8,0},{12,4},{16,24},{20,28},{24,16},{28,20},{1,9},{5... | collective-permute-start | bytes 1769480 | tf_op jit(solution)/shard_map/gather_weights/ppermute | solution.py:334
  35.8 29.1 %collective-permute-start.18 = (bf16[384,768]{1,0:T(8,128)(2,1)}, bf16[384,768]{1,0:T(8,128)(2,1)}, u32[]{:S(2)}, u32[]{:S(2)}) collective-permute-start(bf16[384,768]{1,0:T(8,128)(2,1)} %bitcast.4.rest_0_), channel_id=1, source_target_pairs={{0,16},{4,20},{8,24},{12,28},{16,0},{20,4},{24,8},{28,12},{1,17},{... | collective-permute-start | bytes 1769480 | tf_op jit(solution)/shard_map/gather_weights/ppermute | solution.py:334
  36.8 29.7 %collective-permute-start.19 = (bf16[480,768]{1,0:T(8,128)(2,1)S(1)}, bf16[480,768]{1,0:T(8,128)(2,1)}, u32[]{:S(2)}, u32[]{:S(2)}) collective-permute-start(bf16[480,768]{1,0:T(8,128)(2,1)S(1)} %bitcast_dynamic-update-slice_fusion.rest_8_.rest_0_), channel_id=1, source_target_pairs={{0,8},{4,12},{8,0},{12,4},{16,24},{20,28},{24,16},{28,20},{1,9},{5... | collective-permute-start | bytes 2211848 | tf_op jit(solution)/shard_map/gather_weights/ppermute | solution.py:334
  57.0 30.6 %collective-permute-start.21 = (bf16[480,768]{1,0:T(8,128)(2,1)}, bf16[480,768]{1,0:T(8,128)(2,1)}, u32[]{:S(2)}, u32[]{:S(2)}) collective-permute-start(bf16[480,768]{1,0:T(8,128)(2,1)} %collective-permute-done.15.rest_12_.rest_4_), channel_id=1, source_target_pairs={{0,8},{4,12},{8,0},{12,4},{16,24},{20,28},{24,16},{28,20},{1,9},{5... | collective-permute-start | bytes 2211848 | tf_op jit(solution)/shard_map/gather_weights/ppermute | solution.py:334
  58.6 29.0 %collective-permute-start.20 = (bf16[384,768]{1,0:T(8,128)(2,1)}, bf16[384,768]{1,0:T(8,128)(2,1)}, u32[]{:S(2)}, u32[]{:S(2)}) collective-permute-start(bf16[384,768]{1,0:T(8,128)(2,1)} %collective-permute-done.14.rest_1_), channel_id=1, source_target_pairs={{0,16},{4,20},{8,24},{12,28},{16,0},{20,4},{24,8},{28,12},{1,17},{... | collective-permute-start | bytes 1769480 | tf_op jit(solution)/shard_map/gather_weights/ppermute | solution.py:334
  59.6 29.7 %collective-permute-start.24 = (bf16[480,768]{1,0:T(8,128)(2,1)S(1)}, bf16[480,768]{1,0:T(8,128)(2,1)}, u32[]{:S(2)}, u32[]{:S(2)}) collective-permute-start(bf16[480,768]{1,0:T(8,128)(2,1)S(1)} %bitcast_dynamic-update-slice_fusion.rest_8_.rest_0_), channel_id=1, source_target_pairs={{0,4},{4,0},{8,12},{12,8},{16,20},{20,16},{24,28},{28,24},{1,5},{5... | collective-permute-start | bytes 2211848 | tf_op jit(solution)/shard_map/gather_weights/ppermute | solution.py:334
  64.9 23.9 %collective-permute-start.16 = (bf16[384,768]{1,0:T(8,128)(2,1)}, bf16[384,768]{1,0:T(8,128)(2,1)}, u32[]{:S(2)}, u32[]{:S(2)}) collective-permute-start(bf16[384,768]{1,0:T(8,128)(2,1)} %bitcast.4.rest_0_), channel_id=1, source_target_pairs={{0,4},{4,0},{8,12},{12,8},{16,20},{20,16},{24,28},{28,24},{1,5},{5... | collective-permute-start | bytes 1769480 | tf_op jit(solution)/shard_map/gather_weights/ppermute | solution.py:334
  66.6 22.7 %collective-permute-start.17 = (bf16[384,768]{1,0:T(8,128)(2,1)}, bf16[384,768]{1,0:T(8,128)(2,1)}, u32[]{:S(2)}, u32[]{:S(2)}) collective-permute-start(bf16[384,768]{1,0:T(8,128)(2,1)} %collective-permute-done.14.rest_1_), channel_id=1, source_target_pairs={{0,4},{4,0},{8,12},{12,8},{16,20},{20,16},{24,28},{28,24},{1,5},{5... | collective-permute-start | bytes 1769480 | tf_op jit(solution)/shard_map/gather_weights/ppermute | solution.py:334
  87.6 7.2 %collective-permute-start.25 = (bf16[480,768]{1,0:T(8,128)(2,1)}, bf16[480,768]{1,0:T(8,128)(2,1)}, u32[]{:S(2)}, u32[]{:S(2)}) collective-permute-start(bf16[480,768]{1,0:T(8,128)(2,1)} %collective-permute-done.19.rest_10_.rest_2_), channel_id=1, source_target_pairs={{0,4},{4,0},{8,12},{12,8},{16,20},{20,16},{24,28},{28,24},{1,5},{5... | collective-permute-start | bytes 2211848 | tf_op jit(solution)/shard_map/gather_weights/ppermute | solution.py:334
  170.2 155.8 %all-reduce.3.cloned.1.call-start = ((), (), s32[]{:S(2)}) async-start(), calls=%async_computation.2 | async-start | bytes 2359296 | tf_op jit(solution)/shard_map/psum | solution.py:1032
  242.4 8.5 %collective-permute-start.28 = (bf16[4,384,768]{2,1,0:T(8,128)(2,1)}, bf16[4,384,768]{2,1,0:T(8,128)(2,1)S(1)}, u32[]{:S(2)}, u32[]{:S(2)}) collective-permute-start(bf16[4,384,768]{2,1,0:T(8,128)(2,1)} %get-tuple-element.96), channel_id=1, source_target_pairs={{0,4},{4,0},{8,12},{12,8},{16,20},{20,16},{24,28},{28,24},{1,5},{5... | collective-permute-start | bytes 7077896 | tf_op jit(solution)/shard_map/ppermute | solution.py:334
  254.6 24.8 %collective-permute-start.29 = (bf16[384,768]{1,0:T(8,128)(2,1)}, bf16[384,768]{1,0:T(8,128)(2,1)}, u32[]{:S(2)}, u32[]{:S(2)}) collective-permute-start(bf16[384,768]{1,0:T(8,128)(2,1)} %get-tuple-element.122), channel_id=1, source_target_pairs={{0,8},{4,12},{8,0},{12,4},{16,24},{20,28},{24,16},{28,20},{1,9},{5... | collective-permute-start | bytes 1769480 | tf_op jit(solution)/shard_map/ppermute | solution.py:334
  256.5 29.0 %collective-permute-start.30 = (bf16[384,768]{1,0:T(8,128)(2,1)}, bf16[384,768]{1,0:T(8,128)(2,1)S(1)}, u32[]{:S(2)}, u32[]{:S(2)}) collective-permute-start(bf16[384,768]{1,0:T(8,128)(2,1)} %get-tuple-element.121), channel_id=1, source_target_pairs={{0,16},{4,20},{8,24},{12,28},{16,0},{20,4},{24,8},{28,12},{1,17},{... | collective-permute-start | bytes 1769480 | tf_op jit(solution)/shard_map/ppermute | solution.py:334
  259.3 27.0 %collective-permute-start.31 = (bf16[384,768]{1,0:T(8,128)(2,1)}, bf16[384,768]{1,0:T(8,128)(2,1)}, u32[]{:S(2)}, u32[]{:S(2)}) collective-permute-start(bf16[384,768]{1,0:T(8,128)(2,1)} %get-tuple-element.120), channel_id=1, source_target_pairs={{0,24},{4,28},{8,16},{12,20},{16,8},{20,12},{24,0},{28,4},{1,25},{... | collective-permute-start | bytes 1769480 | tf_op jit(solution)/shard_map/ppermute | solution.py:334
  289.3 28.8 %collective-permute-start.32 = (bf16[96,768]{1,0:T(8,128)(2,1)}, bf16[96,768]{1,0:T(8,128)(2,1)S(1)}, u32[]{:S(2)}, u32[]{:S(2)}) collective-permute-start(bf16[96,768]{1,0:T(8,128)(2,1)} %get-tuple-element.127), channel_id=1, source_target_pairs={{0,2},{1,3},{2,0},{3,1},{4,6},{5,7},{6,4},{7,5},{8,10},{9,11},{10,... | collective-permute-start | bytes 442376 | tf_op jit(solution)/shard_map/ppermute | solution.py:376
  295.0 23.0 %collective-permute-start.33 = (bf16[96,768]{1,0:T(8,128)(2,1)}, bf16[96,768]{1,0:T(8,128)(2,1)S(1)}, u32[]{:S(2)}, u32[]{:S(2)}) collective-permute-start(bf16[96,768]{1,0:T(8,128)(2,1)} %get-tuple-element.126), channel_id=1, source_target_pairs={{0,1},{1,2},{2,3},{3,0},{4,5},{5,6},{6,7},{7,4},{8,9},{9,10},{10,1... | collective-permute-start | bytes 442376 | tf_op jit(solution)/shard_map/ppermute | solution.py:376
  295.0 23.0 %collective-permute-start.34 = (bf16[96,768]{1,0:T(8,128)(2,1)}, bf16[96,768]{1,0:T(8,128)(2,1)S(1)}, u32[]{:S(2)}, u32[]{:S(2)}) collective-permute-start(bf16[96,768]{1,0:T(8,128)(2,1)} %get-tuple-element.125), channel_id=1, source_target_pairs={{0,3},{1,0},{2,1},{3,2},{4,7},{5,4},{6,5},{7,6},{8,11},{9,8},{10,9... | collective-permute-start | bytes 442376 | tf_op jit(solution)/shard_map/ppermute | solution.py:376
  326.1 18.7 %collective-permute-start.40 = (bf16[96,768]{1,0:T(8,128)(2,1)S(1)}, bf16[96,768]{1,0:T(8,128)(2,1)S(1)}, u32[]{:S(2)}, u32[]{:S(2)}) collective-permute-start(bf16[96,768]{1,0:T(8,128)(2,1)S(1)} %fusion.9), channel_id=1, source_target_pairs={{0,1},{1,2},{2,3},{3,0},{4,5},{5,6},{6,7},{7,4},{8,9},{9,10},{10,1... | collective-permute-start | bytes 442376 | tf_op jit(solution)/shard_map/ppermute | solution.py:376
  326.2 18.6 %collective-permute-start.41 = (bf16[96,768]{1,0:T(8,128)(2,1)S(1)}, bf16[96,768]{1,0:T(8,128)(2,1)S(1)}, u32[]{:S(2)}, u32[]{:S(2)}) collective-permute-start(bf16[96,768]{1,0:T(8,128)(2,1)S(1)} %fusion.9), channel_id=1, source_target_pairs={{0,2},{1,3},{2,0},{3,1},{4,6},{5,7},{6,4},{7,5},{8,10},{9,11},{10,... | collective-permute-start | bytes 442376 | tf_op jit(solution)/shard_map/ppermute | solution.py:376
  326.9 17.9 %collective-permute-start.42 = (bf16[96,768]{1,0:T(8,128)(2,1)S(1)}, bf16[96,768]{1,0:T(8,128)(2,1)S(1)}, u32[]{:S(2)}, u32[]{:S(2)}) collective-permute-start(bf16[96,768]{1,0:T(8,128)(2,1)S(1)} %fusion.9), channel_id=1, source_target_pairs={{0,3},{1,0},{2,1},{3,2},{4,7},{5,4},{6,5},{7,6},{8,11},{9,8},{10,9... | collective-permute-start | bytes 442376 | tf_op jit(solution)/shard_map/ppermute | solution.py:376
  (39 other events, 194.6 us)
Sparse Core Ops, SparseCore 0:
  170.3 77.5 reduce-scatter.1
  259.5 66.5 all-reduce.2
